TPU v7x, 32 devices: a whole 2x2x4 slice. The times are simulated.
32 devices in a mesh: dp: 8 (over z, x), tensor: 4 (over y, core).
Axes of the slice: x: 2, y: 2, z: 4, core: 2. Of those that a mesh axis runs over, the one named last changes fastest.
Arguments:
- codons: int32 [32, 1024], P(('dp', 'tensor')), may hold values from 0 to 69
- segments: int32 [32, 1024], P('dp'), may hold values from 0 to 3, never falling along the last dimension, each value on 1 to 512 neighbouring positions
- targets: int32 [32, 1024], P(('dp', 'tensor')), may hold values from 0 to 69
- loss_mask: int32 [32, 1024], P(('dp', 'tensor')), may hold values 0 or 1
- owner_map: int32 [192], replicated, may hold values from 0 to 191, as said below
- step_count: int32 [], replicated, may hold values from 2 to 20
- block_weight: float32 [4, 192, 96, 96], P('tensor', 'dp')
- block_left: float32 [4, 192, 96, 96], P('tensor', 'dp'), as said below
- block_right: float32 [4, 192, 96, 96], P('tensor', 'dp'), as said below
- block_left_root: float32 [4, 192, 96, 96], P('tensor', 'dp'), as said below
- block_right_root: float32 [4, 192, 96, 96], P('tensor', 'dp'), as said below
- embedding_weight: float32 [128, 768], replicated, may hold values from -0.4375 to 0.4375
- table_left: float32 [128, 128], replicated, as said below
- table_right: float32 [768, 768], replicated, as said below
- table_left_root: float32 [128, 128], replicated, as said below
- table_right_root: float32 [768, 768], replicated, as said below
- norm_params: float32 [6, 768], replicated, as said below
- norm_moment: float32 [6, 768], replicated, may hold values from -1.1444092e-05 to 1.1444092e-05
- norm_second: float32 [6, 768], replicated, may hold values from 5.57041e-14 to 2.228164e-13
Outputs:
- loss_value: float32 [], replicated
- grad_norm: float32 [], replicated
- block_grad: float32 [4, 192, 96, 96], P('tensor', 'dp')
- new_block_left: float32 [4, 192, 96, 96], P('tensor', 'dp')
- new_block_right: float32 [4, 192, 96, 96], P('tensor', 'dp')
- new_block_weight: float32 [4, 192, 96, 96], P('tensor', 'dp')
- embedding_clipped_gradient: float32 [128, 768], replicated
- new_table_left: float32 [128, 128], replicated
- new_table_right: float32 [768, 768], replicated
- new_table_weight: float32 [128, 768], replicated
- norm_clipped_gradient: float32 [6, 768], replicated
- new_norm_moment: float32 [6, 768], replicated
- new_norm_second: float32 [6, 768], replicated
- new_norm_params: float32 [6, 768], replicated
Inputs may be any that keep to these rules, and one draw needn't show every extreme that they name: owner_map is a permutation. `block_left`: symmetric. `block_right`: symmetric. `block_left_root`: symmetric positive definite. `block_right_root`: symmetric positive definite. `table_left`: symmetric. `table_right`: symmetric. `table_left_root`: symmetric positive definite. `table_right_root`: symmetric positive definite. `norm_params`: rows 0, 2, 4 are gains, rows 1, 3, 5 biases.
All inputs are finite; a program needn't handle non-finite values. No bound on the sum of `loss_mask` on one device may be relied on, other than what follows from the above.
Results may differ from a plain program's by a relative error of at most 0.0013.
The roundings to bfloat16 on the way count: a program that leaves them out, or rounds other values in their place, can miss the bound.
Values may be sent and summed in bfloat16 or wider, within the bound.
A program may use at most 256 MiB of HBM per device.

v0:
```python
import functools
import math

import jax
import jax.numpy as jnp
from jax import lax
from jax.experimental import pallas as pl
from jax.experimental.pallas import tpu as pltpu
from jax.sharding import PartitionSpec as P

FF = 3072
HS = 64

CLIP_LEVEL = 0.005
STAT_DECAY = 0.5
MATRIX_RATE = 0.03
WEIGHT_DECAY = 0.01
VECTOR_RATE = 0.2
FIRST_BETA = 0.9
SECOND_BETA = 0.999
ADAM_EPSILON = 1e-08
NORM_EPSILON = 1e-05
ROOT_EPSILON = 1e-06
MASK_VALUE = -1e30
ROTARY_BASE = 10000.0
TOP_PRECISION = lax.Precision.HIGHEST

LANES = 128
PACK = 4
VMEM_LIMIT = 60 * 1024 * 1024
BF16 = jnp.bfloat16
F32 = jnp.float32


def dot(left, right):
    return lax.dot_general(left, right, (((1,), (0,)), ((), ())), preferred_element_type=F32)


def dot_nt(left, right):
    return lax.dot_general(left, right, (((1,), (1,)), ((), ())), preferred_element_type=F32)


def dot_tn(left, right):
    return lax.dot_general(left, right, (((0,), (0,)), ((), ())), preferred_element_type=F32)


def split_three(values):
    high = values.astype(BF16)
    rest = values - high.astype(F32)
    middle = rest.astype(BF16)
    low = (rest - middle.astype(F32)).astype(BF16)
    return high, middle, low


def params(**more):
    return pltpu.CompilerParams(vmem_limit_bytes=VMEM_LIMIT, **more)


def whole(shape):
    return pl.BlockSpec(shape, lambda *_: (0,) * len(shape))


def unpack_group(group, edge):
    return [group[:, edge * j : edge * (j + 1)] for j in range(PACK)]


def assemble_kernel(
    place_ref, in_ref, project_ref, outward_ref, expand_ref, contract_ref, store, *, load_steps
):
    step = pl.program_id(0)
    halves, per_step, part, strip_width = in_ref.shape
    edge = strip_width // PACK

    @pl.when(step < load_steps)
    def _():
        def unpack(g, carry):
            for h in range(halves):
                pieces = unpack_group(in_ref[h, g], edge)
                for j in range(PACK):
                    store[(step * per_step + g) * PACK + j, h * part : (h + 1) * part, :edge] = pieces[j]
            return carry

        lax.fori_loop(0, per_step, unpack, 0, unroll=4)

    @pl.when(step >= load_steps)
    def _():
        row = step - load_steps
        strip = PACK * edge

        def fill(out_ref, rows, base):
            strips = out_ref.shape[1] // strip

            def body(k, carry):
                r = k // strips
                c = k - r * strips
                first = base + k * PACK
                blocks = [store[place_ref[first + j]][:, :edge] for j in range(PACK)]
                out_ref[pl.ds(pl.multiple_of(r * edge, edge), edge), pl.ds(pl.multiple_of(c * strip, strip), strip)] = (
                    jnp.concatenate(blocks, axis=1)
                )
                return carry

            lax.fori_loop(0, rows * strips, body, 0, unroll=2)
            return rows * strips * PACK

        steps = pl.num_programs(0) - load_steps
        offset = 0
        for out_ref in (project_ref, outward_ref, expand_ref, contract_ref):
            rows = out_ref.shape[0] // edge
            count = rows * (out_ref.shape[1] // strip) * PACK
            fill(out_ref, rows, offset + row * count)
            offset = offset + count * steps


def assemble(place, packed, width, hidden_width):
    halves, groups, part, strip = packed.shape
    edge = halves * part
    per_step = 16
    load_steps = groups // per_step
    fill_steps = width // edge
    tall = hidden_width // fill_steps

    def late(step, *_):
        return (jnp.maximum(step - load_steps, 0), 0)

    return pl.pallas_call(
        functools.partial(assemble_kernel, load_steps=load_steps),
        out_shape=(
            jax.ShapeDtypeStruct((width, 3 * width), BF16),
            jax.ShapeDtypeStruct((width, width), BF16),
            jax.ShapeDtypeStruct((width, hidden_width), BF16),
            jax.ShapeDtypeStruct((hidden_width, width), BF16),
        ),
        grid_spec=pltpu.PrefetchScalarGridSpec(
            num_scalar_prefetch=1,
            grid=(load_steps + fill_steps,),
            in_specs=[
                pl.BlockSpec(
                    (halves, per_step, part, strip),
                    lambda s, *_: (0, jnp.minimum(s, load_steps - 1), 0, 0),
                )
            ],
            out_specs=[
                pl.BlockSpec((edge, 3 * width), late),
                pl.BlockSpec((edge, width), late),
                pl.BlockSpec((edge, hidden_width), late),
                pl.BlockSpec((tall, width), late),
            ],
            scratch_shapes=[pltpu.VMEM((groups * PACK, edge, LANES), BF16)],
        ),
        compiler_params=params(),
        name="assemble_weights",
    )(place, packed)


def block_tables(slot_place, width, shard_width, hidden_width, edge):
    shards = slot_place.shape[0]
    model = width // edge
    wide = shard_width // edge
    tall = hidden_width // shards // edge
    ends = [3 * wide * model, wide * model, model * tall, tall * model]
    pieces = []
    offset = 0
    for count in ends:
        pieces.append(slot_place[:, offset : offset + count])
        offset += count
    project = pieces[0].reshape(shards, model, 3, wide).transpose(1, 2, 0, 3)
    outward = pieces[1].reshape(shards * wide, model)
    expand = pieces[2].reshape(shards, model, tall).transpose(1, 0, 2)
    contract = pieces[3].reshape(shards * tall, model)
    return [piece.reshape(-1) for piece in (project, outward, expand, contract)]


def norm_parts(values):
    scale = 1.0 / values.shape[-1]
    center = values - jnp.sum(values, -1, keepdims=True) * scale
    spread = jnp.sum(center * center, -1, keepdims=True) * scale
    inverse = lax.rsqrt(spread + NORM_EPSILON)
    return center * inverse, inverse


def norm_back(grad, unit, inverse, gain):
    scale = 1.0 / grad.shape[-1]
    inner = grad * gain
    mean_one = jnp.sum(inner, -1, keepdims=True) * scale
    mean_two = jnp.sum(inner * unit, -1, keepdims=True) * scale
    return (inner - mean_one - unit * mean_two) * inverse


def turn(values, cosine, sine):
    lane = lax.broadcasted_iota(jnp.int32, values.shape, 1)
    half = HS // 2
    ahead = pltpu.roll(values, LANES - half, 1)
    behind = pltpu.roll(values, half, 1)
    other = jnp.where(lane % HS < half, ahead, behind)
    return values * cosine + other * sine


def front_kernel(
    codon_ref, table_ref, norm_ref, project_ref, cos_ref, sin_ref, x_ref, h_ref, q_ref, k_ref, v_ref
):
    rows = codon_ref.shape[0]
    vocab, width = table_ref.shape
    index = lax.broadcasted_iota(jnp.int32, (rows, vocab), 1)
    hot = jnp.where(codon_ref[...] == index, 1.0, 0.0).astype(BF16)
    high, middle, low = split_three(table_ref[...])
    embedded = (dot(hot, high) + dot(hot, middle)) + dot(hot, low)
    embedded = embedded * math.sqrt(width)
    x_ref[...] = embedded
    unit, _ = norm_parts(embedded)
    normed = (unit * norm_ref[0:1, :] + norm_ref[1:2, :]).astype(BF16)
    h_ref[...] = normed
    cosine = cos_ref[...]
    sine = sin_ref[...]
    for part, out_ref in ((0, q_ref), (1, k_ref), (2, v_ref)):
        values = dot(normed, project_ref[:, part * width : (part + 1) * width])
        for c in range(width // LANES):
            piece = values[:, c * LANES : (c + 1) * LANES]
            if part < 2:
                piece = turn(piece, cosine, sine)
            if part == 0:
                piece = piece * HS ** (-0.5)
            out_ref[:, c * LANES : (c + 1) * LANES] = piece.astype(BF16)


def front(codon_column, table, norm_params, project, cosine, sine):
    length = codon_column.shape[0]
    vocab, width = table.shape
    rows = 256
    spec = pl.BlockSpec((rows, width), lambda i: (i, 0))
    low = jax.ShapeDtypeStruct((length, width), BF16)
    return pl.pallas_call(
        front_kernel,
        out_shape=(jax.ShapeDtypeStruct((length, width), F32), low, low, low, low),
        grid=(length // rows,),
        in_specs=[
            pl.BlockSpec((rows, 1), lambda i: (i, 0)),
            whole(table.shape),
            whole(norm_params.shape),
            whole(project.shape),
            pl.BlockSpec((rows, LANES), lambda i: (i, 0)),
            pl.BlockSpec((rows, LANES), lambda i: (i, 0)),
        ],
        out_specs=(spec, spec, spec, spec, spec),
        compiler_params=params(),
        name="embed_project",
    )(codon_column, table, norm_params, project, cosine, sine)


ROWS = 256
TILE = 128


def head_masks(rows):
    lane = lax.broadcasted_iota(jnp.int32, (rows, LANES), 1)
    return [lane // HS == h for h in range(LANES // HS)]


def same_segment(seg_col, seg_row_ref, first, count):
    row = jnp.concatenate([seg_row_ref[first + i] for i in range(count)], axis=1)
    return seg_col == row


def attend_kernel(low_ref, high_ref, q_ref, k_ref, v_ref, seg_col_ref, seg_row_ref, o_ref, lse_ref):
    part = pl.program_id(1)
    first, last = low_ref[part], high_ref[part]
    masks = head_masks(ROWS)

    def run(count):
        query = q_ref[...]
        zero = jnp.zeros_like(query)
        span = pl.ds(pl.multiple_of(first * TILE, TILE), count * TILE)
        keys = k_ref[span, :]
        values = v_ref[span, :]
        same = same_segment(seg_col_ref[...], seg_row_ref, first, count)
        outs, logs = [], []
        for mask in masks:
            scores = jnp.where(same, dot_nt(jnp.where(mask, query, zero), keys), MASK_VALUE)
            top = jnp.max(scores, -1, keepdims=True)
            exps = jnp.exp(scores - top)
            total = jnp.sum(exps, -1, keepdims=True)
            probs = (exps * (1.0 / total)).astype(BF16)
            outs.append(dot(probs, values))
            logs.append(top + jnp.log(total))
        o_ref[...] = jnp.where(masks[0], outs[0], outs[1]).astype(BF16)
        lse_ref[...] = jnp.where(masks[0], logs[0], logs[1])

    for count in range(1, k_ref.shape[0] // TILE + 1):
        pl.when(last - first == count)(functools.partial(run, count))


def attend(low, high, query, keys, values, seg_col, seg_row):
    length, width = query.shape
    tiles = length // TILE
    pairs = width // LANES
    column = pl.BlockSpec((ROWS, LANES), lambda p, i, *_: (i, p))
    full = pl.BlockSpec((length, LANES), lambda p, i, *_: (0, p))
    return pl.pallas_call(
        attend_kernel,
        out_shape=(
            jax.ShapeDtypeStruct((length, width), BF16),
            jax.ShapeDtypeStruct((length, width), F32),
        ),
        grid_spec=pltpu.PrefetchScalarGridSpec(
            num_scalar_prefetch=2,
            grid=(pairs, length // ROWS),
            in_specs=[
                column,
                full,
                full,
                pl.BlockSpec((ROWS, 1), lambda p, i, *_: (i, 0)),
                whole((tiles, 1, TILE)),
            ],
            out_specs=(column, column),
        ),
        compiler_params=params(),
        name="attend_forward",
    )(low, high, query, keys, values, seg_col, seg_row)


def attend_back_kernel(
    low_ref, high_ref, q_ref, k_ref, v_ref, g_ref, lse_ref, seg_col_ref, seg_row_ref, cos_ref, sin_ref,
    out_ref, dk_acc, dv_acc,
):
    part = pl.program_id(1)
    parts = pl.num_programs(1)
    heads = LANES // HS
    first, last = low_ref[part], high_ref[part]
    masks = head_masks(ROWS)

    @pl.when(part == 0)
    def _():
        dk_acc[...] = jnp.zeros_like(dk_acc)
        dv_acc[...] = jnp.zeros_like(dv_acc)

    def run(count):
        query = q_ref[...]
        grad = g_ref[...]
        zero = jnp.zeros_like(query)
        span = pl.ds(pl.multiple_of(first * TILE, TILE), count * TILE)
        keys = k_ref[span, :]
        values = v_ref[span, :]
        same = same_segment(seg_col_ref[...], seg_row_ref, first, count)
        dq = []
        dk = dv = None
        for h, mask in enumerate(masks):
            own_query = jnp.where(mask, query, zero)
            own_grad = jnp.where(mask, grad, zero)
            scores = jnp.where(same, dot_nt(own_query, keys), MASK_VALUE)
            probs = jnp.exp(scores - lse_ref[:, h * HS : h * HS + 1])
            grad_probs = dot_nt(own_grad, values)
            delta = jnp.sum(probs * grad_probs, -1, keepdims=True)
            grad_scores = (probs * (grad_probs - delta)).astype(BF16)
            dq.append(dot(grad_scores, keys))
            more_dk = dot(own_query.T, grad_scores)
            more_dv = dot(own_grad.T, probs.astype(BF16))
            dk = more_dk if dk is None else dk + more_dk
            dv = more_dv if dv is None else dv + more_dv
        for i in range(count):
            lanes = slice(i * TILE, (i + 1) * TILE)
            dk_acc[first + i] += dk[:, lanes]
            dv_acc[first + i] += dv[:, lanes]
        rows = pl.ds(pl.multiple_of(part * ROWS, ROWS), ROWS)
        turned = turn(
            jnp.where(masks[0], dq[0], dq[1]) * HS ** (-0.5), cos_ref[rows, :], -sin_ref[rows, :]
        )
        out_ref[0, rows, :] = turned.astype(BF16)

    for count in range(1, k_ref.shape[0] // TILE + 1):
        pl.when(last - first == count)(functools.partial(run, count))

    @pl.when(part == parts - 1)
    def _():
        for j in range(dk_acc.shape[0]):
            rows = slice(j * TILE, (j + 1) * TILE)
            out_ref[1, rows, :] = turn(dk_acc[j].T, cos_ref[rows, :], -sin_ref[rows, :]).astype(BF16)
            out_ref[2, rows, :] = dv_acc[j].T.astype(BF16)


def attend_back(low, high, query, keys, values, grad, lse, seg_col, seg_row, cosine, sine):
    length, width = query.shape
    tiles = length // TILE
    pairs = width // LANES
    column = pl.BlockSpec((ROWS, LANES), lambda p, i, *_: (i, p))
    full = pl.BlockSpec((length, LANES), lambda p, i, *_: (0, p))
    return pl.pallas_call(
        attend_back_kernel,
        out_shape=jax.ShapeDtypeStruct((3, length, width), BF16),
        grid_spec=pltpu.PrefetchScalarGridSpec(
            num_scalar_prefetch=2,
            grid=(pairs, length // ROWS),
            in_specs=[
                column,
                full,
                full,
                column,
                column,
                pl.BlockSpec((ROWS, 1), lambda p, i, *_: (i, 0)),
                whole((tiles, 1, TILE)),
                whole((length, LANES)),
                whole((length, LANES)),
            ],
            out_specs=pl.BlockSpec((3, length, LANES), lambda p, i, *_: (0, 0, p)),
            scratch_shapes=[
                pltpu.VMEM((tiles, LANES, TILE), F32),
                pltpu.VMEM((tiles, LANES, TILE), F32),
            ],
        ),
        compiler_params=params(),
        name="attend_backward",
    )(low, high, query, keys, values, grad, lse, seg_col, seg_row, cosine, sine)


INV_SQRT_TWO = 2.0 ** (-0.5)
INV_SQRT_TWO_PI = (2.0 * math.pi) ** (-0.5)


def middle_kernel(
    x_ref, att_ref, target_ref, mask_ref, count_ref, norm_ref, table_ref,
    outward_ref, expand_ref, contract_ref,
    h_ref, active_ref, d_two_ref, ghid_ref, d_one_ref, gatt_ref, gx_ref, head_ref, norm_grad_ref,
    slope,
):
    step = pl.program_id(0)
    rows, width = x_ref.shape
    vocab = table_ref.shape[0]
    ff = expand_ref.shape[1]
    part = width

    @pl.when(step == 0)
    def _():
        head_ref[...] = jnp.zeros_like(head_ref)
        norm_grad_ref[...] = jnp.zeros_like(norm_grad_ref)

    middle = x_ref[...] + dot(att_ref[...], outward_ref[...])
    unit_two, inverse_two = norm_parts(middle)
    gain_two = norm_ref[2:3, :]
    normed_two = (unit_two * gain_two + norm_ref[3:4, :]).astype(BF16)
    h_ref[...] = normed_two

    def forward(c, total):
        cols = pl.ds(pl.multiple_of(c * part, part), part)
        hidden = dot(normed_two, expand_ref[:, cols])
        cumulative = 0.5 + 0.5 * lax.erf(hidden * INV_SQRT_TWO)
        active = (hidden * cumulative).astype(BF16)
        density = jnp.exp(-0.5 * hidden * hidden) * INV_SQRT_TWO_PI
        slope[:, cols] = cumulative + hidden * density
        active_ref[:, cols] = active
        return total + dot(active, contract_ref[cols, :])

    branch = lax.fori_loop(0, ff // part, forward, jnp.zeros((rows, width), F32))
    unit, inverse = norm_parts(middle + branch)
    gain = norm_ref[4:5, :]
    final = (unit * gain + norm_ref[5:6, :]).astype(BF16)
    table = table_ref[...].astype(BF16)
    logits = dot_nt(final, table)
    shifted = logits - jnp.max(logits, -1, keepdims=True)
    exps = jnp.exp(shifted)
    sums = jnp.sum(exps, -1, keepdims=True)
    hot = target_ref[...] == lax.broadcasted_iota(jnp.int32, (rows, vocab), 1)
    mask = mask_ref[...]
    log_probs = shifted - jnp.log(sums)
    picked = jnp.sum(jnp.where(hot, log_probs, 0.0) * mask, 0, keepdims=True)
    norm_grad_ref[6:7, 0:vocab] -= picked
    glogits = ((jnp.exp(log_probs) - jnp.where(hot, 1.0, 0.0)) * (mask / count_ref[...])).astype(BF16)
    head_ref[...] += dot_tn(glogits, final)
    gfinal = dot(glogits, table)
    norm_grad_ref[4:5, :] += jnp.sum(gfinal * unit, 0, keepdims=True)
    norm_grad_ref[5:6, :] += jnp.sum(gfinal, 0, keepdims=True)
    gx_two = norm_back(gfinal, unit, inverse, gain)
    d_two = gx_two.astype(BF16)
    d_two_ref[...] = d_two

    def backward(c, total):
        cols = pl.ds(pl.multiple_of(c * part, part), part)
        gactive = dot_nt(d_two, contract_ref[cols, :])
        ghid = (gactive * slope[:, cols]).astype(BF16)
        ghid_ref[:, cols] = ghid
        return total + dot_nt(ghid, expand_ref[:, cols])

    gh = lax.fori_loop(0, ff // part, backward, jnp.zeros((rows, width), F32))
    norm_grad_ref[2:3, :] += jnp.sum(gh * unit_two, 0, keepdims=True)
    norm_grad_ref[3:4, :] += jnp.sum(gh, 0, keepdims=True)
    gx_one = gx_two + norm_back(gh, unit_two, inverse_two, gain_two)
    gx_ref[...] = gx_one
    d_one = gx_one.astype(BF16)
    d_one_ref[...] = d_one
    gatt_ref[...] = dot_nt(d_one, outward_ref[...]).astype(BF16)


def middle_rows(x, att, target_col, mask_col, count, norm_params, table, outward, expand, contract):
    length, width = x.shape
    vocab = table.shape[0]
    ff = expand.shape[1]
    rows = 256
    narrow = pl.BlockSpec((rows, width), lambda i: (i, 0))
    broad = pl.BlockSpec((rows, ff), lambda i: (i, 0))
    column = pl.BlockSpec((rows, 1), lambda i: (i, 0))
    low = jax.ShapeDtypeStruct((length, width), BF16)
    low_broad = jax.ShapeDtypeStruct((length, ff), BF16)
    return pl.pallas_call(
        middle_kernel,
        out_shape=(
            low, low_broad, low, low_broad, low, low,
            jax.ShapeDtypeStruct((length, width), F32),
            jax.ShapeDtypeStruct((vocab, width), F32),
            jax.ShapeDtypeStruct((8, width), F32),
        ),
        grid=(length // rows,),
        in_specs=[
            narrow, narrow, column, column, whole((1, 1)), whole(norm_params.shape), whole(table.shape),
            whole(outward.shape), whole(expand.shape), whole(contract.shape),
        ],
        out_specs=(
            narrow, broad, narrow, broad, narrow, narrow, narrow,
            whole((vocab, width)), whole((8, width)),
        ),
        scratch_shapes=[pltpu.VMEM((rows, ff), F32)],
        compiler_params=params(),
        name="middle_rows",
    )(x, att, target_col, mask_col, count, norm_params, table, outward, expand, contract)


def tail_kernel(
    codon_ref, x_ref, gx_ref, gproj_ref, norm_ref, project_ref, head_ref, norm_in_ref,
    table_grad_ref, norm_grad_ref,
):
    step = pl.program_id(0)
    rows, width = x_ref.shape
    vocab = head_ref.shape[0]

    @pl.when(step == 0)
    def _():
        table_grad_ref[...] = head_ref[...]
        norm_grad_ref[...] = norm_in_ref[...]

    gh = dot_nt(gproj_ref[0], project_ref[:, 0:width])
    gh = gh + dot_nt(gproj_ref[1], project_ref[:, width : 2 * width])
    gh = gh + dot_nt(gproj_ref[2], project_ref[:, 2 * width : 3 * width])
    unit, inverse = norm_parts(x_ref[...])
    norm_grad_ref[0:1, :] += jnp.sum(gh * unit, 0, keepdims=True)
    norm_grad_ref[1:2, :] += jnp.sum(gh, 0, keepdims=True)
    gx = gx_ref[...] + norm_back(gh, unit, inverse, norm_ref[0:1, :])
    hot = jnp.where(codon_ref[...] == lax.broadcasted_iota(jnp.int32, (rows, vocab), 1), 1.0, 0.0)
    hot = hot.T.astype(BF16)
    high, middle, low = split_three(gx)
    total = dot(hot, high) + (dot(hot, middle) + dot(hot, low))
    table_grad_ref[...] += total * math.sqrt(width)


def tail_rows(codon_col, x, gx, gproj, norm_params, project, head, norm_in):
    length, width = x.shape
    rows = 256
    narrow = pl.BlockSpec((rows, width), lambda i: (i, 0))
    return pl.pallas_call(
        tail_kernel,
        out_shape=(
            jax.ShapeDtypeStruct(head.shape, F32),
            jax.ShapeDtypeStruct(norm_in.shape, F32),
        ),
        grid=(length // rows,),
        in_specs=[
            pl.BlockSpec((rows, 1), lambda i: (i, 0)),
            narrow, narrow, pl.BlockSpec((3, rows, width), lambda i: (0, i, 0)),
            whole(norm_params.shape), whole(project.shape), whole(head.shape), whole(norm_in.shape),
        ],
        out_specs=(whole(head.shape), whole(norm_in.shape)),
        compiler_params=params(),
        name="tail_rows",
    )(codon_col, x, gx, gproj, norm_params, project, head, norm_in)


def weight_grad_kernel(place_ref, left_ref, right_ref, *rest, edge):
    out_ref, buf, turned, sem = rest[-4:]
    strip_index = pl.program_id(1)
    step = pl.program_id(0) * pl.num_programs(1) + strip_index
    steps = pl.num_programs(0) * pl.num_programs(1)
    count = buf.shape[1]
    slot = lax.rem(step, 2)
    block_rows = count // PACK

    def drain(which):
        pltpu.make_async_copy(buf.at[which], out_ref.at[pl.ds(0, count)], sem.at[which]).wait()

    @pl.when(strip_index == 0)
    def _():
        turned[...] = left_ref[...].T

    @pl.when(step >= 2)
    def _():
        drain(slot)

    right = right_ref[...]
    for r in range(block_rows):
        result = dot(turned[r * edge : (r + 1) * edge, :], right)
        pieces = unpack_group(result, edge)
        for j in range(PACK):
            buf[slot, r * PACK + j, :, :edge] = pieces[j]
        for j in range(PACK):
            k = r * PACK + j
            target = place_ref[step * count + k]
            pltpu.make_async_copy(buf.at[slot, k], out_ref.at[target], sem.at[slot]).start()

    @pl.when(step == steps - 1)
    def _():
        @pl.when(step >= 1)
        def _():
            drain(1 - slot)

        drain(slot)


def weight_grad(place, left, right, into, blocks, edge, left_cols, name):
    length, tall = left.shape
    strip = PACK * edge
    count = left_cols // edge * PACK
    if right.ndim == 3:
        strips = right.shape[2] // strip
        right_spec = pl.BlockSpec((None, length, strip), lambda a, b, *_: (b // strips, 0, b % strips))
        grid = (tall // left_cols, right.shape[0] * strips)
    else:
        right_spec = pl.BlockSpec((length, strip), lambda a, b, *_: (0, b))
        grid = (tall // left_cols, right.shape[1] // strip)
    operands = [place, left, right]
    in_specs = [pl.BlockSpec((length, left_cols), lambda a, b, *_: (0, a)), right_spec]
    aliases = {}
    if into is not None:
        operands.append(into)
        in_specs.append(pl.BlockSpec(memory_space=pl.ANY))
        aliases = {3: 0}
    return pl.pallas_call(
        functools.partial(weight_grad_kernel, edge=edge),
        out_shape=jax.ShapeDtypeStruct((blocks, edge, LANES), F32),
        grid_spec=pltpu.PrefetchScalarGridSpec(
            num_scalar_prefetch=1,
            grid=grid,
            in_specs=in_specs,
            out_specs=pl.BlockSpec(memory_space=pl.ANY),
            scratch_shapes=[
                pltpu.VMEM((2, count, edge, LANES), F32),
                pltpu.VMEM((left_cols, length), BF16),
                pltpu.SemaphoreType.DMA((2,)),
            ],
        ),
        input_output_aliases=aliases,
        compiler_params=params(),
        name=name,
    )(*operands)


def by_strips(table, rows, cols, chunk):
    shaped = table.reshape(rows // chunk, chunk, cols // PACK, PACK)
    return shaped.transpose(0, 2, 1, 3).reshape(-1)


CORE, NEAR_Y, NEAR_X, NEAR_Z, FAR_Z = range(5)
AXIS_STRIDE = {CORE: 1, NEAR_Y: 2, NEAR_X: 4, NEAR_Z: 8, FAR_Z: 16}
CHUNK_AXES = (
    (NEAR_X, NEAR_Y, NEAR_Z, FAR_Z),
    (NEAR_Y, NEAR_X, NEAR_Z, FAR_Z),
    (NEAR_X, NEAR_Y, NEAR_Z, FAR_Z),
    (NEAR_Y, NEAR_X, NEAR_Z, FAR_Z),
    (NEAR_Z, NEAR_X, NEAR_Y, FAR_Z),
    (NEAR_Z, NEAR_Y, NEAR_X, FAR_Z),
)
PACK_GROUPS = 6
QUARTERS = 4
SUM_CHUNKS = PACK_GROUPS * QUARTERS
SUM_SLOTS = 3
SUM_ORDER = (
    0, 2000, 10, 2010, 20, 2020, 1000, 2001, 1010, 2011, 1020, 2021, 30, 2030, 40, 2040, 50, 2050, 1030, 2031, 1040,
    2041, 1050, 2051, 60, 2060, 70, 2070, 1011, 80, 2012, 2080, 1001, 2002, 1060, 2061, 1070, 1080, 2071, 90, 2090,
    1021, 100, 2100, 1031, 2032, 110, 2110, 2022, 1012, 1090, 2013, 1002, 1100, 2003, 120, 2120, 1041, 1110, 2101,
    1051, 130, 2130, 2042, 140, 2140, 2111, 1013, 2052, 2014, 1120, 1032, 1003, 2081, 2004, 1022, 150, 2150, 1130,
    2091, 1061, 1014, 1140, 160, 2160, 1004, 1071, 2072, 1150, 2062, 170, 2170, 1042, 180, 2180, 1052, 1160, 190,
    2190, 2023, 1170, 1180, 2053, 1101, 200, 2200, 2043, 2033, 210, 2210, 2102, 2161, 1072, 1190, 1062, 1023, 2024,
    1111, 2121, 2112, 1081, 2063, 220, 2220, 2082, 1200, 1053, 2054, 1033, 2034, 1091, 1043, 1210, 1024, 2073, 230,
    2230, 1220, 2092, 2044, 1063, 2064, 1102, 2103, 1054, 2171, 1034, 1230, 2131, 1112, 1073, 2074, 1082, 2151,
    1044, 1064, 1103, 2104, 2083, 2113, 1074, 2141, 1161, 1092, 1121, 2093, 1104, 2162, 1083, 2084, 1113, 2114,
    2221, 1093, 2094, 2231, 1084, 2122, 1114, 2181, 1171, 2172, 1131, 1094, 1162, 1151, 2132, 1141, 2142, 2163,
    1122, 1172, 2123, 2191, 2152, 1221, 1163, 2164, 1132, 2133, 2211, 2173, 1231, 1123, 2124, 1142, 2143, 1181,
    1164, 1133, 2134, 2201, 2222, 1124, 1143, 2144, 1173, 2174, 1152, 2153, 1134, 1153, 2154, 1144, 1174, 2182,
    1191, 2192, 1222, 2223, 1154, 1211, 2212, 1201, 2202, 2232, 1223, 2224, 1182, 2183, 1192, 2193, 1224, 1212,
    2213, 1183, 2184, 1202, 2203, 1193, 2194, 1232, 2233, 1184, 1213, 2214, 1203, 2204, 1233, 2234, 1194, 1214,
    1204, 1234,
)
SMALL_ROWS = 1024
SMALL_AXES = (CORE, NEAR_X, NEAR_Y, NEAR_Z, FAR_Z)
MESH = pl.DeviceIdType.MESH


def on_known_slice(owners, shards, slots):
    return owners == 8 and shards == 4 and slots % PACK == 0 and slots == PACK * PACK_GROUPS


def bits_of(owner, shard):
    return {
        CORE: shard % 2,
        NEAR_Y: shard // 2,
        NEAR_X: owner % 2,
        NEAR_Z: owner // 2 % 2,
        FAR_Z: owner // 4,
    }


def own_bits():
    owner, shard = lax.axis_index("dp"), lax.axis_index("tensor")
    return owner, shard, bits_of(owner, shard)


def partner_of(axis, owner, shard, bits):
    if axis == CORE:
        return (owner, shard + 1 - 2 * bits[CORE])
    if axis == NEAR_Y:
        return (owner, shard + 2 - 4 * bits[NEAR_Y])
    step = {NEAR_X: 1, NEAR_Z: 2, FAR_Z: 4}[axis]
    return (owner + step - 2 * step * bits[axis], shard)


def meet_partners(owner, shard, bits):
    barrier = pltpu.get_barrier_semaphore()
    for axis in range(5):
        pl.semaphore_signal(
            barrier, inc=1, device_id=partner_of(axis, owner, shard, bits), device_id_type=MESH
        )
    pl.semaphore_wait(barrier, 5)


def total_of(values):
    return jnp.sum(jnp.sum(values, 1, keepdims=True), 0, keepdims=True)


def statistics(square_sum, loss_sum, count):
    norm = jnp.sqrt(square_sum)
    factor = CLIP_LEVEL / jnp.maximum(norm, CLIP_LEVEL)
    row = lax.broadcasted_iota(jnp.int32, (8, LANES), 0)
    return jnp.where(row == 0, factor, jnp.where(row == 1, norm, loss_sum / count))


def sum_kernel(
    grads_ref, table_ref, norm_ref, count_ref, owned_ref, table_out, norm_out, stats_out,
    inbuf, stage, r0, r1, r2, r3, r4, small, s0, s1, s2, s3, s4, spread, square, squares,
    in_sem, send_sem, recv_sem, small_send, small_recv, square_send, square_recv,
):
    owner, shard, bits = own_bits()
    edge = grads_ref.shape[3]
    strip = PACK * edge
    part = edge // QUARTERS
    received = (r0, r1, r2, r3, r4)

    def axes_of(c):
        return CHUNK_AXES[c % len(CHUNK_AXES)]

    def fetch(c):
        rows = pl.ds(c % QUARTERS * part, part)
        slot = c % SUM_SLOTS
        return pltpu.make_async_copy(
            grads_ref.at[c // QUARTERS, :, :, rows], inbuf.at[slot], in_sem.at[slot]
        )

    for c in range(SUM_SLOTS):
        fetch(c).start()
    meet_partners(owner, shard, bits)

    def chunk_send(c, k):
        if k == 0:
            axis, source = CORE, stage.at[c % SUM_SLOTS]
        else:
            axis = axes_of(c)[k - 1]
            half = received[k - 1].shape[1] // 2
            source = received[k - 1].at[c, pl.ds(half * (1 - bits[axis]), half)]
        return pltpu.make_async_remote_copy(
            src_ref=source,
            dst_ref=received[k].at[c],
            send_sem=send_sem.at[c, k],
            recv_sem=recv_sem.at[c, k],
            device_id=partner_of(axis, owner, shard, bits),
            device_id_type=MESH,
        )

    def packed(c, e, core):
        d = core
        for k, axis in enumerate(axes_of(c)):
            d = d + e // (8 >> k) % 2 * AXIS_STRIDE[axis]
        blocks = [inbuf[c % SUM_SLOTS, d, j][:, :edge] for j in range(PACK)]
        return jnp.concatenate(blocks, axis=1)

    def pack(c):
        fetch(c).wait()
        if c >= SUM_SLOTS:
            chunk_send(c - SUM_SLOTS, 0).wait_send()

        def body(e, carry):
            stage[c % SUM_SLOTS, e] = packed(c, e, 1 - bits[CORE])
            return carry

        lax.fori_loop(0, 16, body, 0, unroll=4)

    def merge(c, k):
        chunk_send(c, k).wait_recv()
        if k == 0:

            def body(e, carry):
                r0[c, e] = r0[c, e] + packed(c, e, bits[CORE])
                return carry

            lax.fori_loop(0, 16, body, 0, unroll=4)
            if c + SUM_SLOTS < SUM_CHUNKS:
                fetch(c + SUM_SLOTS).start()
            return
        axis = axes_of(c)[k - 1]
        half = received[k].shape[1]
        base = half * bits[axis]

        def body(e, carry):
            received[k][c, e] = received[k][c, e] + received[k - 1][c, base + e]
            return carry

        if k < 4:
            lax.fori_loop(0, half, body, 0, unroll=2)
            return
        group = r4[c, 0] + r3[c, base]
        pieces = unpack_group(group, edge)
        rows = slice(c % QUARTERS * part, (c % QUARTERS + 1) * part)
        for j in range(PACK):
            owned_ref[PACK * (c // QUARTERS) + j, rows, :] = pieces[j]
        parts = group * group
        line = parts[:, :LANES]
        for i in range(1, strip // LANES):
            line = line + parts[:, i * LANES : (i + 1) * LANES]
        total = square[...]
        for r in range(part // 8):
            total = total + line[r * 8 : (r + 1) * 8]
        square[...] = total

    vocab, width = table_ref.shape
    vectors = norm_ref.shape[0]
    columns = width // LANES
    small_parts = (s0, s1, s2, s3, s4)

    def small_fill():
        for c in range(columns):
            lanes = slice(c * LANES, (c + 1) * LANES)
            small[c * vocab : (c + 1) * vocab] = table_ref[:, lanes]
            start = columns * vocab + c * vectors
            small[start : start + vectors] = norm_ref[:, lanes]
        used = columns * (vocab + vectors)
        small[used:] = jnp.zeros((SMALL_ROWS - used, LANES), F32)

    def small_base(k):
        base = 0
        for i in range(k):
            base = base + (SMALL_ROWS >> (i + 1)) * bits[SMALL_AXES[i]]
        return base

    def small_copy(k):
        rows = SMALL_ROWS >> (k + 1)
        start = pl.multiple_of(small_base(k) + rows * (1 - bits[SMALL_AXES[k]]), 8)
        return pltpu.make_async_remote_copy(
            src_ref=small.at[pl.ds(start, rows)],
            dst_ref=small_parts[k],
            send_sem=small_send.at[k],
            recv_sem=small_recv.at[k],
            device_id=partner_of(SMALL_AXES[k], owner, shard, bits),
            device_id_type=MESH,
        )

    def small_merge(k):
        small_copy(k).wait_recv()
        rows = SMALL_ROWS >> (k + 1)
        mine = pl.ds(pl.multiple_of(small_base(k + 1), 8), rows)
        if k < 4:
            small[mine, :] = small[mine, :] + small_parts[k][...]
            small_copy(k + 1).start()
        else:
            spread[mine, :] = small[mine, :] + small_parts[k][...]
            spread_copy(4).start()

    def spread_copy(k):
        rows = SMALL_ROWS >> (k + 1)
        here = pl.ds(pl.multiple_of(small_base(k + 1), 8), rows)
        return pltpu.make_async_remote_copy(
            src_ref=spread.at[here],
            dst_ref=spread.at[here],
            send_sem=small_send.at[5 + k],
            recv_sem=small_recv.at[5 + k],
            device_id=partner_of(SMALL_AXES[k], owner, shard, bits),
            device_id_type=MESH,
        )

    def spread_next(k):
        spread_copy(k).wait_recv()
        if k > 0:
            spread_copy(k - 1).start()
        else:
            for c in range(columns):
                lanes = slice(c * LANES, (c + 1) * LANES)
                table_out[:, lanes] = spread[c * vocab : (c + 1) * vocab]
                start = columns * vocab + c * vectors
                norm_out[:, lanes] = spread[start : start + vectors]

    square[...] = jnp.zeros_like(square)
    small_fill()
    small_copy(0).start()
    extra = [functools.partial(small_merge, k) for k in range(5)]
    extra += [functools.partial(spread_next, k) for k in range(4, -1, -1)]
    for position, code in enumerate(SUM_ORDER):
        c, k = code % 1000 // 10, code % 10
        if code < 1000:
            pack(c)
        elif code < 2000:
            merge(c, k)
        else:
            chunk_send(c, k).start()
        if position >= 60 and position % 12 == 0 and extra:
            extra.pop(0)()
    while extra:
        extra.pop(0)()

    def square_copy(k):
        return pltpu.make_async_remote_copy(
            src_ref=squares.at[k],
            dst_ref=squares.at[5 + k],
            send_sem=square_send.at[k],
            recv_sem=square_recv.at[k],
            device_id=partner_of(SMALL_AXES[k], owner, shard, bits),
            device_id_type=MESH,
        )

    value = square[...]
    for k in range(5):
        squares[k] = value
        square_copy(k).start()
        square_copy(k).wait_recv()
        value = squares[k] + squares[5 + k]
    table_sum, vectors_sum = table_out[...], norm_out[0:6, :]
    stats_out[...] = statistics(
        total_of(value) + total_of(table_sum * table_sum) + total_of(vectors_sum * vectors_sum),
        total_of(norm_out[6:7, :]),
        count_ref[0:1, 0:1],
    )

    for c in range(SUM_CHUNKS):
        for k in range(5):
            if k > 0 or c >= SUM_CHUNKS - SUM_SLOTS:
                chunk_send(c, k).wait_send()
    for k in range(5):
        small_copy(k).wait_send()
        spread_copy(k).wait_send()
        square_copy(k).wait_send()


def sum_everywhere(grads, table_grad, norm_grad, count):
    groups, devices, _, edge, _ = grads.shape
    strip = PACK * edge
    part = edge // QUARTERS
    group = lambda count: pltpu.VMEM((SUM_CHUNKS, count, part, strip), F32)
    small = lambda rows: pltpu.VMEM((rows, LANES), F32)
    return pl.pallas_call(
        sum_kernel,
        out_shape=(
            jax.ShapeDtypeStruct((groups * PACK, edge, edge), F32),
            jax.ShapeDtypeStruct(table_grad.shape, F32),
            jax.ShapeDtypeStruct(norm_grad.shape, F32),
            jax.ShapeDtypeStruct((8, LANES), F32),
        ),
        in_specs=[
            pl.BlockSpec(memory_space=pl.ANY),
            pl.BlockSpec(memory_space=pltpu.VMEM),
            pl.BlockSpec(memory_space=pltpu.VMEM),
            pl.BlockSpec(memory_space=pltpu.VMEM),
        ],
        out_specs=(pl.BlockSpec(memory_space=pltpu.VMEM),) * 4,
        scratch_shapes=[
            pltpu.VMEM((SUM_SLOTS, devices, PACK, part, LANES), F32),
            pltpu.VMEM((SUM_SLOTS, devices // 2, part, strip), F32),
            group(16), group(8), group(4), group(2), group(1),
            small(SMALL_ROWS), small(512), small(256), small(128), small(64), small(32), small(SMALL_ROWS),
            pltpu.VMEM((8, LANES), F32),
            pltpu.VMEM((10, 8, LANES), F32),
            pltpu.SemaphoreType.DMA((SUM_SLOTS,)),
            pltpu.SemaphoreType.DMA((SUM_CHUNKS, 5)),
            pltpu.SemaphoreType.DMA((SUM_CHUNKS, 5)),
            pltpu.SemaphoreType.DMA((10,)),
            pltpu.SemaphoreType.DMA((10,)),
            pltpu.SemaphoreType.DMA((5,)),
            pltpu.SemaphoreType.DMA((5,)),
        ],
        compiler_params=pltpu.CompilerParams(
            vmem_limit_bytes=66_000_000, collective_id=1, has_side_effects=True
        ),
        name="sum_gradients",
    )(grads, table_grad, norm_grad, count)


GATHER_AXES = (
    (NEAR_Z, NEAR_X, NEAR_Y),
    (NEAR_Z, NEAR_Y, NEAR_X),
    (NEAR_X, NEAR_Y, NEAR_Z),
    (NEAR_Y, NEAR_X, NEAR_Z),
    (NEAR_X, NEAR_Y, NEAR_Z),
    (NEAR_Y, NEAR_X, NEAR_Z),
)
HALVES = 2
GATHER_CHUNKS = PACK_GROUPS * HALVES
GATHER_ORDER = (
    2000, 2010, 2020, 2030, 1000, 2001, 1010, 2011, 2040, 2050, 1020, 2021, 1030, 1001, 2002, 1011, 2012, 2060,
    2070, 2031, 1040, 2041, 1050, 1021, 2022, 2080, 2090, 2051, 1031, 2032, 1002, 1012, 1060, 1070, 2003, 1041,
    2061, 2100, 2110, 2071, 2042, 1051, 1022, 1080, 1090, 2052, 1032, 1061, 2033, 1071, 1100, 1110, 2081, 2062,
    1042, 2091, 1003, 2004, 1052, 2101, 2023, 1081, 2111, 2072, 1091, 1004, 1062, 2013, 1101, 1033, 2034, 1111,
    2082, 2092, 1034, 1072, 2102, 1023, 2024, 2063, 2112, 1082, 2053, 1013, 2014, 1092, 1024, 2043, 1102, 1014,
    1112, 2073, 2093, 1063, 2064, 2083, 1053, 2054, 1043, 2044, 1064, 1054, 2113, 1073, 2074, 1044, 2103, 1093,
    2094, 1074, 1083, 2084, 1094, 1084, 1113, 2114, 1103, 2104, 1114, 1104,
)


def gather_entry(group, bits):
    first, second, third = GATHER_AXES[group]
    return 16 * bits[CORE] + 8 * bits[first] + 4 * bits[second] + 2 * bits[third] + bits[FAR_Z]


def gather_kernel(own_ref, mask_ref, out_ref, count_ref, counts, own_sem, send_sem, recv_sem, count_send, count_recv):
    owner, shard, bits = own_bits()
    rows = own_ref.shape[1] // HALVES

    def place(c):
        return gather_entry(c % PACK_GROUPS, bits)

    def keep(c):
        part = pl.ds(c // PACK_GROUPS * rows, rows)
        return pltpu.make_async_copy(
            own_ref.at[c % PACK_GROUPS, part], out_ref.at[c, place(c)], own_sem.at[c]
        )

    def move(c, k):
        if k == 0:
            axis = FAR_Z
            source = own_ref.at[c % PACK_GROUPS, pl.ds(c // PACK_GROUPS * rows, rows)]
            target = out_ref.at[c, place(c)]
        else:
            axis = CORE if k == 4 else GATHER_AXES[c % PACK_GROUPS][3 - k]
            size = 1 << k
            base = place(c) // size * size
            source = out_ref.at[c, pl.ds(base, size)]
            target = source
        return pltpu.make_async_remote_copy(
            src_ref=source,
            dst_ref=target,
            send_sem=send_sem.at[c, k],
            recv_sem=recv_sem.at[c, k],
            device_id=partner_of(axis, owner, shard, bits),
            device_id_type=MESH,
        )

    def count_copy(k):
        return pltpu.make_async_remote_copy(
            src_ref=counts.at[k],
            dst_ref=counts.at[5 + k],
            send_sem=count_send.at[k],
            recv_sem=count_recv.at[k],
            device_id=partner_of(SMALL_AXES[k], owner, shard, bits),
            device_id_type=MESH,
        )

    for c in range(GATHER_CHUNKS):
        keep(c).start()
    total = jnp.broadcast_to(jnp.sum(mask_ref[...].astype(F32), keepdims=True), count_ref.shape)
    counts[0] = total
    meet_partners(owner, shard, bits)
    stage = 0
    for position, code in enumerate(GATHER_ORDER):
        c, k = code % 1000 // 10, code % 10
        if code < 2000:
            move(c, k).wait_recv()
        else:
            if k == 1:
                keep(c).wait()
            move(c, k).start()
        if position == 0:
            count_copy(0).start()
        elif position % 12 == 0 and stage < 5:
            count_copy(stage).wait_recv()
            total = counts[stage] + counts[5 + stage]
            stage += 1
            if stage < 5:
                counts[stage] = total
                count_copy(stage).start()
    count_ref[...] = jnp.maximum(total, 1.0)
    for c in range(GATHER_CHUNKS):
        for k in range(5):
            move(c, k).wait_send()
    for k in range(5):
        count_copy(k).wait_send()


def gather_everywhere(own, mask):
    groups, edge, strip = own.shape
    return pl.pallas_call(
        gather_kernel,
        out_shape=(
            jax.ShapeDtypeStruct((GATHER_CHUNKS, 32, edge // HALVES, strip), own.dtype),
            jax.ShapeDtypeStruct((8, LANES), F32),
        ),
        in_specs=[pl.BlockSpec(memory_space=pltpu.VMEM)] * 2,
        out_specs=(pl.BlockSpec(memory_space=pl.ANY), pl.BlockSpec(memory_space=pltpu.VMEM)),
        scratch_shapes=[
            pltpu.VMEM((10, 8, LANES), F32),
            pltpu.SemaphoreType.DMA((GATHER_CHUNKS,)),
            pltpu.SemaphoreType.DMA((GATHER_CHUNKS, 5)),
            pltpu.SemaphoreType.DMA((GATHER_CHUNKS, 5)),
            pltpu.SemaphoreType.DMA((5,)),
            pltpu.SemaphoreType.DMA((5,)),
        ],
        compiler_params=pltpu.CompilerParams(collective_id=2, has_side_effects=True),
        name="gather_weights",
    )(own, mask)


def dot_top(left, right, dims):
    return lax.dot_general(
        left, right, (dims, ((), ())), precision=TOP_PRECISION, preferred_element_type=F32
    )


def shampoo_parts(grad, left, right, left_root, right_root, weight):
    new_left = STAT_DECAY * left + (1.0 - STAT_DECAY) * dot_top(grad, grad, ((1,), (1,)))
    new_right = STAT_DECAY * right + (1.0 - STAT_DECAY) * dot_top(grad, grad, ((0,), (0,)))
    precond = dot_top(dot_top(left_root, grad, ((1,), (0,))), right_root, ((1,), (0,)))
    scale = 1.0 / (grad.shape[0] * grad.shape[1])
    mean = jnp.sum(jnp.sum(precond * precond, 1, keepdims=True), 0, keepdims=True) * scale
    scale_back = lax.rsqrt(mean + ROOT_EPSILON)
    new_weight = weight * (1.0 - MATRIX_RATE * WEIGHT_DECAY) - MATRIX_RATE * precond * scale_back
    return new_left, new_right, new_weight


def block_update_kernel(
    stats_ref, grad_ref, left_ref, right_ref, left_root_ref, right_root_ref, weight_ref,
    grad_out, left_out, right_out, weight_out,
):
    factor = stats_ref[0:1, 0:1]
    for b in range(grad_ref.shape[0]):
        grad = grad_ref[b] * factor
        grad_out[b] = grad
        left_out[b], right_out[b], weight_out[b] = shampoo_parts(
            grad, left_ref[b], right_ref[b], left_root_ref[b], right_root_ref[b], weight_ref[b]
        )


def update_blocks(stats, grads, left, right, left_root, right_root, weight):
    count, edge, _ = grads.shape
    per_step = PACK if count % PACK == 0 else 1
    spec = pl.BlockSpec((per_step, edge, edge), lambda i: (i, 0, 0))
    out = jax.ShapeDtypeStruct(grads.shape, F32)
    return pl.pallas_call(
        block_update_kernel,
        out_shape=(out,) * 4,
        grid=(count // per_step,),
        in_specs=[whole(stats.shape)] + [spec] * 6,
        out_specs=(spec,) * 4,
        compiler_params=params(),
        name="update_blocks",
    )(stats, grads, left, right, left_root, right_root, weight)


def table_update_kernel(
    step_ref, stats_ref, grad_ref, left_ref, right_ref, left_root_ref, right_root_ref, weight_ref,
    norm_grad_ref, moment_ref, second_ref, norm_ref,
    grad_out, left_out, right_out, weight_out, norm_grad_out, moment_out, second_out, norm_out,
):
    factor = stats_ref[0:1, 0:1]
    grad = grad_ref[...] * factor
    grad_out[...] = grad
    left_out[...], right_out[...], weight_out[...] = shampoo_parts(
        grad, left_ref[...], right_ref[...], left_root_ref[...], right_root_ref[...], weight_ref[...]
    )
    rows = norm_ref.shape[0]
    clipped = norm_grad_ref[0:rows, :] * factor
    norm_grad_out[...] = clipped
    moment = FIRST_BETA * moment_ref[...] + (1.0 - FIRST_BETA) * clipped
    second = SECOND_BETA * second_ref[...] + (1.0 - SECOND_BETA) * clipped * clipped
    moment_out[...] = moment
    second_out[...] = second
    one = moment / step_ref[0:1, 0:1]
    two = second / step_ref[0:1, 1:2]
    weight = norm_ref[...]
    norm_out[...] = weight - VECTOR_RATE * (one / (jnp.sqrt(two) + ADAM_EPSILON) + WEIGHT_DECAY * weight)


def update_table(corrections, stats, grad, left, right, left_root, right_root, weight, norm_grad, moment, second, norms):
    like = lambda array: jax.ShapeDtypeStruct(array.shape, F32)
    return pl.pallas_call(
        table_update_kernel,
        out_shape=(like(grad), like(left), like(right), like(weight)) + (like(norms),) * 4,
        compiler_params=params(),
        name="update_table",
    )(corrections, stats, grad, left, right, left_root, right_root, weight, norm_grad, moment, second, norms)


def rotary_tables(length):
    half = HS // 2
    freqs = jnp.exp(-math.log(ROTARY_BASE) * (2.0 * jnp.arange(half, dtype=F32) / HS))
    angles = jnp.arange(length, dtype=F32)[:, None] * freqs[None, :]
    cosine, sine = jnp.cos(angles), jnp.sin(angles)
    repeats = LANES // HS
    return (
        jnp.concatenate([cosine, cosine] * repeats, -1),
        jnp.concatenate([-sine, sine] * repeats, -1),
    )


def pack_blocks(blocks):
    count, edge, _ = blocks.shape
    groups = blocks.reshape(count // PACK, PACK, edge, edge).transpose(0, 2, 1, 3)
    return groups.reshape(count // PACK, edge, PACK * edge)


def gather_weights(own, mask, known):
    everyone = ("dp", "tensor")
    slots, edge, _ = own.shape
    strip = PACK * edge
    if known:
        packed, count = gather_everywhere(pack_blocks(own), mask)
        packed = packed.reshape(HALVES, -1, edge // HALVES, strip)

        def place_of(owner, shard, slot):
            bits = bits_of(owner, shard)
            group = slot // PACK
            entry = gather_entry(0, bits)
            for g in range(1, PACK_GROUPS):
                entry = jnp.where(group == g, gather_entry(g, bits), entry)
            return (group * 32 + entry) * PACK + slot % PACK

        return packed, place_of, count
    packed = pack_blocks(lax.all_gather(own, everyone, axis=0, tiled=True))
    packed = packed.reshape(-1, HALVES, edge // HALVES, strip).transpose(1, 0, 2, 3)
    shards = lax.axis_size("tensor")
    count = jnp.maximum(lax.psum(jnp.sum(mask.astype(F32)), everyone), 1.0)
    return (
        packed,
        lambda owner, shard, slot: (owner * shards + shard) * slots + slot,
        jnp.broadcast_to(count, (8, LANES)),
    )


def body(
    codons,
    segments,
    targets,
    loss_mask,
    owner_map,
    step_count,
    block_weight,
    block_left,
    block_right,
    block_left_root,
    block_right_root,
    embedding_weight,
    table_left,
    table_right,
    table_left_root,
    table_right_root,
    norm_params,
    norm_moment,
    norm_second,
):
    everyone = ("dp", "tensor")
    vocab, width = embedding_weight.shape
    shards = lax.axis_size("tensor")
    owners = lax.axis_size("dp")
    slots = block_weight.shape[1]
    edge = block_weight.shape[-1]
    blocks = owner_map.shape[0]
    length = codons.shape[1]
    shard_width = width // shards

    known = on_known_slice(owners, shards, slots)
    packed, place_of, count = gather_weights(block_weight[0].astype(BF16), loss_mask, known)
    owner = jnp.broadcast_to((owner_map // slots)[None, :], (shards, blocks))
    slot = jnp.broadcast_to((owner_map % slots)[None, :], (shards, blocks))
    shard = jnp.broadcast_to(jnp.arange(shards, dtype=jnp.int32)[:, None], (shards, blocks))
    device = owner * shards + shard
    place = jnp.concatenate(block_tables(place_of(owner, shard, slot), width, shard_width, FF, edge))
    project, outward, expand, contract = assemble(place, packed, width, FF)

    mask_col = loss_mask.reshape(length, 1).astype(F32)
    codon_col = codons.reshape(length, 1)
    target_col = targets.reshape(length, 1)
    segment = lax.dynamic_index_in_dim(segments, lax.axis_index("tensor"), 0, keepdims=False)
    tiles = length // TILE
    seg_col = segment.reshape(length, 1)
    seg_row = segment.reshape(tiles, 1, TILE)
    tiled = segment.reshape(length // ROWS, ROWS)
    before = jnp.sum((segment[None, :] < tiled[:, :1]).astype(jnp.int32), -1)
    until = jnp.sum((segment[None, :] <= tiled[:, -1:]).astype(jnp.int32), -1)
    low, high = before // TILE, (until + TILE - 1) // TILE
    cosine, sine = rotary_tables(length)

    x0, h1, query, keys, values = front(codon_col, embedding_weight, norm_params, project, cosine, sine)
    attended, lse = attend(low, high, query, keys, values, seg_col, seg_row)
    (h2, active, d_two, ghid, d_one, gatt, gx, head_grad, norm_grad) = middle_rows(
        x0, attended, target_col, mask_col, count[:1, :1], norm_params, embedding_weight,
        outward, expand, contract,
    )
    gproj = attend_back(
        low, high, query, keys, values, gatt, lse, seg_col, seg_row, cosine, sine
    )
    table_grad, norm_grad = tail_rows(
        codon_col, x0, gx, gproj, norm_params, project, head_grad, norm_grad
    )

    if known:
        home = (slot // PACK * (owners * shards) + device) * PACK + slot % PACK
    else:
        home = device * slots + slot
    home = block_tables(home, width, shard_width, FF, edge)
    model = width // edge
    total = shards * blocks
    grads = weight_grad(by_strips(home[0], model, 3 * model, model), h1, gproj, None, total, edge, width, "grad_project")
    grads = weight_grad(by_strips(home[1], model, model, model), attended, d_one, grads, total, edge, width, "grad_outward")
    grads = weight_grad(by_strips(home[2], model, FF // edge, model), h2, ghid, grads, total, edge, width, "grad_expand")
    grads = weight_grad(by_strips(home[3], FF // edge, model, model), active, d_two, grads, total, edge, width, "grad_contract")
    if known:
        owned, table_grad, norm_grad, stats = sum_everywhere(
            grads.reshape(slots // PACK, owners * shards, PACK, edge, LANES), table_grad, norm_grad, count
        )
    else:
        owned = lax.psum_scatter(grads[:, :, :edge], everyone, scatter_dimension=0, tiled=True)
        table_grad, norm_grad, square_sum = lax.psum((table_grad, norm_grad), everyone) + (
            lax.psum(jnp.sum(owned * owned), everyone),
        )
        vectors = norm_grad[:6]
        square_sum = square_sum + jnp.sum(table_grad * table_grad) + jnp.sum(vectors * vectors)
        stats = statistics(square_sum, jnp.sum(norm_grad[6]), count[:1, :1])
    loss_value, grad_norm = stats[2, 0], stats[1, 0]
    step_value = step_count.astype(F32)
    corrections = jnp.stack([1.0 - FIRST_BETA**step_value, 1.0 - SECOND_BETA**step_value]).reshape(1, 2)
    block_grad, new_left, new_right, new_weight = update_blocks(
        stats, owned, block_left[0], block_right[0], block_left_root[0], block_right_root[0], block_weight[0]
    )
    (
        table_clipped, table_left_new, table_right_new, table_weight_new,
        norm_clipped, moment_new, second_new, params_new,
    ) = update_table(
        corrections, stats, table_grad, table_left, table_right, table_left_root, table_right_root,
        embedding_weight, norm_grad, norm_moment, norm_second, norm_params,
    )
    return (
        loss_value,
        grad_norm,
        block_grad[None],
        new_left[None],
        new_right[None],
        new_weight[None],
        table_clipped,
        table_left_new,
        table_right_new,
        table_weight_new,
        norm_clipped,
        moment_new,
        second_new,
        params_new,
    )


def solution(mesh):
    in_specs = (
        P(("dp", "tensor"), None),
        P("dp", None),
        P(("dp", "tensor"), None),
        P(("dp", "tensor"), None),
        P(),
        P(),
        P("tensor", "dp", None, None),
        P("tensor", "dp", None, None),
        P("tensor", "dp", None, None),
        P("tensor", "dp", None, None),
        P("tensor", "dp", None, None),
        P(),
        P(),
        P(),
        P(),
        P(),
        P(),
        P(),
        P(),
    )
    out_specs = (
        P(),
        P(),
        P("tensor", "dp", None, None),
        P("tensor", "dp", None, None),
        P("tensor", "dp", None, None),
        P("tensor", "dp", None, None),
        P(),
        P(),
        P(),
        P(),
        P(),
        P(),
        P(),
        P(),
    )
    return jax.shard_map(body, mesh=mesh, in_specs=in_specs, out_specs=out_specs, check_vma=False)
```

profile of v0, /device:TPU:0, one launch (start us, length us, event | category | flops | bytes accessed | tf_op | source)
XLA Modules:
  0.0 501.7 jit_solution(15964534524756916722)
XLA Ops:
  0.6 0.0 copy-start.3
  0.7 0.0 copy-start.2
  1.4 0.7 maximum_bitcast_fusion.step_ref
  2.1 0.7 convert_bitcast_fusion
  2.8 0.7 compare_and_fusion.1
  3.5 0.7 broadcast_add_fusion.3
  4.2 0.5 broadcast.190
  4.8 1.4 fusion.24
  6.1 0.0 copy-start.1
  6.2 0.2 slice_reduce_fusion
  6.3 0.2 convert_reduce_fusion
  6.6 0.5 and_select_fusion
  7.1 0.4 select_add_fusion.4
  7.6 0.1 copy.78
  7.6 0.1 reshape_reshape.12
  7.8 0.0 copy-start
  7.8 0.1 copy.79
  7.9 0.1 reshape.117
  8.0 0.1 copy.80
  8.1 0.1 reshape_reshape.13
  8.1 0.3 copy.77
  8.4 0.2 reshape.115
  8.6 0.7 pad_add_fusion.place_ref
  9.2 0.2 select_add_fusion.5
  9.5 0.1 copy.89
  9.6 0.1 reshape_reshape_reshape.7
  9.7 0.6 reshape.126.place_ref
  10.3 0.1 copy.87
  10.4 0.2 copy.95
  10.6 0.7 reshape.112.place_ref
  11.3 0.1 copy.91
  11.4 0.1 copy.92
  11.5 0.7 reshape.128.place_ref
  12.2 0.1 copy.88
  12.3 0.7 reshape.125.place_ref
  13.0 1.0 copy.85.mask_ref
  14.0 1.0 copy.83.seg_col_ref
  15.0 0.0 copy-done.2
  15.0 1.0 copy.82.codon_ref
  16.1 0.0 copy-done.3
  16.1 1.0 copy.84.target_ref
  17.1 0.0 copy-done.1
  17.1 0.0 copy-done
  17.1 0.1 convert_element_type.21
  17.2 0.3 copy.99
  17.5 1.2 reshape.118.own_ref
  18.7 2.0 fusion.2
  20.6 1.8 pad_maximum_fusion
  22.5 75.7 %gather_weights.1 = (bf16[12,32,48,384]{3,2,1,0:T(8,128)(2,1)}, f32[8,128]{1,0:T(8,128)}) custom-call(bf16[6,96,384]{2,1,0:T(8,128)(2,1)} %reshape.118.own_ref, s32[1,1024]{1,0:T(1,128)} %mask_ref.1), custom_call_target="tpu_custom_call" | custom-call | tf_op jit(solution)/shard_map/gather_weights/pallas_call | solution.py:1098
  98.1 1.2 slice.46.count_ref
  99.3 28.5 %assemble_weights.1 = (bf16[768,2304]{1,0:T(8,128)(2,1)}, bf16[768,768]{1,0:T(8,128)(2,1)}, bf16[768,3072]{1,0:T(8,128)(2,1)}, bf16[3072,768]{1,0:T(8,128)(2,1)}) custom-call(s32[768]{0:T(1024)} %pad_add_fusion.place_ref, bf16[2,192,48,384]{3,2,1,0:T(8,128)(2,1)} %bitcast.60), custom_call_target="tpu_custom_call" | custom-call | tf_op jit(solution)/shard_map/assemble_weights/pallas_call | solution.py:126
  127.8 11.5 %embed_project.1 = (f32[1024,768]{1,0:T(8,128)}, bf16[1024,768]{1,0:T(8,128)(2,1)}, bf16[1024,768]{1,0:T(8,128)(2,1)}, bf16[1024,768]{1,0:T(8,128)(2,1)}, bf16[1024,768]{1,0:T(8,128)(2,1)}) custom-call(s32[1024,1]{1,0:T(8,128)} %copy.82.codon_ref, f32[128,768]{1,0:T(8,128)} %weight_ref.1, f32[6,768]{1,0:T(8,128)} %norm_ref.7, ...), custom_call_target="tpu_custom_call" | custom-call | tf_op jit(solution)/shard_map/embed_project/pallas_call | solution.py:232
  139.4 33.4 %attend_forward.1 = (bf16[1024,768]{1,0:T(8,128)(2,1)}, f32[1024,768]{1,0:T(8,128)}) custom-call(s32[4]{0:T(128)} %get-tuple-element.139.low_ref, s32[4]{0:T(128)} %get-tuple-element.138.high_ref, bf16[1024,768]{1,0:T(8,128)(2,1)} %get-tuple-element.57.q_ref, bf16[1024,768]{1,0:T(8,128)(2,1)} %get-tuple-element.58.k_ref, ...), custom_call_target="tpu_custom_call" | custom-call | tf_op jit(solution)/shard_map/attend_forward/pallas_call | solution.py:298
  172.8 54.0 %middle_rows.1 = (bf16[1024,768]{1,0:T(8,128)(2,1)}, bf16[1024,3072]{1,0:T(8,128)(2,1)}, bf16[1024,768]{1,0:T(8,128)(2,1)}, bf16[1024,3072]{1,0:T(8,128)(2,1)}, ...) custom-call(f32[1024,768]{1,0:T(8,128)} %get-tuple-element.56.x_ref,, ...), custom_call_target="tpu_custom_call" | custom-call | tf_op jit(solution)/shard_map/middle_rows/pallas_call | solution.py:501
  226.8 44.0 %attend_backward.1.right_ref.gproj_ref = bf16[3,1024,768]{2,1,0:T(8,128)(2,1)} custom-call(s32[4]{0:T(128)} %get-tuple-element.139.low_ref, s32[4]{0:T(128)} %get-tuple-element.138.high_ref, bf16[1024,768]{1,0:T(8,128)(2,1)} %get-tuple-element.57.q_ref, bf16[1024,768]{1,0:T(8,128)(2,1)} %get-tuple-element.58.k_ref, ...), custom_call_target="tpu_custom_call" | custom-call | tf_op jit(solution)/shard_map/attend_backward/pallas_call | solution.py:386
  270.8 12.2 %tail_rows.1 = (f32[128,768]{1,0:T(8,128)}, f32[8,768]{1,0:T(8,128)}) custom-call(s32[1024,1]{1,0:T(8,128)} %copy.82.codon_ref, f32[1024,768]{1,0:T(8,128)} %get-tuple-element.56.x_ref, f32[1024,768]{1,0:T(8,128)} %get-tuple-element.73.gx_ref, bf16[3,1024,768]{2,1,0:T(8,128)(2,1)} %attend_backward.1.right_ref.gproj_ref, f32[6,768]{1,0:T(8,128)} %norm_ref.7, ...), custom_call_target="tpu_custom_call" | custom-call | tf_op jit(solution)/shard_map/tail_rows/pallas_call | solution.py:555
  282.9 11.3 %grad_project.1.rest_0_ = f32[768,96,128]{2,1,0:T(8,128)} custom-call(s32[192]{0:T(256)} %reshape.128.place_ref, bf16[1024,768]{1,0:T(8,128)(2,1)} %get-tuple-element.70.left_ref, bf16[3,1024,768]{2,1,0:T(8,128)(2,1)} %attend_backward.1.right_ref.gproj_ref), custom_call_target="tpu_custom_call" | custom-call | tf_op jit(solution)/shard_map/grad_project/pallas_call | solution.py:631
  294.3 6.0 %grad_outward.1.rest_0_ = f32[768,96,128]{2,1,0:T(8,128)} custom-call(s32[64]{0:T(128)} %reshape.126.place_ref, bf16[1024,768]{1,0:T(8,128)(2,1)} %get-tuple-element.60.att_ref.left_ref, bf16[1024,768]{1,0:T(8,128)(2,1)} %get-tuple-element.69.right_ref, f32[768,96,128]{2,1,0:T(8,128)} %grad_project.1.rest_0_), custom_call_target="tpu_custom_call", output_to_operand_aliasing={{}: (3, {})} | custom-call | tf_op jit(solution)/shard_map/grad_outward/pallas_call | solution.py:631
  300.3 13.6 %grad_expand.1.rest_0_ = f32[768,96,128]{2,1,0:T(8,128)} custom-call(s32[256]{0:T(256)} %reshape.125.place_ref, bf16[1024,768]{1,0:T(8,128)(2,1)} %get-tuple-element.67.left_ref, bf16[1024,3072]{1,0:T(8,128)(2,1)} %get-tuple-element.68.right_ref, f32[768,96,128]{2,1,0:T(8,128)} %grad_outward.1.rest_0_), custom_call_target="tpu_custom_call", output_to_operand_aliasing={{}: (3, {})} | custom-call | tf_op jit(solution)/shard_map/grad_expand/pallas_call | solution.py:631
  314.0 17.8 %grad_contract.1 = f32[768,96,128]{2,1,0:T(8,128)} custom-call(s32[256]{0:T(256)} %reshape.112.place_ref, bf16[1024,3072]{1,0:T(8,128)(2,1)} %get-tuple-element.65.left_ref, bf16[1024,768]{1,0:T(8,128)(2,1)} %get-tuple-element.66.right_ref, f32[768,96,128]{2,1,0:T(8,128)} %grad_expand.1.rest_0_), custom_call_target="tpu_custom_call", output_to_operand_aliasing={{}: (3, {})} | custom-call | tf_op jit(solution)/shard_map/grad_contract/pallas_call | solution.py:631
  331.7 148.7 %sum_gradients.1 = (f32[24,96,96]{2,1,0:T(8,128)}, f32[128,768]{1,0:T(8,128)}, f32[8,768]{1,0:T(8,128)}, f32[8,128]{1,0:T(8,128)}) custom-call(f32[6,32,4,96,128]{4,3,2,1,0:T(8,128)} %bitcast.59, f32[128,768]{1,0:T(8,128)} %get-tuple-element.76.table_ref, f32[8,768]{1,0:T(8,128)} %get-tuple-element.77.norm_ref, f32[8,128]{1,0:T(8,128)} %get-tuple-element.61.count_ref), custom_call_target="tpu_custom_call" | custom-call | tf_op jit(solution)/shard_map/sum_gradients/pallas_call | solution.py:959
  480.4 1.3 fusion.25
  481.7 7.5 %update_table.1 = (f32[128,768]{1,0:T(8,128)}, f32[128,128]{1,0:T(8,128)}, f32[768,768]{1,0:T(8,128)}, f32[128,768]{1,0:T(8,128)}, f32[6,768]{1,0:T(8,128)}, /*i...) custom-call(f32[1,2]{1,0:T(1,128)} %maximum_bitcast_fusion.step_ref, f32[8,128]{1,0:T(8,128)} %get-tuple-element.78.stats_ref, ...), custom_call_target="tpu_custom_call" | custom-call | tf_op jit(solution)/shard_map/update_table/pallas_call | solution.py:1191
  489.2 12.3 %update_blocks.1 = (f32[24,96,96]{2,1,0:T(8,128)}, f32[24,96,96]{2,1,0:T(8,128)}, f32[24,96,96]{2,1,0:T(8,128)}, f32[24,96,96]{2,1,0:T(8,128)}) custom-call(f32[8,128]{1,0:T(8,128)} %get-tuple-element.78.stats_ref, f32[24,96,96]{2,1,0:T(8,128)} %get-tuple-element.79.grad_ref, f32[24,96,96]{2,1,0:T(8,128)} %bitcast.64, f32[24,96,96]{2,1,0:T(8,128)} %bitcast.65, ...), custom_call_target="tpu_custom_call" | custom-call | tf_op jit(solution)/shard_map/update_blocks/pallas_call | solution.py:1154
  (15 shorter events, 0.1 us)
Async XLA Ops:
  0.6 15.4 %copy-start.3 = (s32[1,1024]{1,0:T(1,128)S(1)}, s32[1,1024]{1,0:T(1,128)}, u32[]{:S(2)}) copy-start(s32[1,1024]{1,0:T(1,128)} %param.21) | copy-start | bytes 12292
  0.7 14.4 %copy-start.2 = (s32[1,1024]{1,0:T(1,128)S(1)}, s32[1,1024]{1,0:T(1,128)}, u32[]{:S(2)}) copy-start(s32[1,1024]{1,0:T(1,128)} %param.19) | copy-start | bytes 12292
  6.1 11.0 %copy-start.1 = (s32[1,1024]{1,0:T(1,128)}, s32[1,1024]{1,0:T(1,128)S(1)}, u32[]{:S(2)}) copy-start(s32[1,1024]{1,0:T(1,128)S(1)} %get-tuple-element.99) | copy-start | bytes 12292
  7.8 9.4 %copy-start = (f32[1,24,96,96]{3,2,1,0:T(8,128)S(1)}, f32[1,24,96,96]{3,2,1,0:T(8,128)}, u32[]{:S(2)}) copy-start(f32[1,24,96,96]{3,2,1,0:T(8,128)} %param.25) | copy-start | bytes 2654212
where the time goes:
time: 508 us; the launch traced here: 502 us
  Pallas kernels  476 us (94%)
  local copies, waits for them, and re-layouts  14.6 us (3%)
  other arithmetic  8.81 us (2%)
    pallas_call x1, Pallas kernels, sum_everywhere(): pl.pallas_call(sum_kernel, out_shape=(jax.ShapeDtypeStruct((groups * PACK...  149 us
    pallas_call x1, Pallas kernels, gather_everywhere(): pl.pallas_call(gather_kernel, out_shape=(jax.ShapeDtypeStruct((GATHER_CHU...  75.7 us
    pallas_call x1, Pallas kernels, middle_rows(): pl.pallas_call(middle_kernel, out_shape=(low, low_broad, low, low_broad,...  54 us
    pallas_call x4, Pallas kernels, weight_grad(): pl.pallas_call(functools.partial(weight_grad_kernel, edge=edge), out_shap...  48.8 us
    pallas_call x1, Pallas kernels, attend_back(): pl.pallas_call(attend_back_kernel, out_shape=jax.ShapeDtypeStruct((3, len...  44 us
    pallas_call x1, Pallas kernels, attend(): pl.pallas_call(attend_kernel, out_shape=(jax.ShapeDtypeStruct((length, wi...  33.4 us
    pallas_call x1, Pallas kernels, assemble(): pl.pallas_call(functools.partial(assemble_kernel, load_steps=load_steps),...  28.5 us
    pallas_call x1, Pallas kernels, update_blocks(): pl.pallas_call(block_update_kernel, out_shape=(out,) * 4, grid=(count //...  12.3 us

commit v1 on v0

--- a/solution.py
+++ b/solution.py
@@ -64,57 +64,86 @@
     return [group[:, edge * j : edge * (j + 1)] for j in range(PACK)]
 
 
+def block_index(shard, block, blocks):
+    return shard * blocks + block
+
+
+def matrix_rows(row, width, shards, shard_width, hidden_width, edge):
+    model = width // edge
+    wide = shard_width // edge
+    tall = hidden_width // shards // edge
+    starts = [0, 3 * wide * model, 4 * wide * model, 4 * wide * model + model * tall]
+    blocks = starts[3] + tall * model
+    project = [
+        block_index(c % (shards * wide) // wide, row * 3 * wide + c // (shards * wide) * wide + c % wide, blocks)
+        for c in range(3 * model)
+    ]
+    outward = [
+        block_index(row // wide, starts[1] + row % wide * model + c, blocks) for c in range(model)
+    ]
+    expand = [
+        block_index(c // tall, starts[2] + row * tall + c % tall, blocks) for c in range(shards * tall)
+    ]
+    steps = model
+    each = shards * tall // steps
+    contract = []
+    for q in range(each):
+        r = row * each + q
+        contract.append(
+            [block_index(r // tall, starts[3] + r % tall * model + c, blocks) for c in range(model)]
+        )
+    return [project], [outward], [expand], contract
+
+
+def assemble_rows(tables, place_ref, store, targets, edge):
+    strip = PACK * edge
+    for block_rows, target in zip(tables, targets):
+        for r, places in enumerate(block_rows):
+            for c in range(len(places) // PACK):
+                blocks = [store[place_ref[places[c * PACK + j]]][:, :edge] for j in range(PACK)]
+                target[r * edge : (r + 1) * edge, c * strip : (c + 1) * strip] = jnp.concatenate(
+                    blocks, axis=1
+                )
+
+
+def unpack_rows(store, first, group, offset, edge):
+    pieces = unpack_group(group, edge)
+    for j in range(PACK):
+        store[first + j, offset : offset + group.shape[0], :edge] = pieces[j]
+
+
 def assemble_kernel(
-    place_ref, in_ref, project_ref, outward_ref, expand_ref, contract_ref, store, *, load_steps
+    place_ref, in_ref, project_ref, outward_ref, expand_ref, contract_ref, store, *, load_steps, sizes
 ):
     step = pl.program_id(0)
-    halves, per_step, part, strip_width = in_ref.shape
-    edge = strip_width // PACK
+    per_step, edge, _ = in_ref.shape
 
     @pl.when(step < load_steps)
     def _():
         def unpack(g, carry):
-            for h in range(halves):
-                pieces = unpack_group(in_ref[h, g], edge)
-                for j in range(PACK):
-                    store[(step * per_step + g) * PACK + j, h * part : (h + 1) * part, :edge] = pieces[j]
+            unpack_rows(store, (step * per_step + g) * PACK, in_ref[g], 0, edge)
             return carry
 
-        lax.fori_loop(0, per_step, unpack, 0, unroll=4)
+        lax.fori_loop(0, per_step, unpack, 0)
 
     @pl.when(step >= load_steps)
     def _():
-        row = step - load_steps
-        strip = PACK * edge
-
-        def fill(out_ref, rows, base):
-            strips = out_ref.shape[1] // strip
-
-            def body(k, carry):
-                r = k // strips
-                c = k - r * strips
-                first = base + k * PACK
-                blocks = [store[place_ref[first + j]][:, :edge] for j in range(PACK)]
-                out_ref[pl.ds(pl.multiple_of(r * edge, edge), edge), pl.ds(pl.multiple_of(c * strip, strip), strip)] = (
-                    jnp.concatenate(blocks, axis=1)
-                )
-                return carry
-
-            lax.fori_loop(0, rows * strips, body, 0, unroll=2)
-            return rows * strips * PACK
-
-        steps = pl.num_programs(0) - load_steps
-        offset = 0
-        for out_ref in (project_ref, outward_ref, expand_ref, contract_ref):
-            rows = out_ref.shape[0] // edge
-            count = rows * (out_ref.shape[1] // strip) * PACK
-            fill(out_ref, rows, offset + row * count)
-            offset = offset + count * steps
-
-
-def assemble(place, packed, width, hidden_width):
-    halves, groups, part, strip = packed.shape
-    edge = halves * part
+        tables = matrix_rows(step - load_steps, *sizes, edge)
+        assemble_rows(tables, place_ref, store, (project_ref, outward_ref, expand_ref, contract_ref), edge)
+
+
+def matrix_shapes(width, hidden_width):
+    return (
+        jax.ShapeDtypeStruct((width, 3 * width), BF16),
+        jax.ShapeDtypeStruct((width, width), BF16),
+        jax.ShapeDtypeStruct((width, hidden_width), BF16),
+        jax.ShapeDtypeStruct((hidden_width, width), BF16),
+    )
+
+
+def assemble(place, packed, sizes):
+    groups, edge, strip = packed.shape
+    width, _, _, hidden_width = sizes
     per_step = 16
     load_steps = groups // per_step
     fill_steps = width // edge
@@ -124,20 +153,14 @@
         return (jnp.maximum(step - load_steps, 0), 0)
 
     return pl.pallas_call(
-        functools.partial(assemble_kernel, load_steps=load_steps),
-        out_shape=(
-            jax.ShapeDtypeStruct((width, 3 * width), BF16),
-            jax.ShapeDtypeStruct((width, width), BF16),
-            jax.ShapeDtypeStruct((width, hidden_width), BF16),
-            jax.ShapeDtypeStruct((hidden_width, width), BF16),
-        ),
+        functools.partial(assemble_kernel, load_steps=load_steps, sizes=sizes),
+        out_shape=matrix_shapes(width, hidden_width),
         grid_spec=pltpu.PrefetchScalarGridSpec(
             num_scalar_prefetch=1,
             grid=(load_steps + fill_steps,),
             in_specs=[
                 pl.BlockSpec(
-                    (halves, per_step, part, strip),
-                    lambda s, *_: (0, jnp.minimum(s, load_steps - 1), 0, 0),
+                    (per_step, edge, strip), lambda s, *_: (jnp.minimum(s, load_steps - 1), 0, 0)
                 )
             ],
             out_specs=[
@@ -153,24 +176,6 @@
     )(place, packed)
 
 
-def block_tables(slot_place, width, shard_width, hidden_width, edge):
-    shards = slot_place.shape[0]
-    model = width // edge
-    wide = shard_width // edge
-    tall = hidden_width // shards // edge
-    ends = [3 * wide * model, wide * model, model * tall, tall * model]
-    pieces = []
-    offset = 0
-    for count in ends:
-        pieces.append(slot_place[:, offset : offset + count])
-        offset += count
-    project = pieces[0].reshape(shards, model, 3, wide).transpose(1, 2, 0, 3)
-    outward = pieces[1].reshape(shards * wide, model)
-    expand = pieces[2].reshape(shards, model, tall).transpose(1, 0, 2)
-    contract = pieces[3].reshape(shards * tall, model)
-    return [piece.reshape(-1) for piece in (project, outward, expand, contract)]
-
-
 def norm_parts(values):
     scale = 1.0 / values.shape[-1]
     center = values - jnp.sum(values, -1, keepdims=True) * scale
@@ -197,12 +202,12 @@
 
 
 def front_kernel(
-    codon_ref, table_ref, norm_ref, project_ref, cos_ref, sin_ref, x_ref, h_ref, q_ref, k_ref, v_ref
+    column_ref, table_ref, norm_ref, project_ref, cos_ref, sin_ref, x_ref, h_ref, q_ref, k_ref, v_ref
 ):
-    rows = codon_ref.shape[0]
+    rows = column_ref.shape[0]
     vocab, width = table_ref.shape
     index = lax.broadcasted_iota(jnp.int32, (rows, vocab), 1)
-    hot = jnp.where(codon_ref[...] == index, 1.0, 0.0).astype(BF16)
+    hot = jnp.where(column_ref[:, 0:1] == index, 1.0, 0.0).astype(BF16)
     high, middle, low = split_three(table_ref[...])
     embedded = (dot(hot, high) + dot(hot, middle)) + dot(hot, low)
     embedded = embedded * math.sqrt(width)
@@ -223,8 +228,8 @@
             out_ref[:, c * LANES : (c + 1) * LANES] = piece.astype(BF16)
 
 
-def front(codon_column, table, norm_params, project, cosine, sine):
-    length = codon_column.shape[0]
+def front(columns, table, norm_params, project, cosine, sine):
+    length, kinds = columns.shape
     vocab, width = table.shape
     rows = 256
     spec = pl.BlockSpec((rows, width), lambda i: (i, 0))
@@ -234,7 +239,7 @@
         out_shape=(jax.ShapeDtypeStruct((length, width), F32), low, low, low, low),
         grid=(length // rows,),
         in_specs=[
-            pl.BlockSpec((rows, 1), lambda i: (i, 0)),
+            pl.BlockSpec((rows, kinds), lambda i: (i, 0)),
             whole(table.shape),
             whole(norm_params.shape),
             whole(project.shape),
@@ -244,7 +249,7 @@
         out_specs=(spec, spec, spec, spec, spec),
         compiler_params=params(),
         name="embed_project",
-    )(codon_column, table, norm_params, project, cosine, sine)
+    )(columns, table, norm_params, project, cosine, sine)
 
 
 ROWS = 256
@@ -261,7 +266,7 @@
     return seg_col == row
 
 
-def attend_kernel(low_ref, high_ref, q_ref, k_ref, v_ref, seg_col_ref, seg_row_ref, o_ref, lse_ref):
+def attend_kernel(low_ref, high_ref, q_ref, k_ref, v_ref, column_ref, seg_row_ref, o_ref, lse_ref):
     part = pl.program_id(1)
     first, last = low_ref[part], high_ref[part]
     masks = head_masks(ROWS)
@@ -272,7 +277,7 @@
         span = pl.ds(pl.multiple_of(first * TILE, TILE), count * TILE)
         keys = k_ref[span, :]
         values = v_ref[span, :]
-        same = same_segment(seg_col_ref[...], seg_row_ref, first, count)
+        same = same_segment(column_ref[:, 3:4], seg_row_ref, first, count)
         outs, logs = [], []
         for mask in masks:
             scores = jnp.where(same, dot_nt(jnp.where(mask, query, zero), keys), MASK_VALUE)
@@ -289,7 +294,7 @@
         pl.when(last - first == count)(functools.partial(run, count))
 
 
-def attend(low, high, query, keys, values, seg_col, seg_row):
+def attend(low, high, query, keys, values, columns, seg_row):
     length, width = query.shape
     tiles = length // TILE
     pairs = width // LANES
@@ -308,18 +313,18 @@
                 column,
                 full,
                 full,
-                pl.BlockSpec((ROWS, 1), lambda p, i, *_: (i, 0)),
+                pl.BlockSpec((ROWS, columns.shape[1]), lambda p, i, *_: (i, 0)),
                 whole((tiles, 1, TILE)),
             ],
             out_specs=(column, column),
         ),
         compiler_params=params(),
         name="attend_forward",
-    )(low, high, query, keys, values, seg_col, seg_row)
+    )(low, high, query, keys, values, columns, seg_row)
 
 
 def attend_back_kernel(
-    low_ref, high_ref, q_ref, k_ref, v_ref, g_ref, lse_ref, seg_col_ref, seg_row_ref, cos_ref, sin_ref,
+    low_ref, high_ref, q_ref, k_ref, v_ref, g_ref, lse_ref, column_ref, seg_row_ref, cos_ref, sin_ref,
     out_ref, dk_acc, dv_acc,
 ):
     part = pl.program_id(1)
@@ -340,7 +345,7 @@
         span = pl.ds(pl.multiple_of(first * TILE, TILE), count * TILE)
         keys = k_ref[span, :]
         values = v_ref[span, :]
-        same = same_segment(seg_col_ref[...], seg_row_ref, first, count)
+        same = same_segment(column_ref[:, 3:4], seg_row_ref, first, count)
         dq = []
         dk = dv = None
         for h, mask in enumerate(masks):
@@ -377,7 +382,7 @@
             out_ref[2, rows, :] = dv_acc[j].T.astype(BF16)
 
 
-def attend_back(low, high, query, keys, values, grad, lse, seg_col, seg_row, cosine, sine):
+def attend_back(low, high, query, keys, values, grad, lse, columns, seg_row, cosine, sine):
     length, width = query.shape
     tiles = length // TILE
     pairs = width // LANES
@@ -395,7 +400,7 @@
                 full,
                 column,
                 column,
-                pl.BlockSpec((ROWS, 1), lambda p, i, *_: (i, 0)),
+                pl.BlockSpec((ROWS, columns.shape[1]), lambda p, i, *_: (i, 0)),
                 whole((tiles, 1, TILE)),
                 whole((length, LANES)),
                 whole((length, LANES)),
@@ -408,7 +413,7 @@
         ),
         compiler_params=params(),
         name="attend_backward",
-    )(low, high, query, keys, values, grad, lse, seg_col, seg_row, cosine, sine)
+    )(low, high, query, keys, values, grad, lse, columns, seg_row, cosine, sine)
 
 
 INV_SQRT_TWO = 2.0 ** (-0.5)
@@ -416,7 +421,7 @@
 
 
 def middle_kernel(
-    x_ref, att_ref, target_ref, mask_ref, count_ref, norm_ref, table_ref,
+    x_ref, att_ref, column_ref, count_ref, norm_ref, table_ref,
     outward_ref, expand_ref, contract_ref,
     h_ref, active_ref, d_two_ref, ghid_ref, d_one_ref, gatt_ref, gx_ref, head_ref, norm_grad_ref,
     slope,
@@ -457,12 +462,12 @@
     shifted = logits - jnp.max(logits, -1, keepdims=True)
     exps = jnp.exp(shifted)
     sums = jnp.sum(exps, -1, keepdims=True)
-    hot = target_ref[...] == lax.broadcasted_iota(jnp.int32, (rows, vocab), 1)
-    mask = mask_ref[...]
+    hot = column_ref[:, 1:2] == lax.broadcasted_iota(jnp.int32, (rows, vocab), 1)
+    mask = column_ref[:, 2:3].astype(F32)
     log_probs = shifted - jnp.log(sums)
     picked = jnp.sum(jnp.where(hot, log_probs, 0.0) * mask, 0, keepdims=True)
     norm_grad_ref[6:7, 0:vocab] -= picked
-    glogits = ((jnp.exp(log_probs) - jnp.where(hot, 1.0, 0.0)) * (mask / count_ref[...])).astype(BF16)
+    glogits = ((jnp.exp(log_probs) - jnp.where(hot, 1.0, 0.0)) * (mask / count_ref[0:1, 0:1])).astype(BF16)
     head_ref[...] += dot_tn(glogits, final)
     gfinal = dot(glogits, table)
     norm_grad_ref[4:5, :] += jnp.sum(gfinal * unit, 0, keepdims=True)
@@ -488,14 +493,14 @@
     gatt_ref[...] = dot_nt(d_one, outward_ref[...]).astype(BF16)
 
 
-def middle_rows(x, att, target_col, mask_col, count, norm_params, table, outward, expand, contract):
+def middle_rows(x, att, columns, count, norm_params, table, outward, expand, contract):
     length, width = x.shape
     vocab = table.shape[0]
     ff = expand.shape[1]
-    rows = 256
+    rows = 512
     narrow = pl.BlockSpec((rows, width), lambda i: (i, 0))
     broad = pl.BlockSpec((rows, ff), lambda i: (i, 0))
-    column = pl.BlockSpec((rows, 1), lambda i: (i, 0))
+    column = pl.BlockSpec((rows, columns.shape[1]), lambda i: (i, 0))
     low = jax.ShapeDtypeStruct((length, width), BF16)
     low_broad = jax.ShapeDtypeStruct((length, ff), BF16)
     return pl.pallas_call(
@@ -508,7 +513,7 @@
         ),
         grid=(length // rows,),
         in_specs=[
-            narrow, narrow, column, column, whole((1, 1)), whole(norm_params.shape), whole(table.shape),
+            narrow, narrow, column, whole(count.shape), whole(norm_params.shape), whole(table.shape),
             whole(outward.shape), whole(expand.shape), whole(contract.shape),
         ],
         out_specs=(
@@ -518,11 +523,11 @@
         scratch_shapes=[pltpu.VMEM((rows, ff), F32)],
         compiler_params=params(),
         name="middle_rows",
-    )(x, att, target_col, mask_col, count, norm_params, table, outward, expand, contract)
+    )(x, att, columns, count, norm_params, table, outward, expand, contract)
 
 
 def tail_kernel(
-    codon_ref, x_ref, gx_ref, gproj_ref, norm_ref, project_ref, head_ref, norm_in_ref,
+    column_ref, x_ref, gx_ref, gproj_ref, norm_ref, project_ref, head_ref, norm_in_ref,
     table_grad_ref, norm_grad_ref,
 ):
     step = pl.program_id(0)
@@ -541,14 +546,14 @@
     norm_grad_ref[0:1, :] += jnp.sum(gh * unit, 0, keepdims=True)
     norm_grad_ref[1:2, :] += jnp.sum(gh, 0, keepdims=True)
     gx = gx_ref[...] + norm_back(gh, unit, inverse, norm_ref[0:1, :])
-    hot = jnp.where(codon_ref[...] == lax.broadcasted_iota(jnp.int32, (rows, vocab), 1), 1.0, 0.0)
+    hot = jnp.where(column_ref[:, 0:1] == lax.broadcasted_iota(jnp.int32, (rows, vocab), 1), 1.0, 0.0)
     hot = hot.T.astype(BF16)
     high, middle, low = split_three(gx)
     total = dot(hot, high) + (dot(hot, middle) + dot(hot, low))
     table_grad_ref[...] += total * math.sqrt(width)
 
 
-def tail_rows(codon_col, x, gx, gproj, norm_params, project, head, norm_in):
+def tail_rows(columns, x, gx, gproj, norm_params, project, head, norm_in):
     length, width = x.shape
     rows = 256
     narrow = pl.BlockSpec((rows, width), lambda i: (i, 0))
@@ -560,97 +565,131 @@
         ),
         grid=(length // rows,),
         in_specs=[
-            pl.BlockSpec((rows, 1), lambda i: (i, 0)),
+            pl.BlockSpec((rows, columns.shape[1]), lambda i: (i, 0)),
             narrow, narrow, pl.BlockSpec((3, rows, width), lambda i: (0, i, 0)),
             whole(norm_params.shape), whole(project.shape), whole(head.shape), whole(norm_in.shape),
         ],
         out_specs=(whole(head.shape), whole(norm_in.shape)),
         compiler_params=params(),
         name="tail_rows",
-    )(codon_col, x, gx, gproj, norm_params, project, head, norm_in)
-
-
-def weight_grad_kernel(place_ref, left_ref, right_ref, *rest, edge):
-    out_ref, buf, turned, sem = rest[-4:]
-    strip_index = pl.program_id(1)
-    step = pl.program_id(0) * pl.num_programs(1) + strip_index
-    steps = pl.num_programs(0) * pl.num_programs(1)
+    )(columns, x, gx, gproj, norm_params, project, head, norm_in)
+
+
+def weight_grad_kernel(
+    place_ref, h_one, att, h_two, active, gproj, d_one, ghid, d_two, out_ref,
+    left, right, turned, buf, left_sem, right_sem, out_sem, *, sizes, edge,
+):
+    width, shards, shard_width, hidden_width = sizes
+    model = width // edge
+    wide = shard_width // edge
+    tall = hidden_width // shards // edge
+    starts = [0, 3 * wide * model, 4 * wide * model, 4 * wide * model + model * tall]
+    blocks = starts[3] + tall * model
+    part = hidden_width // shards
+    columns = lambda ref, t: ref.at[:, pl.ds(t * part, part)]
+    lefts = [h_one, att, h_two] + [columns(active, t) for t in range(shards)]
+    rights = [gproj.at[i] for i in range(3)] + [d_one] + [columns(ghid, t) for t in range(shards)] + [d_two]
+    plan = [(0, 0), (0, 1), (0, 2), (1, 3)]
+    plan += [(2, 4 + t) for t in range(shards)]
+    plan += [(3 + t, 4 + shards) for t in range(shards)]
+    step = pl.program_id(0)
+    slot = step % 2
     count = buf.shape[1]
-    slot = lax.rem(step, 2)
-    block_rows = count // PACK
+
+    def fetches(n):
+        found = []
+        if n == 0 or plan[n][0] != plan[n - 1][0]:
+            which = plan[n][0] % 2
+            found.append(pltpu.make_async_copy(lefts[plan[n][0]], left.at[which], left_sem.at[which]))
+        if n == 0 or plan[n][1] != plan[n - 1][1]:
+            which = plan[n][1] % 2
+            found.append(pltpu.make_async_copy(rights[plan[n][1]], right.at[which], right_sem.at[which]))
+        return found
 
     def drain(which):
-        pltpu.make_async_copy(buf.at[which], out_ref.at[pl.ds(0, count)], sem.at[which]).wait()
-
-    @pl.when(strip_index == 0)
-    def _():
-        turned[...] = left_ref[...].T
+        pltpu.make_async_copy(buf.at[which], out_ref.at[pl.ds(0, count)], out_sem.at[which]).wait()
+
+    for n in range(len(plan)):
+
+        @pl.when(step == n)
+        def _():
+            if n == 0:
+                for copy in fetches(0):
+                    copy.start()
+            for copy in fetches(n):
+                copy.wait()
+            if n + 1 < len(plan):
+                for copy in fetches(n + 1):
+                    copy.start()
+            if n == 0 or plan[n][0] != plan[n - 1][0]:
+                turned[...] = left[plan[n][0] % 2].T
 
     @pl.when(step >= 2)
     def _():
         drain(slot)
 
-    right = right_ref[...]
-    for r in range(block_rows):
-        result = dot(turned[r * edge : (r + 1) * edge, :], right)
-        pieces = unpack_group(result, edge)
-        for j in range(PACK):
-            buf[slot, r * PACK + j, :, :edge] = pieces[j]
-        for j in range(PACK):
-            k = r * PACK + j
-            target = place_ref[step * count + k]
-            pltpu.make_async_copy(buf.at[slot, k], out_ref.at[target], sem.at[slot]).start()
-
-    @pl.when(step == steps - 1)
+    which = jnp.minimum(step, 4 + shards) % 2
+    rows = turned.shape[0] // 2
+    for half in range(2):
+        result = dot(turned[half * rows : (half + 1) * rows], right[which])
+        for i in range(rows // edge):
+            r = half * (rows // edge) + i
+            for c in range(model // PACK):
+                pieces = unpack_group(
+                    result[i * edge : (i + 1) * edge, c * PACK * edge : (c + 1) * PACK * edge], edge
+                )
+                for j in range(PACK):
+                    buf[slot, r * model + c * PACK + j, :, :edge] = pieces[j]
+            for c in range(model):
+                index = block_index(c // wide, r * 3 * wide + step * wide + c % wide, blocks)
+                index = jnp.where(
+                    step == 3, block_index(r // wide, starts[1] + r % wide * model + c, blocks), index
+                )
+                index = jnp.where(
+                    step >= 4, block_index(step - 4, starts[2] + r * tall + c, blocks), index
+                )
+                index = jnp.where(
+                    step >= 4 + shards,
+                    block_index(step - 4 - shards, starts[3] + r * model + c, blocks),
+                    index,
+                )
+                k = r * model + c
+                pltpu.make_async_copy(
+                    buf.at[slot, k], out_ref.at[place_ref[index]], out_sem.at[slot]
+                ).start()
+
+    @pl.when(step == len(plan) - 1)
     def _():
-        @pl.when(step >= 1)
-        def _():
-            drain(1 - slot)
-
+        drain(1 - slot)
         drain(slot)
 
 
-def weight_grad(place, left, right, into, blocks, edge, left_cols, name):
-    length, tall = left.shape
-    strip = PACK * edge
-    count = left_cols // edge * PACK
-    if right.ndim == 3:
-        strips = right.shape[2] // strip
-        right_spec = pl.BlockSpec((None, length, strip), lambda a, b, *_: (b // strips, 0, b % strips))
-        grid = (tall // left_cols, right.shape[0] * strips)
-    else:
-        right_spec = pl.BlockSpec((length, strip), lambda a, b, *_: (0, b))
-        grid = (tall // left_cols, right.shape[1] // strip)
-    operands = [place, left, right]
-    in_specs = [pl.BlockSpec((length, left_cols), lambda a, b, *_: (0, a)), right_spec]
-    aliases = {}
-    if into is not None:
-        operands.append(into)
-        in_specs.append(pl.BlockSpec(memory_space=pl.ANY))
-        aliases = {3: 0}
+def weight_grads(place, h_one, att, h_two, active, gproj, d_one, ghid, d_two, sizes, blocks, edge):
+    length, width = h_one.shape
+    shards = sizes[1]
+    count = (width // edge) ** 2
+    anywhere = pl.BlockSpec(memory_space=pl.ANY)
     return pl.pallas_call(
-        functools.partial(weight_grad_kernel, edge=edge),
+        functools.partial(weight_grad_kernel, sizes=sizes, edge=edge),
         out_shape=jax.ShapeDtypeStruct((blocks, edge, LANES), F32),
         grid_spec=pltpu.PrefetchScalarGridSpec(
             num_scalar_prefetch=1,
-            grid=grid,
-            in_specs=in_specs,
-            out_specs=pl.BlockSpec(memory_space=pl.ANY),
+            grid=(4 + 2 * shards,),
+            in_specs=[anywhere] * 8,
+            out_specs=anywhere,
             scratch_shapes=[
+                pltpu.VMEM((2, length, width), BF16),
+                pltpu.VMEM((2, length, width), BF16),
+                pltpu.VMEM((width, length), BF16),
                 pltpu.VMEM((2, count, edge, LANES), F32),
-                pltpu.VMEM((left_cols, length), BF16),
+                pltpu.SemaphoreType.DMA((2,)),
+                pltpu.SemaphoreType.DMA((2,)),
                 pltpu.SemaphoreType.DMA((2,)),
             ],
         ),
-        input_output_aliases=aliases,
         compiler_params=params(),
-        name=name,
-    )(*operands)
-
-
-def by_strips(table, rows, cols, chunk):
-    shaped = table.reshape(rows // chunk, chunk, cols // PACK, PACK)
-    return shaped.transpose(0, 2, 1, 3).reshape(-1)
+        name="weight_gradients",
+    )(place, h_one, att, h_two, active, gproj, d_one, ghid, d_two)
 
 
 CORE, NEAR_Y, NEAR_X, NEAR_Z, FAR_Z = range(5)
@@ -717,13 +756,16 @@
     return (owner + step - 2 * step * bits[axis], shard)
 
 
-def meet_partners(owner, shard, bits):
+def greet_partners(owner, shard, bits):
     barrier = pltpu.get_barrier_semaphore()
     for axis in range(5):
         pl.semaphore_signal(
             barrier, inc=1, device_id=partner_of(axis, owner, shard, bits), device_id_type=MESH
         )
-    pl.semaphore_wait(barrier, 5)
+
+
+def await_partners():
+    pl.semaphore_wait(pltpu.get_barrier_semaphore(), 5)
 
 
 def total_of(values):
@@ -760,7 +802,8 @@
 
     for c in range(SUM_SLOTS):
         fetch(c).start()
-    meet_partners(owner, shard, bits)
+    greet_partners(owner, shard, bits)
+    await_partners()
 
     def chunk_send(c, k):
         if k == 0:
@@ -994,54 +1037,59 @@
 
 
 GATHER_AXES = (
-    (NEAR_Z, NEAR_X, NEAR_Y),
-    (NEAR_Z, NEAR_Y, NEAR_X),
-    (NEAR_X, NEAR_Y, NEAR_Z),
-    (NEAR_Y, NEAR_X, NEAR_Z),
-    (NEAR_X, NEAR_Y, NEAR_Z),
-    (NEAR_Y, NEAR_X, NEAR_Z),
+    (NEAR_Z, NEAR_Y, NEAR_X, FAR_Z),
+    (NEAR_X, NEAR_Y, NEAR_Z, FAR_Z),
+    (NEAR_Y, NEAR_X, FAR_Z, NEAR_Z),
+    (NEAR_Z, NEAR_Y, FAR_Z, NEAR_X),
+    (NEAR_X, NEAR_Z, FAR_Z, NEAR_Y),
+    (NEAR_Y, NEAR_X, FAR_Z, NEAR_Z),
 )
 HALVES = 2
 GATHER_CHUNKS = PACK_GROUPS * HALVES
 GATHER_ORDER = (
-    2000, 2010, 2020, 2030, 1000, 2001, 1010, 2011, 2040, 2050, 1020, 2021, 1030, 1001, 2002, 1011, 2012, 2060,
-    2070, 2031, 1040, 2041, 1050, 1021, 2022, 2080, 2090, 2051, 1031, 2032, 1002, 1012, 1060, 1070, 2003, 1041,
-    2061, 2100, 2110, 2071, 2042, 1051, 1022, 1080, 1090, 2052, 1032, 1061, 2033, 1071, 1100, 1110, 2081, 2062,
-    1042, 2091, 1003, 2004, 1052, 2101, 2023, 1081, 2111, 2072, 1091, 1004, 1062, 2013, 1101, 1033, 2034, 1111,
-    2082, 2092, 1034, 1072, 2102, 1023, 2024, 2063, 2112, 1082, 2053, 1013, 2014, 1092, 1024, 2043, 1102, 1014,
-    1112, 2073, 2093, 1063, 2064, 2083, 1053, 2054, 1043, 2044, 1064, 1054, 2113, 1073, 2074, 1044, 2103, 1093,
-    2094, 1074, 1083, 2084, 1094, 1084, 1113, 2114, 1103, 2104, 1114, 1104,
+    2030, 2090, 2100, 2040, 2080, 2060, 2020, 2070, 2110, 2010, 1080, 1030, 1100, 1090, 1040, 1060, 2061, 2050,
+    2081, 1020, 1070, 2071, 1110, 1010, 2021, 1061, 2062, 1050, 2011, 1081, 2082, 2031, 1071, 2072, 1062, 2063,
+    1021, 2022, 2101, 1011, 2012, 1082, 2083, 1072, 2073, 1031, 2032, 2111, 1022, 1101, 2000, 2023, 2091, 1012,
+    2013, 1111, 2112, 1000, 2001, 2041, 1073, 2074, 2102, 1063, 2064, 1091, 2092, 1074, 2051, 1032, 1064, 1041,
+    1001, 2033, 1112, 2113, 1102, 2103, 1051, 2052, 1083, 2084, 1013, 2014, 2002, 1084, 2042, 1092, 1014, 1033,
+    2034, 1023, 2024, 2093, 1052, 2053, 1034, 1042, 2043, 1024, 1103, 2104, 1002, 2003, 1104, 1093, 2094, 1113,
+    2114, 1043, 2044, 1094, 1114, 1053, 2054, 1044, 1003, 2004, 1054, 1004,
 )
 
 
 def gather_entry(group, bits):
-    first, second, third = GATHER_AXES[group]
-    return 16 * bits[CORE] + 8 * bits[first] + 4 * bits[second] + 2 * bits[third] + bits[FAR_Z]
-
-
-def gather_kernel(own_ref, mask_ref, out_ref, count_ref, counts, own_sem, send_sem, recv_sem, count_send, count_recv):
+    first, second, third, fourth = GATHER_AXES[group]
+    return 16 * bits[CORE] + 8 * bits[first] + 4 * bits[second] + 2 * bits[third] + bits[fourth]
+
+
+def gather_kernel(
+    place_ref, own_ref, mask_ref, project_out, outward_out, expand_out, contract_out, count_ref,
+    packed, held, store, project, outward, expand, contract, counts,
+    own_sem, send_sem, recv_sem, count_send, count_recv, out_sem, *, sizes,
+):
     owner, shard, bits = own_bits()
-    rows = own_ref.shape[1] // HALVES
+    edge = own_ref.shape[1]
+    rows = edge // HALVES
+    devices = held.shape[1]
 
     def place(c):
         return gather_entry(c % PACK_GROUPS, bits)
 
+    def own_part(c):
+        return packed.at[c % PACK_GROUPS, pl.ds(c // PACK_GROUPS * rows, rows)]
+
     def keep(c):
-        part = pl.ds(c // PACK_GROUPS * rows, rows)
-        return pltpu.make_async_copy(
-            own_ref.at[c % PACK_GROUPS, part], out_ref.at[c, place(c)], own_sem.at[c]
-        )
+        return pltpu.make_async_copy(own_part(c), held.at[c, place(c)], own_sem.at[c])
 
     def move(c, k):
+        axis = CORE if k == 4 else GATHER_AXES[c % PACK_GROUPS][3 - k]
         if k == 0:
-            axis = FAR_Z
-            source = own_ref.at[c % PACK_GROUPS, pl.ds(c // PACK_GROUPS * rows, rows)]
-            target = out_ref.at[c, place(c)]
+            source = own_part(c)
+            target = held.at[c, place(c)]
         else:
-            axis = CORE if k == 4 else GATHER_AXES[c % PACK_GROUPS][3 - k]
             size = 1 << k
             base = place(c) // size * size
-            source = out_ref.at[c, pl.ds(base, size)]
+            source = held.at[c, pl.ds(base, size)]
             target = source
         return pltpu.make_async_remote_copy(
             src_ref=source,
@@ -1062,20 +1110,37 @@
             device_id_type=MESH,
         )
 
+    greet_partners(owner, shard, bits)
+    for g in range(PACK_GROUPS):
+        blocks = [own_ref[g * PACK + b].astype(BF16) for b in range(PACK)]
+        packed[g] = jnp.concatenate(blocks, axis=1)
+    total = jnp.broadcast_to(jnp.sum(mask_ref[...].astype(F32), keepdims=True), count_ref.shape)
+    counts[0] = total
+    await_partners()
     for c in range(GATHER_CHUNKS):
         keep(c).start()
-    total = jnp.broadcast_to(jnp.sum(mask_ref[...].astype(F32), keepdims=True), count_ref.shape)
-    counts[0] = total
-    meet_partners(owner, shard, bits)
+
+    def unpack(c):
+        group = c % PACK_GROUPS
+        offset = c // PACK_GROUPS * rows
+
+        def body(e, carry):
+            unpack_rows(store, (group * devices + e) * PACK, held[c, e], offset, edge)
+            return carry
+
+        lax.fori_loop(0, devices, body, 0, unroll=2)
+
     stage = 0
     for position, code in enumerate(GATHER_ORDER):
         c, k = code % 1000 // 10, code % 10
-        if code < 2000:
-            move(c, k).wait_recv()
-        else:
+        if code >= 2000:
             if k == 1:
                 keep(c).wait()
             move(c, k).start()
+        else:
+            move(c, k).wait_recv()
+            if k == 4:
+                unpack(c)
         if position == 0:
             count_copy(0).start()
         elif position % 12 == 0 and stage < 5:
@@ -1086,34 +1151,63 @@
                 counts[stage] = total
                 count_copy(stage).start()
     count_ref[...] = jnp.maximum(total, 1.0)
+
+    steps = project.shape[0] // edge
+    staged = ((project, project_out), (outward, outward_out), (expand, expand_out), (contract, contract_out))
+
+    def body(row, carry):
+        tables = matrix_rows(row, *sizes, edge)
+        targets, copies = [], []
+        for n, (inside, outside) in enumerate(staged):
+            size = inside.shape[0] // steps
+            part = pl.ds(pl.multiple_of(row * size, size), size)
+            targets.append(inside.at[part])
+            copies.append(pltpu.make_async_copy(inside.at[part], outside.at[part], out_sem.at[n]))
+        assemble_rows(tables, place_ref, store, targets, edge)
+        for copy in copies:
+            copy.start()
+        return carry
+
+    lax.fori_loop(0, steps, body, 0)
     for c in range(GATHER_CHUNKS):
         for k in range(5):
             move(c, k).wait_send()
     for k in range(5):
         count_copy(k).wait_send()
-
-
-def gather_everywhere(own, mask):
-    groups, edge, strip = own.shape
+    for n, (inside, outside) in enumerate(staged):
+        pltpu.make_async_copy(inside, outside, out_sem.at[n]).wait()
+
+
+def gather_everywhere(place, own, mask, devices, sizes):
+    slots, edge, _ = own.shape
+    width, _, _, hidden_width = sizes
+    strip = PACK * edge
+    shapes = matrix_shapes(width, hidden_width)
     return pl.pallas_call(
-        gather_kernel,
-        out_shape=(
-            jax.ShapeDtypeStruct((GATHER_CHUNKS, 32, edge // HALVES, strip), own.dtype),
-            jax.ShapeDtypeStruct((8, LANES), F32),
-        ),
-        in_specs=[pl.BlockSpec(memory_space=pltpu.VMEM)] * 2,
-        out_specs=(pl.BlockSpec(memory_space=pl.ANY), pl.BlockSpec(memory_space=pltpu.VMEM)),
+        functools.partial(gather_kernel, sizes=sizes),
+        out_shape=shapes + (jax.ShapeDtypeStruct((8, LANES), F32),),
+        in_specs=[
+            pl.BlockSpec(memory_space=pltpu.SMEM),
+            pl.BlockSpec(memory_space=pltpu.VMEM),
+            pl.BlockSpec(memory_space=pltpu.VMEM),
+        ],
+        out_specs=(pl.BlockSpec(memory_space=pl.ANY),) * 4 + (pl.BlockSpec(memory_space=pltpu.VMEM),),
         scratch_shapes=[
+            pltpu.VMEM((PACK_GROUPS, edge, strip), BF16),
+            pltpu.VMEM((GATHER_CHUNKS, devices, edge // HALVES, strip), BF16),
+            pltpu.VMEM((devices * slots, edge, LANES), BF16),
+            *[pltpu.VMEM(shape.shape, shape.dtype) for shape in shapes],
             pltpu.VMEM((10, 8, LANES), F32),
             pltpu.SemaphoreType.DMA((GATHER_CHUNKS,)),
             pltpu.SemaphoreType.DMA((GATHER_CHUNKS, 5)),
             pltpu.SemaphoreType.DMA((GATHER_CHUNKS, 5)),
             pltpu.SemaphoreType.DMA((5,)),
             pltpu.SemaphoreType.DMA((5,)),
+            pltpu.SemaphoreType.DMA((4,)),
         ],
-        compiler_params=pltpu.CompilerParams(collective_id=2, has_side_effects=True),
+        compiler_params=params(collective_id=2, has_side_effects=True),
         name="gather_weights",
-    )(own, mask)
+    )(place, own, mask)
 
 
 def dot_top(left, right, dims):
@@ -1197,15 +1291,12 @@
 
 
 def rotary_tables(length):
+    lane = jnp.arange(LANES, dtype=jnp.int32)[None, :]
     half = HS // 2
-    freqs = jnp.exp(-math.log(ROTARY_BASE) * (2.0 * jnp.arange(half, dtype=F32) / HS))
-    angles = jnp.arange(length, dtype=F32)[:, None] * freqs[None, :]
-    cosine, sine = jnp.cos(angles), jnp.sin(angles)
-    repeats = LANES // HS
-    return (
-        jnp.concatenate([cosine, cosine] * repeats, -1),
-        jnp.concatenate([-sine, sine] * repeats, -1),
-    )
+    freqs = jnp.exp(-math.log(ROTARY_BASE) * (2.0 * (lane % half).astype(F32) / HS))
+    angles = jnp.arange(length, dtype=F32)[:, None] * freqs
+    sine = jnp.sin(angles)
+    return jnp.cos(angles), jnp.where(lane % HS < half, -sine, sine)
 
 
 def pack_blocks(blocks):
@@ -1214,32 +1305,24 @@
     return groups.reshape(count // PACK, edge, PACK * edge)
 
 
-def gather_weights(own, mask, known):
+def gather_weights(own, mask, owner_map, known, sizes):
     everyone = ("dp", "tensor")
     slots, edge, _ = own.shape
-    strip = PACK * edge
+    shards = sizes[1]
+    owner, slot = owner_map[None, :] // slots, owner_map[None, :] % slots
+    shard = jnp.arange(shards, dtype=jnp.int32)[:, None]
     if known:
-        packed, count = gather_everywhere(pack_blocks(own), mask)
-        packed = packed.reshape(HALVES, -1, edge // HALVES, strip)
-
-        def place_of(owner, shard, slot):
-            bits = bits_of(owner, shard)
-            group = slot // PACK
-            entry = gather_entry(0, bits)
-            for g in range(1, PACK_GROUPS):
-                entry = jnp.where(group == g, gather_entry(g, bits), entry)
-            return (group * 32 + entry) * PACK + slot % PACK
-
-        return packed, place_of, count
-    packed = pack_blocks(lax.all_gather(own, everyone, axis=0, tiled=True))
-    packed = packed.reshape(-1, HALVES, edge // HALVES, strip).transpose(1, 0, 2, 3)
-    shards = lax.axis_size("tensor")
+        bits = bits_of(owner, shard)
+        group = slot // PACK
+        entry = gather_entry(0, bits)
+        for g in range(1, PACK_GROUPS):
+            entry = jnp.where(group == g, gather_entry(g, bits), entry)
+        place = ((group * 32 + entry) * PACK + slot % PACK).reshape(-1)
+        return gather_everywhere(place, own, mask, 32, sizes)
+    packed = pack_blocks(lax.all_gather(own.astype(BF16), everyone, axis=0, tiled=True))
     count = jnp.maximum(lax.psum(jnp.sum(mask.astype(F32)), everyone), 1.0)
-    return (
-        packed,
-        lambda owner, shard, slot: (owner * shards + shard) * slots + slot,
-        jnp.broadcast_to(count, (8, LANES)),
-    )
+    place = ((owner * shards + shard) * slots + slot).reshape(-1)
+    return assemble(place, packed, sizes) + (jnp.broadcast_to(count, (8, LANES)),)
 
 
 def body(
@@ -1274,20 +1357,13 @@
     shard_width = width // shards
 
     known = on_known_slice(owners, shards, slots)
-    packed, place_of, count = gather_weights(block_weight[0].astype(BF16), loss_mask, known)
-    owner = jnp.broadcast_to((owner_map // slots)[None, :], (shards, blocks))
-    slot = jnp.broadcast_to((owner_map % slots)[None, :], (shards, blocks))
-    shard = jnp.broadcast_to(jnp.arange(shards, dtype=jnp.int32)[:, None], (shards, blocks))
-    device = owner * shards + shard
-    place = jnp.concatenate(block_tables(place_of(owner, shard, slot), width, shard_width, FF, edge))
-    project, outward, expand, contract = assemble(place, packed, width, FF)
-
-    mask_col = loss_mask.reshape(length, 1).astype(F32)
-    codon_col = codons.reshape(length, 1)
-    target_col = targets.reshape(length, 1)
+    sizes = (width, shards, shard_width, FF)
+    project, outward, expand, contract, count = gather_weights(
+        block_weight[0], loss_mask, owner_map, known, sizes
+    )
     segment = lax.dynamic_index_in_dim(segments, lax.axis_index("tensor"), 0, keepdims=False)
     tiles = length // TILE
-    seg_col = segment.reshape(length, 1)
+    columns = jnp.stack([codons[0], targets[0], loss_mask[0], segment], 1)
     seg_row = segment.reshape(tiles, 1, TILE)
     tiled = segment.reshape(length // ROWS, ROWS)
     before = jnp.sum((segment[None, :] < tiled[:, :1]).astype(jnp.int32), -1)
@@ -1295,30 +1371,28 @@
     low, high = before // TILE, (until + TILE - 1) // TILE
     cosine, sine = rotary_tables(length)
 
-    x0, h1, query, keys, values = front(codon_col, embedding_weight, norm_params, project, cosine, sine)
-    attended, lse = attend(low, high, query, keys, values, seg_col, seg_row)
+    x0, h1, query, keys, values = front(columns, embedding_weight, norm_params, project, cosine, sine)
+    attended, lse = attend(low, high, query, keys, values, columns, seg_row)
     (h2, active, d_two, ghid, d_one, gatt, gx, head_grad, norm_grad) = middle_rows(
-        x0, attended, target_col, mask_col, count[:1, :1], norm_params, embedding_weight,
+        x0, attended, columns, count, norm_params, embedding_weight,
         outward, expand, contract,
     )
     gproj = attend_back(
-        low, high, query, keys, values, gatt, lse, seg_col, seg_row, cosine, sine
+        low, high, query, keys, values, gatt, lse, columns, seg_row, cosine, sine
     )
     table_grad, norm_grad = tail_rows(
-        codon_col, x0, gx, gproj, norm_params, project, head_grad, norm_grad
+        columns, x0, gx, gproj, norm_params, project, head_grad, norm_grad
     )
 
+    owner, slot = owner_map[None, :] // slots, owner_map[None, :] % slots
+    device = owner * shards + jnp.arange(shards, dtype=jnp.int32)[:, None]
     if known:
         home = (slot // PACK * (owners * shards) + device) * PACK + slot % PACK
     else:
         home = device * slots + slot
-    home = block_tables(home, width, shard_width, FF, edge)
-    model = width // edge
-    total = shards * blocks
-    grads = weight_grad(by_strips(home[0], model, 3 * model, model), h1, gproj, None, total, edge, width, "grad_project")
-    grads = weight_grad(by_strips(home[1], model, model, model), attended, d_one, grads, total, edge, width, "grad_outward")
-    grads = weight_grad(by_strips(home[2], model, FF // edge, model), h2, ghid, grads, total, edge, width, "grad_expand")
-    grads = weight_grad(by_strips(home[3], FF // edge, model, model), active, d_two, grads, total, edge, width, "grad_contract")
+    grads = weight_grads(
+        home.reshape(-1), h1, attended, h2, active, gproj, d_one, ghid, d_two, sizes, shards * blocks, edge
+    )
     if known:
         owned, table_grad, norm_grad, stats = sum_everywhere(
             grads.reshape(slots // PACK, owners * shards, PACK, edge, LANES), table_grad, norm_grad, count

time: 508 us -> 453 us (0.89)
  Pallas kernels: 476 us -> 430 us
  local copies, waits for them, and re-layouts: 14.6 us -> 5.33 us
    pallas_call x6 -> x2, Pallas kernels: 153 us -> 111 us  [the longest x1 80 us: gather_everywhere(): pl.pallas_call(functools.partial(gather_kernel, sizes=sizes), out_shape=s...]
    pallas_call x1, Pallas kernels: 149 us -> 162 us  [sum_everywhere(): pl.pallas_call(sum_kernel, out_shape=(jax.ShapeDtypeStruct((groups * PACK...]
    reshape x12 -> x0, local copies, waits for them, and re-layouts: 7.23 us -> none  [the longest x4 2.59 us: by_strips(): return shaped.transpose(0, 2, 1, 3).reshape(-1)]
    pallas_call x1, Pallas kernels: 44 us -> 36.8 us  [attend_back(): pl.pallas_call(attend_back_kernel, out_shape=jax.ShapeDtypeStruct((3, len...]
    pallas_call x1, Pallas kernels: 54 us -> 48.2 us  [middle_rows(): pl.pallas_call(middle_kernel, out_shape=(low, low_broad, low, low_broad,...]
where the time goes in v1:
time: 453 us; the launch traced here: 444 us
  Pallas kernels  430 us (95%)
  other arithmetic  7.07 us (2%)
  local copies, waits for them, and re-layouts  5.33 us (1%)
    pallas_call x1, Pallas kernels, sum_everywhere(): pl.pallas_call(sum_kernel, out_shape=(jax.ShapeDtypeStruct((groups * PACK...  162 us
    pallas_call x1, Pallas kernels, gather_everywhere(): pl.pallas_call(functools.partial(gather_kernel, sizes=sizes), out_shape=s...  80 us
    pallas_call x1, Pallas kernels, middle_rows(): pl.pallas_call(middle_kernel, out_shape=(low, low_broad, low, low_broad,...  48.2 us
    pallas_call x1, Pallas kernels, attend_back(): pl.pallas_call(attend_back_kernel, out_shape=jax.ShapeDtypeStruct((3, len...  36.8 us
    pallas_call x1, Pallas kernels, weight_grads(): pl.pallas_call(functools.partial(weight_grad_kernel, sizes=sizes, edge=ed...  31.2 us
    pallas_call x1, Pallas kernels, attend(): pl.pallas_call(attend_kernel, out_shape=(jax.ShapeDtypeStruct((length, wi...  29 us
    pallas_call x1, Pallas kernels, update_blocks(): pl.pallas_call(block_update_kernel, out_shape=(out,) * 4, grid=(count //...  12.3 us
    pallas_call x1, Pallas kernels, tail_rows(): pl.pallas_call(tail_kernel, out_shape=(jax.ShapeDtypeStruct(head.shape, F...  12.1 us

profile of v1, /device:TPU:0, one launch (start us, length us, event | category | flops | bytes accessed | tf_op | source)
XLA Modules:
  0.0 444.5 jit_solution(3936382116850036377)
XLA Ops:
  0.6 0.7 broadcast_multiply_fusion.7
  1.4 0.7 broadcast_compare_fusion.4
  2.1 0.1 fusion.5
  2.2 0.1 add.400
  2.3 0.1 add.409
  2.3 0.1 add.417
  2.4 0.1 reshape.314
  2.5 0.1 add.382
  2.6 0.1 broadcast_in_dim.71
  2.7 0.1 broadcast_in_dim.73
  2.8 0.1 broadcast_in_dim.75
  2.9 0.1 broadcast_in_dim.77
  3.0 0.1 add.386
  3.1 0.1 add.378
  3.2 0.6 multiply_add_fusion
  3.8 80.0 %gather_weights.1 = (bf16[768,2304]{1,0:T(8,128)(2,1)}, bf16[768,768]{1,0:T(8,128)(2,1)}, bf16[768,3072]{1,0:T(8,128)(2,1)}, bf16[3072,768]{1,0:T(8,128)(2,1)}, f32[8,128]{1,0:T(8,128)}) custom-call(s32[768]{0:T(1024)} %get-tuple-element.107.place_ref, f32[24,96,96]{2,1,0:T(8,128)} %bitcast.23, s32[1,1024]{1,0:T(1,128)} %mask_ref.1), custom_call_target="tpu_custom_call" | custom-call | tf_op jit(solution)/shard_map/gather_weights/pallas_call | solution.py:1186
  83.8 0.5 broadcast.410
  84.3 1.4 fusion.12
  85.7 0.0 copy-start
  85.7 0.7 pad_add_fusion
  86.5 1.0 copy.46.column_ref
  87.5 2.8 negate_select_fusion
  90.4 11.5 %embed_project.1 = (f32[1024,768]{1,0:T(8,128)}, bf16[1024,768]{1,0:T(8,128)(2,1)}, bf16[1024,768]{1,0:T(8,128)(2,1)}, bf16[1024,768]{1,0:T(8,128)(2,1)}, bf16[1024,768]{1,0:T(8,128)(2,1)}) custom-call(s32[1024,4]{1,0:T(8,128)} %copy.46.column_ref, f32[128,768]{1,0:T(8,128)} %weight_ref.1, f32[6,768]{1,0:T(8,128)} %norm_ref.7, ...), custom_call_target="tpu_custom_call" | custom-call | tf_op jit(solution)/shard_map/embed_project/pallas_call | solution.py:237
  101.9 0.2 slice_reduce_fusion
  102.1 0.0 copy-done
  102.1 0.2 convert_reduce_fusion
  102.3 0.5 and_select_fusion
  102.9 29.0 %attend_forward.1 = (bf16[1024,768]{1,0:T(8,128)(2,1)}, f32[1024,768]{1,0:T(8,128)}) custom-call(s32[4]{0:T(128)} %get-tuple-element.139.low_ref, s32[4]{0:T(128)} %get-tuple-element.138.high_ref, bf16[1024,768]{1,0:T(8,128)(2,1)} %get-tuple-element.55.q_ref, bf16[1024,768]{1,0:T(8,128)(2,1)} %get-tuple-element.56.k_ref, ...), custom_call_target="tpu_custom_call" | custom-call | tf_op jit(solution)/shard_map/attend_forward/pallas_call | solution.py:303
  131.9 48.2 %middle_rows.1 = (bf16[1024,768]{1,0:T(8,128)(2,1)}, bf16[1024,3072]{1,0:T(8,128)(2,1)}, bf16[1024,768]{1,0:T(8,128)(2,1)}, bf16[1024,3072]{1,0:T(8,128)(2,1)}, ...) custom-call(f32[1024,768]{1,0:T(8,128)} %get-tuple-element.59.x_ref,, ...), custom_call_target="tpu_custom_call" | custom-call | tf_op jit(solution)/shard_map/middle_rows/pallas_call | solution.py:506
  180.1 36.8 %attend_backward.1.gproj.gproj_ref = bf16[3,1024,768]{2,1,0:T(8,128)(2,1)} custom-call(s32[4]{0:T(128)} %get-tuple-element.139.low_ref, s32[4]{0:T(128)} %get-tuple-element.138.high_ref, bf16[1024,768]{1,0:T(8,128)(2,1)} %get-tuple-element.55.q_ref, bf16[1024,768]{1,0:T(8,128)(2,1)} %get-tuple-element.56.k_ref, bf16[1024,768]{1,0:T(8,128)(2,1)} %get-tuple-element.57.v_ref, ...), custom_call_target="tpu_custom_call" | custom-call | tf_op jit(solution)/shard_map/attend_backward/pallas_call | solution.py:391
  216.9 12.1 %tail_rows.1 = (f32[128,768]{1,0:T(8,128)}, f32[8,768]{1,0:T(8,128)}) custom-call(s32[1024,4]{1,0:T(8,128)} %copy.46.column_ref, f32[1024,768]{1,0:T(8,128)} %get-tuple-element.59.x_ref, f32[1024,768]{1,0:T(8,128)} %get-tuple-element.71.gx_ref, bf16[3,1024,768]{2,1,0:T(8,128)(2,1)} %attend_backward.1.gproj.gproj_ref, f32[6,768]{1,0:T(8,128)} %norm_ref.7, ...), custom_call_target="tpu_custom_call" | custom-call | tf_op jit(solution)/shard_map/tail_rows/pallas_call | solution.py:560
  229.0 31.2 %weight_gradients.1 = f32[768,96,128]{2,1,0:T(8,128)} custom-call(s32[768]{0:T(1024)} %get-tuple-element.108.place_ref, bf16[1024,768]{1,0:T(8,128)(2,1)} %get-tuple-element.54.h_one, bf16[1024,768]{1,0:T(8,128)(2,1)} %get-tuple-element.58.att_ref.att, bf16[1024,768]{1,0:T(8,128)(2,1)} %get-tuple-element.64.h_two, ...), custom_call_target="tpu_custom_call" | custom-call | tf_op jit(solution)/shard_map/weight_gradients/pallas_call | solution.py:672
  260.2 161.5 %sum_gradients.1 = (f32[24,96,96]{2,1,0:T(8,128)}, f32[128,768]{1,0:T(8,128)}, f32[8,768]{1,0:T(8,128)}, f32[8,128]{1,0:T(8,128)}) custom-call(f32[6,32,4,96,128]{4,3,2,1,0:T(8,128)} %bitcast.22, f32[128,768]{1,0:T(8,128)} %get-tuple-element.74.table_ref, f32[8,768]{1,0:T(8,128)} %get-tuple-element.75.norm_ref, f32[8,128]{1,0:T(8,128)} %get-tuple-element.60.count_ref), custom_call_target="tpu_custom_call" | custom-call | tf_op jit(solution)/shard_map/sum_gradients/pallas_call | solution.py:1002
  422.4 0.6 maximum_bitcast_fusion.step_ref
  423.0 7.5 %update_table.1 = (f32[128,768]{1,0:T(8,128)}, f32[128,128]{1,0:T(8,128)}, f32[768,768]{1,0:T(8,128)}, f32[128,768]{1,0:T(8,128)}, f32[6,768]{1,0:T(8,128)}, /*i...) custom-call(f32[1,2]{1,0:T(1,128)} %maximum_bitcast_fusion.step_ref, f32[8,128]{1,0:T(8,128)} %get-tuple-element.76.stats_ref, ...), custom_call_target="tpu_custom_call" | custom-call | tf_op jit(solution)/shard_map/update_table/pallas_call | solution.py:1285
  430.5 12.3 %update_blocks.1 = (f32[24,96,96]{2,1,0:T(8,128)}, f32[24,96,96]{2,1,0:T(8,128)}, f32[24,96,96]{2,1,0:T(8,128)}, f32[24,96,96]{2,1,0:T(8,128)}) custom-call(f32[8,128]{1,0:T(8,128)} %get-tuple-element.76.stats_ref, f32[24,96,96]{2,1,0:T(8,128)} %get-tuple-element.77.grad_ref, f32[24,96,96]{2,1,0:T(8,128)} %bitcast.25, f32[24,96,96]{2,1,0:T(8,128)} %bitcast.26, ...), custom_call_target="tpu_custom_call" | custom-call | tf_op jit(solution)/shard_map/update_blocks/pallas_call | solution.py:1248
  442.7 1.3 fusion.13
  (16 shorter events, 0.1 us)
Async XLA Ops:
  85.7 16.4 %copy-start = (s32[1,1024]{1,0:T(1,128)}, s32[1,1024]{1,0:T(1,128)S(1)}, u32[]{:S(2)}) copy-start(s32[1,1024]{1,0:T(1,128)S(1)} %get-tuple-element.97) | copy-start | bytes 12292

commit v2 on v1

--- a/solution.py
+++ b/solution.py
@@ -23,7 +23,6 @@
 ROOT_EPSILON = 1e-06
 MASK_VALUE = -1e30
 ROTARY_BASE = 10000.0
-TOP_PRECISION = lax.Precision.HIGHEST
 
 LANES = 128
 PACK = 4
@@ -58,6 +57,37 @@
 
 def whole(shape):
     return pl.BlockSpec(shape, lambda *_: (0,) * len(shape))
+
+
+def dense_rows(edge):
+    return edge * edge // LANES
+
+
+def to_dense(block):
+    half, quarter = block.shape[0] // 2, block.shape[0] // 4
+    wide, slim = LANES // 2, LANES // 4
+    return (
+        jnp.concatenate([block[:half, :wide], block[half:, :wide]], axis=1),
+        jnp.concatenate(
+            [block[i * quarter : (i + 1) * quarter, wide : wide + slim] for i in range(4)], axis=1
+        ),
+    )
+
+
+def from_dense(dense):
+    half = dense.shape[0] * 2 // 3
+    quarter = half // 2
+    wide, slim = LANES // 2, LANES // 4
+    quarters = []
+    for i in range(4):
+        start = i % 2 * quarter
+        lanes = slice(i // 2 * wide, (i // 2 + 1) * wide)
+        quarters.append(
+            jnp.concatenate(
+                [dense[start : start + quarter, lanes], dense[half:, i * slim : (i + 1) * slim]], axis=1
+            )
+        )
+    return quarters
 
 
 def unpack_group(group, edge):
@@ -266,9 +296,9 @@
     return seg_col == row
 
 
-def attend_kernel(low_ref, high_ref, q_ref, k_ref, v_ref, column_ref, seg_row_ref, o_ref, lse_ref):
+def attend_kernel(low_ref, half_ref, q_ref, k_ref, v_ref, column_ref, seg_row_ref, o_ref, lse_ref):
     part = pl.program_id(1)
-    first, last = low_ref[part], high_ref[part]
+    first, half = low_ref[part], half_ref[part]
     masks = head_masks(ROWS)
 
     def run(count):
@@ -290,11 +320,11 @@
         o_ref[...] = jnp.where(masks[0], outs[0], outs[1]).astype(BF16)
         lse_ref[...] = jnp.where(masks[0], logs[0], logs[1])
 
-    for count in range(1, k_ref.shape[0] // TILE + 1):
-        pl.when(last - first == count)(functools.partial(run, count))
-
-
-def attend(low, high, query, keys, values, columns, seg_row):
+    for n in range(1, k_ref.shape[0] // TILE // 2 + 1):
+        pl.when(half == n)(functools.partial(run, 2 * n))
+
+
+def attend(low, half, query, keys, values, columns, seg_row):
     length, width = query.shape
     tiles = length // TILE
     pairs = width // LANES
@@ -320,17 +350,17 @@
         ),
         compiler_params=params(),
         name="attend_forward",
-    )(low, high, query, keys, values, columns, seg_row)
+    )(low, half, query, keys, values, columns, seg_row)
 
 
 def attend_back_kernel(
-    low_ref, high_ref, q_ref, k_ref, v_ref, g_ref, lse_ref, column_ref, seg_row_ref, cos_ref, sin_ref,
+    low_ref, half_ref, q_ref, k_ref, v_ref, g_ref, lse_ref, column_ref, seg_row_ref, cos_ref, sin_ref,
     out_ref, dk_acc, dv_acc,
 ):
     part = pl.program_id(1)
     parts = pl.num_programs(1)
     heads = LANES // HS
-    first, last = low_ref[part], high_ref[part]
+    first, half = low_ref[part], half_ref[part]
     masks = head_masks(ROWS)
 
     @pl.when(part == 0)
@@ -371,8 +401,8 @@
         )
         out_ref[0, rows, :] = turned.astype(BF16)
 
-    for count in range(1, k_ref.shape[0] // TILE + 1):
-        pl.when(last - first == count)(functools.partial(run, count))
+    for n in range(1, k_ref.shape[0] // TILE // 2 + 1):
+        pl.when(half == n)(functools.partial(run, 2 * n))
 
     @pl.when(part == parts - 1)
     def _():
@@ -382,7 +412,7 @@
             out_ref[2, rows, :] = dv_acc[j].T.astype(BF16)
 
 
-def attend_back(low, high, query, keys, values, grad, lse, columns, seg_row, cosine, sine):
+def attend_back(low, half, query, keys, values, grad, lse, columns, seg_row, cosine, sine):
     length, width = query.shape
     tiles = length // TILE
     pairs = width // LANES
@@ -413,7 +443,7 @@
         ),
         compiler_params=params(),
         name="attend_backward",
-    )(low, high, query, keys, values, grad, lse, columns, seg_row, cosine, sine)
+    )(low, half, query, keys, values, grad, lse, columns, seg_row, cosine, sine)
 
 
 INV_SQRT_TWO = 2.0 ** (-0.5)
@@ -526,31 +556,36 @@
     )(x, att, columns, count, norm_params, table, outward, expand, contract)
 
 
+def tail_part(codon_col, x, gx, gprojs, norm_params, project, table_acc, norm_acc):
+    rows, width = x.shape
+    vocab = table_acc.shape[0]
+    gh = dot_nt(gprojs[0], project[:, 0:width])
+    gh = gh + dot_nt(gprojs[1], project[:, width : 2 * width])
+    gh = gh + dot_nt(gprojs[2], project[:, 2 * width : 3 * width])
+    unit, inverse = norm_parts(x)
+    norm_acc[0:1, :] += jnp.sum(gh * unit, 0, keepdims=True)
+    norm_acc[1:2, :] += jnp.sum(gh, 0, keepdims=True)
+    gx = gx + norm_back(gh, unit, inverse, norm_params[0:1, :])
+    hot = jnp.where(codon_col == lax.broadcasted_iota(jnp.int32, (rows, vocab), 1), 1.0, 0.0)
+    hot = hot.T.astype(BF16)
+    high, middle, low = split_three(gx)
+    total = dot(hot, high) + (dot(hot, middle) + dot(hot, low))
+    table_acc[...] += total * math.sqrt(width)
+
+
 def tail_kernel(
     column_ref, x_ref, gx_ref, gproj_ref, norm_ref, project_ref, head_ref, norm_in_ref,
     table_grad_ref, norm_grad_ref,
 ):
-    step = pl.program_id(0)
-    rows, width = x_ref.shape
-    vocab = head_ref.shape[0]
-
-    @pl.when(step == 0)
+    @pl.when(pl.program_id(0) == 0)
     def _():
         table_grad_ref[...] = head_ref[...]
         norm_grad_ref[...] = norm_in_ref[...]
 
-    gh = dot_nt(gproj_ref[0], project_ref[:, 0:width])
-    gh = gh + dot_nt(gproj_ref[1], project_ref[:, width : 2 * width])
-    gh = gh + dot_nt(gproj_ref[2], project_ref[:, 2 * width : 3 * width])
-    unit, inverse = norm_parts(x_ref[...])
-    norm_grad_ref[0:1, :] += jnp.sum(gh * unit, 0, keepdims=True)
-    norm_grad_ref[1:2, :] += jnp.sum(gh, 0, keepdims=True)
-    gx = gx_ref[...] + norm_back(gh, unit, inverse, norm_ref[0:1, :])
-    hot = jnp.where(column_ref[:, 0:1] == lax.broadcasted_iota(jnp.int32, (rows, vocab), 1), 1.0, 0.0)
-    hot = hot.T.astype(BF16)
-    high, middle, low = split_three(gx)
-    total = dot(hot, high) + (dot(hot, middle) + dot(hot, low))
-    table_grad_ref[...] += total * math.sqrt(width)
+    tail_part(
+        column_ref[:, 0:1], x_ref[...], gx_ref[...], gproj_ref, norm_ref, project_ref,
+        table_grad_ref, norm_grad_ref,
+    )
 
 
 def tail_rows(columns, x, gx, gproj, norm_params, project, head, norm_in):
@@ -634,12 +669,11 @@
         result = dot(turned[half * rows : (half + 1) * rows], right[which])
         for i in range(rows // edge):
             r = half * (rows // edge) + i
-            for c in range(model // PACK):
-                pieces = unpack_group(
-                    result[i * edge : (i + 1) * edge, c * PACK * edge : (c + 1) * PACK * edge], edge
-                )
-                for j in range(PACK):
-                    buf[slot, r * model + c * PACK + j, :, :edge] = pieces[j]
+            for c in range(model):
+                block = result[i * edge : (i + 1) * edge, c * edge : (c + 1) * edge]
+                upper, lower = to_dense(block)
+                buf[slot, r * model + c, : edge // 2] = upper
+                buf[slot, r * model + c, edge // 2 :] = lower
             for c in range(model):
                 index = block_index(c // wide, r * 3 * wide + step * wide + c % wide, blocks)
                 index = jnp.where(
@@ -671,7 +705,7 @@
     anywhere = pl.BlockSpec(memory_space=pl.ANY)
     return pl.pallas_call(
         functools.partial(weight_grad_kernel, sizes=sizes, edge=edge),
-        out_shape=jax.ShapeDtypeStruct((blocks, edge, LANES), F32),
+        out_shape=jax.ShapeDtypeStruct((blocks, dense_rows(edge), LANES), F32),
         grid_spec=pltpu.PrefetchScalarGridSpec(
             num_scalar_prefetch=1,
             grid=(4 + 2 * shards,),
@@ -681,7 +715,7 @@
                 pltpu.VMEM((2, length, width), BF16),
                 pltpu.VMEM((2, length, width), BF16),
                 pltpu.VMEM((width, length), BF16),
-                pltpu.VMEM((2, count, edge, LANES), F32),
+                pltpu.VMEM((2, count, dense_rows(edge), LANES), F32),
                 pltpu.SemaphoreType.DMA((2,)),
                 pltpu.SemaphoreType.DMA((2,)),
                 pltpu.SemaphoreType.DMA((2,)),
@@ -694,6 +728,7 @@
 
 CORE, NEAR_Y, NEAR_X, NEAR_Z, FAR_Z = range(5)
 AXIS_STRIDE = {CORE: 1, NEAR_Y: 2, NEAR_X: 4, NEAR_Z: 8, FAR_Z: 16}
+NATURAL = (FAR_Z, NEAR_Z, NEAR_X, NEAR_Y)
 CHUNK_AXES = (
     (NEAR_X, NEAR_Y, NEAR_Z, FAR_Z),
     (NEAR_Y, NEAR_X, NEAR_Z, FAR_Z),
@@ -703,25 +738,24 @@
     (NEAR_Z, NEAR_Y, NEAR_X, FAR_Z),
 )
 PACK_GROUPS = 6
-QUARTERS = 4
-SUM_CHUNKS = PACK_GROUPS * QUARTERS
-SUM_SLOTS = 3
+SUM_CHUNKS = PACK_GROUPS * PACK
+SUM_SLOTS = 6
 SUM_ORDER = (
-    0, 2000, 10, 2010, 20, 2020, 1000, 2001, 1010, 2011, 1020, 2021, 30, 2030, 40, 2040, 50, 2050, 1030, 2031, 1040,
-    2041, 1050, 2051, 60, 2060, 70, 2070, 1011, 80, 2012, 2080, 1001, 2002, 1060, 2061, 1070, 1080, 2071, 90, 2090,
-    1021, 100, 2100, 1031, 2032, 110, 2110, 2022, 1012, 1090, 2013, 1002, 1100, 2003, 120, 2120, 1041, 1110, 2101,
-    1051, 130, 2130, 2042, 140, 2140, 2111, 1013, 2052, 2014, 1120, 1032, 1003, 2081, 2004, 1022, 150, 2150, 1130,
-    2091, 1061, 1014, 1140, 160, 2160, 1004, 1071, 2072, 1150, 2062, 170, 2170, 1042, 180, 2180, 1052, 1160, 190,
-    2190, 2023, 1170, 1180, 2053, 1101, 200, 2200, 2043, 2033, 210, 2210, 2102, 2161, 1072, 1190, 1062, 1023, 2024,
-    1111, 2121, 2112, 1081, 2063, 220, 2220, 2082, 1200, 1053, 2054, 1033, 2034, 1091, 1043, 1210, 1024, 2073, 230,
-    2230, 1220, 2092, 2044, 1063, 2064, 1102, 2103, 1054, 2171, 1034, 1230, 2131, 1112, 1073, 2074, 1082, 2151,
-    1044, 1064, 1103, 2104, 2083, 2113, 1074, 2141, 1161, 1092, 1121, 2093, 1104, 2162, 1083, 2084, 1113, 2114,
-    2221, 1093, 2094, 2231, 1084, 2122, 1114, 2181, 1171, 2172, 1131, 1094, 1162, 1151, 2132, 1141, 2142, 2163,
-    1122, 1172, 2123, 2191, 2152, 1221, 1163, 2164, 1132, 2133, 2211, 2173, 1231, 1123, 2124, 1142, 2143, 1181,
-    1164, 1133, 2134, 2201, 2222, 1124, 1143, 2144, 1173, 2174, 1152, 2153, 1134, 1153, 2154, 1144, 1174, 2182,
-    1191, 2192, 1222, 2223, 1154, 1211, 2212, 1201, 2202, 2232, 1223, 2224, 1182, 2183, 1192, 2193, 1224, 1212,
-    2213, 1183, 2184, 1202, 2203, 1193, 2194, 1232, 2233, 1184, 1213, 2214, 1203, 2204, 1233, 2234, 1194, 1214,
-    1204, 1234,
+    0, 2000, 10, 20, 2010, 30, 40, 50, 2020, 1000, 2001, 2030, 60, 1010, 2011, 2040, 70, 1020, 2021, 2050, 80, 1030,
+    2031, 2060, 90, 1040, 2041, 2070, 100, 1050, 2051, 2080, 110, 1060, 2090, 120, 1070, 2100, 130, 1080, 2061,
+    2110, 140, 1090, 2071, 2120, 150, 1100, 1001, 2130, 160, 1110, 1011, 2140, 170, 2012, 1120, 2150, 180, 2002,
+    1130, 2101, 2160, 190, 1140, 1021, 2170, 200, 2111, 1150, 1031, 1041, 2180, 210, 1160, 2190, 220, 2032, 1170,
+    1051, 2200, 230, 2022, 1180, 2042, 2210, 1190, 2052, 1012, 2220, 1200, 1002, 1061, 2230, 1210, 1071, 2072, 1220,
+    2062, 1230, 2081, 2003, 1032, 2091, 2013, 1022, 1101, 1042, 2023, 1052, 2053, 1111, 2033, 2043, 1003, 2004,
+    2161, 1072, 2102, 1013, 2014, 1062, 2112, 1023, 2024, 2063, 1053, 2054, 1004, 1043, 2044, 2121, 1033, 2034,
+    2131, 2141, 1014, 2151, 1081, 1024, 2073, 1091, 1102, 1054, 1112, 1063, 2064, 1044, 2171, 1034, 1073, 2074,
+    1064, 2221, 2092, 2082, 2113, 2103, 1161, 1121, 1074, 1131, 1141, 2132, 1151, 2122, 2152, 1113, 2114, 2142,
+    1103, 2104, 1092, 2093, 1082, 2162, 2191, 1171, 2181, 2083, 1114, 1132, 2172, 2133, 1104, 1122, 1152, 1093,
+    2094, 2123, 1142, 1221, 2201, 2143, 1083, 2084, 1162, 2163, 1133, 2134, 2153, 1094, 2231, 1172, 2211, 1123,
+    2124, 1084, 2173, 1143, 2144, 1163, 2164, 1134, 1191, 1181, 2182, 2192, 1153, 2154, 2222, 1124, 1173, 2174,
+    1144, 1201, 2202, 1164, 1154, 1211, 2212, 1231, 2232, 1182, 2183, 1174, 1192, 2193, 1222, 2223, 1202, 2203,
+    1212, 2213, 1183, 2184, 1193, 2194, 1223, 1232, 2233, 2224, 1203, 1213, 2204, 2214, 1184, 1233, 2234, 1194,
+    1224, 1204, 1214, 1234,
 )
 SMALL_ROWS = 1024
 SMALL_AXES = (CORE, NEAR_X, NEAR_Y, NEAR_Z, FAR_Z)
@@ -756,16 +790,25 @@
     return (owner + step - 2 * step * bits[axis], shard)
 
 
-def greet_partners(owner, shard, bits):
-    barrier = pltpu.get_barrier_semaphore()
-    for axis in range(5):
+def axis_partners(owner, shard, bits):
+    return [partner_of(axis, owner, shard, bits) for axis in range(5)]
+
+
+def group_partners(owner, shard):
+    same_owner = [(owner, (shard + i) % 4) for i in range(1, 4)]
+    same_shard = [((owner + i) % 8, shard) for i in range(1, 8)]
+    return same_owner, same_shard
+
+
+def greet(partners):
+    for partner in partners:
         pl.semaphore_signal(
-            barrier, inc=1, device_id=partner_of(axis, owner, shard, bits), device_id_type=MESH
+            pltpu.get_barrier_semaphore(), inc=1, device_id=partner, device_id_type=MESH
         )
 
 
-def await_partners():
-    pl.semaphore_wait(pltpu.get_barrier_semaphore(), 5)
+def await_greetings(count):
+    pl.semaphore_wait(pltpu.get_barrier_semaphore(), count)
 
 
 def total_of(values):
@@ -780,38 +823,38 @@
 
 
 def sum_kernel(
-    grads_ref, table_ref, norm_ref, count_ref, owned_ref, table_out, norm_out, stats_out,
-    inbuf, stage, r0, r1, r2, r3, r4, small, s0, s1, s2, s3, s4, spread, square, squares,
+    grads_ref, table_ref, norm_ref, count_ref,
+    owned_ref, table_out, norm_out, stats_out,
+    inbuf, r0, r1, r2, r3, r4, small, s0, s1, s2, s3, s4, spread, square, near_squares, far_squares,
     in_sem, send_sem, recv_sem, small_send, small_recv, square_send, square_recv,
 ):
     owner, shard, bits = own_bits()
-    edge = grads_ref.shape[3]
-    strip = PACK * edge
-    part = edge // QUARTERS
     received = (r0, r1, r2, r3, r4)
 
     def axes_of(c):
         return CHUNK_AXES[c % len(CHUNK_AXES)]
 
+    def half_of(ref, c, k, bit):
+        left = [axis for axis in NATURAL if axis not in axes_of(c)[:k]]
+        place = left.index(axes_of(c)[k])
+        return ref.at[(c,) + (slice(None),) * place + (bit,)]
+
     def fetch(c):
-        rows = pl.ds(c % QUARTERS * part, part)
         slot = c % SUM_SLOTS
         return pltpu.make_async_copy(
-            grads_ref.at[c // QUARTERS, :, :, rows], inbuf.at[slot], in_sem.at[slot]
+            grads_ref.at[c, :, :, :, :, bits[CORE]], inbuf.at[slot], in_sem.at[slot]
         )
 
-    for c in range(SUM_SLOTS):
-        fetch(c).start()
-    greet_partners(owner, shard, bits)
-    await_partners()
+    same_owner, same_shard = group_partners(owner, shard)
+    greet(same_owner + same_shard)
+    await_greetings(len(same_owner) + len(same_shard))
 
     def chunk_send(c, k):
         if k == 0:
-            axis, source = CORE, stage.at[c % SUM_SLOTS]
+            axis, source = CORE, grads_ref.at[c, :, :, :, :, 1 - bits[CORE]]
         else:
             axis = axes_of(c)[k - 1]
-            half = received[k - 1].shape[1] // 2
-            source = received[k - 1].at[c, pl.ds(half * (1 - bits[axis]), half)]
+            source = half_of(received[k - 1], c, k - 1, 1 - bits[axis])
         return pltpu.make_async_remote_copy(
             src_ref=source,
             dst_ref=received[k].at[c],
@@ -821,59 +864,24 @@
             device_id_type=MESH,
         )
 
-    def packed(c, e, core):
-        d = core
-        for k, axis in enumerate(axes_of(c)):
-            d = d + e // (8 >> k) % 2 * AXIS_STRIDE[axis]
-        blocks = [inbuf[c % SUM_SLOTS, d, j][:, :edge] for j in range(PACK)]
-        return jnp.concatenate(blocks, axis=1)
-
-    def pack(c):
-        fetch(c).wait()
-        if c >= SUM_SLOTS:
-            chunk_send(c - SUM_SLOTS, 0).wait_send()
-
-        def body(e, carry):
-            stage[c % SUM_SLOTS, e] = packed(c, e, 1 - bits[CORE])
-            return carry
-
-        lax.fori_loop(0, 16, body, 0, unroll=4)
-
     def merge(c, k):
         chunk_send(c, k).wait_recv()
         if k == 0:
-
-            def body(e, carry):
-                r0[c, e] = r0[c, e] + packed(c, e, bits[CORE])
-                return carry
-
-            lax.fori_loop(0, 16, body, 0, unroll=4)
-            if c + SUM_SLOTS < SUM_CHUNKS:
-                fetch(c + SUM_SLOTS).start()
+            fetch(c).wait()
+            r0[c] = r0[c] + inbuf[c % SUM_SLOTS]
             return
-        axis = axes_of(c)[k - 1]
-        half = received[k].shape[1]
-        base = half * bits[axis]
-
-        def body(e, carry):
-            received[k][c, e] = received[k][c, e] + received[k - 1][c, base + e]
-            return carry
-
+        own = half_of(received[k - 1], c, k - 1, bits[axes_of(c)[k - 1]])[...]
         if k < 4:
-            lax.fori_loop(0, half, body, 0, unroll=2)
+            received[k][c] = received[k][c] + own
             return
-        group = r4[c, 0] + r3[c, base]
-        pieces = unpack_group(group, edge)
-        rows = slice(c % QUARTERS * part, (c % QUARTERS + 1) * part)
-        for j in range(PACK):
-            owned_ref[PACK * (c // QUARTERS) + j, rows, :] = pieces[j]
-        parts = group * group
-        line = parts[:, :LANES]
-        for i in range(1, strip // LANES):
-            line = line + parts[:, i * LANES : (i + 1) * LANES]
+        dense = r4[c] + own
+        quarter = owned_ref.shape[1] // 4
+        for i, rows in enumerate(from_dense(dense)):
+            owned_ref[c, i * quarter : (i + 1) * quarter, :] = rows
+        parts = dense * dense
         total = square[...]
-        for r in range(part // 8):
-            total = total + line[r * 8 : (r + 1) * 8]
+        for r in range(dense.shape[0] // 8):
+            total = total + parts[r * 8 : (r + 1) * 8]
         square[...] = total
 
     vocab, width = table_ref.shape
@@ -945,37 +953,46 @@
     square[...] = jnp.zeros_like(square)
     small_fill()
     small_copy(0).start()
-    extra = [functools.partial(small_merge, k) for k in range(5)]
+    extra = []
+    extra += [functools.partial(small_merge, k) for k in range(5)]
     extra += [functools.partial(spread_next, k) for k in range(4, -1, -1)]
     for position, code in enumerate(SUM_ORDER):
         c, k = code % 1000 // 10, code % 10
         if code < 1000:
-            pack(c)
+            fetch(c).start()
         elif code < 2000:
             merge(c, k)
         else:
             chunk_send(c, k).start()
-        if position >= 60 and position % 12 == 0 and extra:
+        if position >= 70 and position % 16 == 0 and extra:
             extra.pop(0)()
     while extra:
         extra.pop(0)()
 
-    def square_copy(k):
-        return pltpu.make_async_remote_copy(
-            src_ref=squares.at[k],
-            dst_ref=squares.at[5 + k],
-            send_sem=square_send.at[k],
-            recv_sem=square_recv.at[k],
-            device_id=partner_of(SMALL_AXES[k], owner, shard, bits),
-            device_id_type=MESH,
-        )
-
-    value = square[...]
-    for k in range(5):
-        squares[k] = value
-        square_copy(k).start()
-        square_copy(k).wait_recv()
-        value = squares[k] + squares[5 + k]
+    def exchange(partners, mine, slots, first):
+        slots[mine] = square[...]
+        copies = [
+            pltpu.make_async_remote_copy(
+                src_ref=square,
+                dst_ref=slots.at[mine],
+                send_sem=square_send.at[first + i],
+                recv_sem=square_recv.at[first + i],
+                device_id=partner,
+                device_id_type=MESH,
+            )
+            for i, partner in enumerate(partners)
+        ]
+        for copy in copies:
+            copy.start()
+        for copy in copies:
+            copy.wait()
+        value = slots[0]
+        for i in range(1, slots.shape[0]):
+            value = value + slots[i]
+        return value
+
+    square[...] = exchange(same_owner, shard, near_squares, 0)
+    value = exchange(same_shard, owner, far_squares, 3)
     table_sum, vectors_sum = table_out[...], norm_out[0:6, :]
     stats_out[...] = statistics(
         total_of(value) + total_of(table_sum * table_sum) + total_of(vectors_sum * vectors_sum),
@@ -985,49 +1002,43 @@
 
     for c in range(SUM_CHUNKS):
         for k in range(5):
-            if k > 0 or c >= SUM_CHUNKS - SUM_SLOTS:
-                chunk_send(c, k).wait_send()
+            chunk_send(c, k).wait_send()
     for k in range(5):
         small_copy(k).wait_send()
         spread_copy(k).wait_send()
-        square_copy(k).wait_send()
 
 
 def sum_everywhere(grads, table_grad, norm_grad, count):
-    groups, devices, _, edge, _ = grads.shape
-    strip = PACK * edge
-    part = edge // QUARTERS
-    group = lambda count: pltpu.VMEM((SUM_CHUNKS, count, part, strip), F32)
+    chunks = grads.shape[0]
+    block = grads.shape[-2:]
+    edge = math.isqrt(block[0] * block[1])
+    group = lambda count: pltpu.VMEM((chunks,) + (2,) * count + block, F32)
     small = lambda rows: pltpu.VMEM((rows, LANES), F32)
+    anywhere, inside = pl.BlockSpec(memory_space=pl.ANY), pl.BlockSpec(memory_space=pltpu.VMEM)
     return pl.pallas_call(
         sum_kernel,
         out_shape=(
-            jax.ShapeDtypeStruct((groups * PACK, edge, edge), F32),
+            jax.ShapeDtypeStruct((chunks, edge, edge), F32),
             jax.ShapeDtypeStruct(table_grad.shape, F32),
             jax.ShapeDtypeStruct(norm_grad.shape, F32),
             jax.ShapeDtypeStruct((8, LANES), F32),
         ),
-        in_specs=[
-            pl.BlockSpec(memory_space=pl.ANY),
-            pl.BlockSpec(memory_space=pltpu.VMEM),
-            pl.BlockSpec(memory_space=pltpu.VMEM),
-            pl.BlockSpec(memory_space=pltpu.VMEM),
-        ],
-        out_specs=(pl.BlockSpec(memory_space=pltpu.VMEM),) * 4,
+        in_specs=[anywhere, inside, inside, inside],
+        out_specs=(inside,) * 4,
         scratch_shapes=[
-            pltpu.VMEM((SUM_SLOTS, devices, PACK, part, LANES), F32),
-            pltpu.VMEM((SUM_SLOTS, devices // 2, part, strip), F32),
-            group(16), group(8), group(4), group(2), group(1),
+            pltpu.VMEM((SUM_SLOTS,) + (2,) * 4 + block, F32),
+            group(4), group(3), group(2), group(1), group(0),
             small(SMALL_ROWS), small(512), small(256), small(128), small(64), small(32), small(SMALL_ROWS),
             pltpu.VMEM((8, LANES), F32),
-            pltpu.VMEM((10, 8, LANES), F32),
+            pltpu.VMEM((4, 8, LANES), F32),
+            pltpu.VMEM((8, 8, LANES), F32),
             pltpu.SemaphoreType.DMA((SUM_SLOTS,)),
             pltpu.SemaphoreType.DMA((SUM_CHUNKS, 5)),
             pltpu.SemaphoreType.DMA((SUM_CHUNKS, 5)),
             pltpu.SemaphoreType.DMA((10,)),
             pltpu.SemaphoreType.DMA((10,)),
-            pltpu.SemaphoreType.DMA((5,)),
-            pltpu.SemaphoreType.DMA((5,)),
+            pltpu.SemaphoreType.DMA((10,)),
+            pltpu.SemaphoreType.DMA((10,)),
         ],
         compiler_params=pltpu.CompilerParams(
             vmem_limit_bytes=66_000_000, collective_id=1, has_side_effects=True
@@ -1110,13 +1121,13 @@
             device_id_type=MESH,
         )
 
-    greet_partners(owner, shard, bits)
+    greet(axis_partners(owner, shard, bits))
     for g in range(PACK_GROUPS):
         blocks = [own_ref[g * PACK + b].astype(BF16) for b in range(PACK)]
         packed[g] = jnp.concatenate(blocks, axis=1)
     total = jnp.broadcast_to(jnp.sum(mask_ref[...].astype(F32), keepdims=True), count_ref.shape)
     counts[0] = total
-    await_partners()
+    await_greetings(5)
     for c in range(GATHER_CHUNKS):
         keep(c).start()
 
@@ -1210,16 +1221,22 @@
     )(place, own, mask)
 
 
-def dot_top(left, right, dims):
-    return lax.dot_general(
-        left, right, (dims, ((), ())), precision=TOP_PRECISION, preferred_element_type=F32
-    )
+def split_two(values):
+    high = values.astype(BF16)
+    return high, (values - high.astype(F32)).astype(BF16)
+
+
+def dot_split(left, right, dims):
+    product = lambda a, b: lax.dot_general(a, b, (dims, ((), ())), preferred_element_type=F32)
+    return product(left[0], right[0]) + (product(left[0], right[1]) + product(left[1], right[0]))
 
 
 def shampoo_parts(grad, left, right, left_root, right_root, weight):
-    new_left = STAT_DECAY * left + (1.0 - STAT_DECAY) * dot_top(grad, grad, ((1,), (1,)))
-    new_right = STAT_DECAY * right + (1.0 - STAT_DECAY) * dot_top(grad, grad, ((0,), (0,)))
-    precond = dot_top(dot_top(left_root, grad, ((1,), (0,))), right_root, ((1,), (0,)))
+    parts = split_two(grad)
+    new_left = STAT_DECAY * left + (1.0 - STAT_DECAY) * dot_split(parts, parts, ((1,), (1,)))
+    new_right = STAT_DECAY * right + (1.0 - STAT_DECAY) * dot_split(parts, parts, ((0,), (0,)))
+    half = dot_split(split_two(left_root), parts, ((1,), (0,)))
+    precond = dot_split(split_two(half), split_two(right_root), ((1,), (0,)))
     scale = 1.0 / (grad.shape[0] * grad.shape[1])
     mean = jnp.sum(jnp.sum(precond * precond, 1, keepdims=True), 0, keepdims=True) * scale
     scale_back = lax.rsqrt(mean + ROOT_EPSILON)
@@ -1260,12 +1277,33 @@
     step_ref, stats_ref, grad_ref, left_ref, right_ref, left_root_ref, right_root_ref, weight_ref,
     norm_grad_ref, moment_ref, second_ref, norm_ref,
     grad_out, left_out, right_out, weight_out, norm_grad_out, moment_out, second_out, norm_out,
+    grad_parts, precond,
 ):
     factor = stats_ref[0:1, 0:1]
     grad = grad_ref[...] * factor
     grad_out[...] = grad
-    left_out[...], right_out[...], weight_out[...] = shampoo_parts(
-        grad, left_ref[...], right_ref[...], left_root_ref[...], right_root_ref[...], weight_ref[...]
+    parts = split_two(grad)
+    left_out[...] = STAT_DECAY * left_ref[...] + (1.0 - STAT_DECAY) * dot_split(parts, parts, ((1,), (1,)))
+    half = split_two(dot_split(split_two(left_root_ref[...]), parts, ((1,), (0,))))
+    for n in range(2):
+        grad_parts[n] = parts[n]
+    width = grad.shape[1]
+    strip = width // 3
+
+    def strip_body(i, carry):
+        cols = pl.ds(pl.multiple_of(i * strip, strip), strip)
+        own = (grad_parts[0, :, cols], grad_parts[1, :, cols])
+        right_out[cols, :] = STAT_DECAY * right_ref[cols, :] + (1.0 - STAT_DECAY) * dot_split(
+            own, parts, ((0,), (0,))
+        )
+        precond[:, cols] = dot_split(half, split_two(right_root_ref[:, cols]), ((1,), (0,)))
+        return carry
+
+    lax.fori_loop(0, 3, strip_body, 0)
+    turned = precond[...]
+    mean = total_of(turned * turned) * (1.0 / (grad.shape[0] * width))
+    weight_out[...] = weight_ref[...] * (1.0 - MATRIX_RATE * WEIGHT_DECAY) - MATRIX_RATE * turned * lax.rsqrt(
+        mean + ROOT_EPSILON
     )
     rows = norm_ref.shape[0]
     clipped = norm_grad_ref[0:rows, :] * factor
@@ -1285,6 +1323,7 @@
     return pl.pallas_call(
         table_update_kernel,
         out_shape=(like(grad), like(left), like(right), like(weight)) + (like(norms),) * 4,
+        scratch_shapes=[pltpu.VMEM((2,) + grad.shape, BF16), pltpu.VMEM(grad.shape, F32)],
         compiler_params=params(),
         name="update_table",
     )(corrections, stats, grad, left, right, left_root, right_root, weight, norm_grad, moment, second, norms)
@@ -1369,25 +1408,26 @@
     before = jnp.sum((segment[None, :] < tiled[:, :1]).astype(jnp.int32), -1)
     until = jnp.sum((segment[None, :] <= tiled[:, -1:]).astype(jnp.int32), -1)
     low, high = before // TILE, (until + TILE - 1) // TILE
+    half = (high - low + 1) // 2
+    low = jnp.minimum(low, tiles - 2 * half)
     cosine, sine = rotary_tables(length)
 
     x0, h1, query, keys, values = front(columns, embedding_weight, norm_params, project, cosine, sine)
-    attended, lse = attend(low, high, query, keys, values, columns, seg_row)
+    attended, lse = attend(low, half, query, keys, values, columns, seg_row)
     (h2, active, d_two, ghid, d_one, gatt, gx, head_grad, norm_grad) = middle_rows(
         x0, attended, columns, count, norm_params, embedding_weight,
         outward, expand, contract,
     )
     gproj = attend_back(
-        low, high, query, keys, values, gatt, lse, columns, seg_row, cosine, sine
+        low, half, query, keys, values, gatt, lse, columns, seg_row, cosine, sine
     )
     table_grad, norm_grad = tail_rows(
         columns, x0, gx, gproj, norm_params, project, head_grad, norm_grad
     )
-
     owner, slot = owner_map[None, :] // slots, owner_map[None, :] % slots
     device = owner * shards + jnp.arange(shards, dtype=jnp.int32)[:, None]
     if known:
-        home = (slot // PACK * (owners * shards) + device) * PACK + slot % PACK
+        home = slot * (owners * shards) + device
     else:
         home = device * slots + slot
     grads = weight_grads(
@@ -1395,10 +1435,12 @@
     )
     if known:
         owned, table_grad, norm_grad, stats = sum_everywhere(
-            grads.reshape(slots // PACK, owners * shards, PACK, edge, LANES), table_grad, norm_grad, count
+            grads.reshape((slots,) + (2,) * 5 + grads.shape[1:]),
+            table_grad, norm_grad, count,
         )
     else:
-        owned = lax.psum_scatter(grads[:, :, :edge], everyone, scatter_dimension=0, tiled=True)
+        owned = lax.psum_scatter(grads, everyone, scatter_dimension=0, tiled=True)
+        owned = jnp.stack([jnp.concatenate(from_dense(owned[b]), 0) for b in range(slots)])
         table_grad, norm_grad, square_sum = lax.psum((table_grad, norm_grad), everyone) + (
             lax.psum(jnp.sum(owned * owned), everyone),
         )

time: 453 us -> 426 us (0.940); the launches traced: 444 us -> 425 us
  Pallas kernels: 430 us -> 411 us
    pallas_call x1, Pallas kernels: 162 us -> 133 us  [sum_everywhere(): pl.pallas_call(sum_kernel, out_shape=(jax.ShapeDtypeStruct((chunks, edge,...]
    pallas_call x1, Pallas kernels: 36.8 us -> 44.6 us  [attend_back(): pl.pallas_call(attend_back_kernel, out_shape=jax.ShapeDtypeStruct((3, len...]
where the time goes in v2:
time: 426 us; the launch traced here: 425 us
  Pallas kernels  411 us (96%)
  other arithmetic  7.08 us (2%)
  local copies, waits for them, and re-layouts  5.92 us (1%)
    pallas_call x1, Pallas kernels, sum_everywhere(): pl.pallas_call(sum_kernel, out_shape=(jax.ShapeDtypeStruct((chunks, edge,...  133 us
    pallas_call x1, Pallas kernels, gather_everywhere(): pl.pallas_call(functools.partial(gather_kernel, sizes=sizes), out_shape=s...  80.1 us
    pallas_call x1, Pallas kernels, middle_rows(): pl.pallas_call(middle_kernel, out_shape=(low, low_broad, low, low_broad,...  47.9 us
    pallas_call x1, Pallas kernels, attend_back(): pl.pallas_call(attend_back_kernel, out_shape=jax.ShapeDtypeStruct((3, len...  44.6 us
    pallas_call x1, Pallas kernels, attend(): pl.pallas_call(attend_kernel, out_shape=(jax.ShapeDtypeStruct((length, wi...  33.1 us
    pallas_call x1, Pallas kernels, weight_grads(): pl.pallas_call(functools.partial(weight_grad_kernel, sizes=sizes, edge=ed...  32 us
    pallas_call x1, Pallas kernels, tail_rows(): pl.pallas_call(tail_kernel, out_shape=(jax.ShapeDtypeStruct(head.shape, F...  12.1 us
    pallas_call x1, Pallas kernels, front(): pl.pallas_call(front_kernel, out_shape=(jax.ShapeDtypeStruct((length, wid...  11.5 us

profile of v2, /device:TPU:0, one launch (start us, length us, event | category | flops | bytes accessed | tf_op | source)
XLA Modules:
  0.0 425.3 jit_solution(15090211391140340801)
XLA Ops:
  0.6 0.7 broadcast_multiply_fusion.3
  1.4 0.7 broadcast_compare_fusion.4
  2.1 0.1 fusion.5
  2.2 0.1 add.395
  2.3 0.1 add.404
  2.3 0.1 add.412
  2.4 0.1 reshape.316
  2.5 0.1 add.383
  2.6 0.1 add.426
  2.7 0.1 broadcast_in_dim.71
  2.8 0.1 broadcast_in_dim.73
  2.9 0.1 broadcast_in_dim.75
  3.0 0.1 broadcast_in_dim.77
  3.1 0.6 multiply_add_fusion.place_ref
  3.7 80.1 %gather_weights.1 = (bf16[768,2304]{1,0:T(8,128)(2,1)}, bf16[768,768]{1,0:T(8,128)(2,1)}, bf16[768,3072]{1,0:T(8,128)(2,1)}, bf16[3072,768]{1,0:T(8,128)(2,1)}, f32[8,128]{1,0:T(8,128)}) custom-call(s32[768]{0:T(1024)} %multiply_add_fusion.place_ref, f32[24,96,96]{2,1,0:T(8,128)} %bitcast.23, s32[1,1024]{1,0:T(1,128)} %mask_ref.1), custom_call_target="tpu_custom_call" | custom-call | tf_op jit(solution)/shard_map/gather_weights/pallas_call | solution.py:1197
  83.8 0.5 broadcast.422
  84.3 1.4 fusion.12
  85.7 0.0 copy-start
  85.7 0.7 pad_add_fusion
  86.4 1.0 copy.46.column_ref
  87.5 2.8 negate_select_fusion
  90.3 11.5 %embed_project.1 = (f32[1024,768]{1,0:T(8,128)}, bf16[1024,768]{1,0:T(8,128)(2,1)}, bf16[1024,768]{1,0:T(8,128)(2,1)}, bf16[1024,768]{1,0:T(8,128)(2,1)}, bf16[1024,768]{1,0:T(8,128)(2,1)}) custom-call(s32[1024,4]{1,0:T(8,128)} %copy.46.column_ref, f32[128,768]{1,0:T(8,128)} %weight_ref.1, f32[6,768]{1,0:T(8,128)} %norm_ref.7, ...), custom_call_target="tpu_custom_call" | custom-call | tf_op jit(solution)/shard_map/embed_project/pallas_call | solution.py:267
  101.9 0.2 slice_reduce_fusion
  102.1 0.0 copy-done
  102.1 0.2 convert_reduce_fusion
  102.3 0.5 subtract_minimum_fusion
  102.8 33.1 %attend_forward.1 = (bf16[1024,768]{1,0:T(8,128)(2,1)}, f32[1024,768]{1,0:T(8,128)}) custom-call(s32[4]{0:T(128)} %get-tuple-element.96.low_ref, s32[4]{0:T(128)} %get-tuple-element.97.half_ref, bf16[1024,768]{1,0:T(8,128)(2,1)} %get-tuple-element.55.q_ref, bf16[1024,768]{1,0:T(8,128)(2,1)} %get-tuple-element.56.k_ref, ...), custom_call_target="tpu_custom_call" | custom-call | tf_op jit(solution)/shard_map/attend_forward/pallas_call | solution.py:333
  135.9 47.9 %middle_rows.1 = (bf16[1024,768]{1,0:T(8,128)(2,1)}, bf16[1024,3072]{1,0:T(8,128)(2,1)}, bf16[1024,768]{1,0:T(8,128)(2,1)}, bf16[1024,3072]{1,0:T(8,128)(2,1)}, ...) custom-call(f32[1024,768]{1,0:T(8,128)} %get-tuple-element.59.x_ref,, ...), custom_call_target="tpu_custom_call" | custom-call | tf_op jit(solution)/shard_map/middle_rows/pallas_call | solution.py:536
  183.9 44.6 %attend_backward.1.gproj.gproj_ref = bf16[3,1024,768]{2,1,0:T(8,128)(2,1)} custom-call(s32[4]{0:T(128)} %get-tuple-element.96.low_ref, s32[4]{0:T(128)} %get-tuple-element.97.half_ref, bf16[1024,768]{1,0:T(8,128)(2,1)} %get-tuple-element.55.q_ref, bf16[1024,768]{1,0:T(8,128)(2,1)} %get-tuple-element.56.k_ref, bf16[1024,768]{1,0:T(8,128)(2,1)} %get-tuple-element.57.v_ref, ...), custom_call_target="tpu_custom_call" | custom-call | tf_op jit(solution)/shard_map/attend_backward/pallas_call | solution.py:421
  228.4 12.1 %tail_rows.1 = (f32[128,768]{1,0:T(8,128)}, f32[8,768]{1,0:T(8,128)}) custom-call(s32[1024,4]{1,0:T(8,128)} %copy.46.column_ref, f32[1024,768]{1,0:T(8,128)} %get-tuple-element.59.x_ref, f32[1024,768]{1,0:T(8,128)} %get-tuple-element.71.gx_ref, bf16[3,1024,768]{2,1,0:T(8,128)(2,1)} %attend_backward.1.gproj.gproj_ref, f32[6,768]{1,0:T(8,128)} %norm_ref.7, ...), custom_call_target="tpu_custom_call" | custom-call | tf_op jit(solution)/shard_map/tail_rows/pallas_call | solution.py:595
  240.6 0.7 add.380.place_ref
  241.3 32.0 %weight_gradients.1 = f32[768,72,128]{2,1,0:T(8,128)} custom-call(s32[768]{0:T(1024)} %add.380.place_ref, bf16[1024,768]{1,0:T(8,128)(2,1)} %get-tuple-element.54.h_one, bf16[1024,768]{1,0:T(8,128)(2,1)} %get-tuple-element.58.att_ref.att, bf16[1024,768]{1,0:T(8,128)(2,1)} %get-tuple-element.64.h_two, bf16[1024,3072]{1,0:T(8,128)(2,1)} %get-tuple-element.65.active, ...), custom_call_target="tpu_custom_call" | custom-call | tf_op jit(solution)/shard_map/weight_gradients/pallas_call | solution.py:706
  273.3 132.8 %sum_gradients.1 = (f32[24,96,96]{2,1,0:T(8,128)}, f32[128,768]{1,0:T(8,128)}, f32[8,768]{1,0:T(8,128)}, f32[8,128]{1,0:T(8,128)}) custom-call(f32[24,2,2,2,2,2,72,128]{7,6,5,4,3,2,1,0:T(8,128)} %bitcast.22, f32[128,768]{1,0:T(8,128)} %get-tuple-element.74.table_ref, f32[8,768]{1,0:T(8,128)} %get-tuple-element.75.norm_ref, f32[8,128]{1,0:T(8,128)} %get-tuple-element.60.count_ref), custom_call_target="tpu_custom_call" | custom-call | tf_op jit(solution)/shard_map/sum_gradients/pallas_call | solution.py:1018
  406.8 0.6 maximum_bitcast_fusion.step_ref
  407.4 6.8 %update_table.1 = (f32[128,768]{1,0:T(8,128)}, f32[128,128]{1,0:T(8,128)}, f32[768,768]{1,0:T(8,128)}, f32[128,768]{1,0:T(8,128)}, f32[6,768]{1,0:T(8,128)}, /*i...) custom-call(f32[1,2]{1,0:T(1,128)} %maximum_bitcast_fusion.step_ref, f32[8,128]{1,0:T(8,128)} %get-tuple-element.76.stats_ref, ...), custom_call_target="tpu_custom_call" | custom-call | tf_op jit(solution)/shard_map/update_table/pallas_call | solution.py:1323
  414.2 9.8 %update_blocks.1 = (f32[24,96,96]{2,1,0:T(8,128)}, f32[24,96,96]{2,1,0:T(8,128)}, f32[24,96,96]{2,1,0:T(8,128)}, f32[24,96,96]{2,1,0:T(8,128)}) custom-call(f32[8,128]{1,0:T(8,128)} %get-tuple-element.76.stats_ref, f32[24,96,96]{2,1,0:T(8,128)} %get-tuple-element.77.grad_ref, f32[24,96,96]{2,1,0:T(8,128)} %bitcast.25, f32[24,96,96]{2,1,0:T(8,128)} %bitcast.26, ...), custom_call_target="tpu_custom_call" | custom-call | tf_op jit(solution)/shard_map/update_blocks/pallas_call | solution.py:1265
  424.0 1.3 fusion.13
  (16 shorter events, 0.1 us)
Async XLA Ops:
  85.7 16.4 %copy-start = (s32[1,1024]{1,0:T(1,128)}, s32[1,1024]{1,0:T(1,128)S(1)}, u32[]{:S(2)}) copy-start(s32[1,1024]{1,0:T(1,128)S(1)} %get-tuple-element.99) | copy-start | bytes 12292

commit v3 on v2

--- a/solution.py
+++ b/solution.py
@@ -282,8 +282,9 @@
     )(columns, table, norm_params, project, cosine, sine)
 
 
-ROWS = 256
+ROWS = 512
 TILE = 128
+SHORTEST = 3
 
 
 def head_masks(rows):
@@ -320,7 +321,7 @@
         o_ref[...] = jnp.where(masks[0], outs[0], outs[1]).astype(BF16)
         lse_ref[...] = jnp.where(masks[0], logs[0], logs[1])
 
-    for n in range(1, k_ref.shape[0] // TILE // 2 + 1):
+    for n in range(SHORTEST, k_ref.shape[0] // TILE // 2 + 1):
         pl.when(half == n)(functools.partial(run, 2 * n))
 
 
@@ -376,8 +377,8 @@
         keys = k_ref[span, :]
         values = v_ref[span, :]
         same = same_segment(column_ref[:, 3:4], seg_row_ref, first, count)
-        dq = []
-        dk = dv = None
+        dq, dk, dv = [], [], []
+        query_turned, grad_turned = query.T, grad.T
         for h, mask in enumerate(masks):
             own_query = jnp.where(mask, query, zero)
             own_grad = jnp.where(mask, grad, zero)
@@ -387,10 +388,10 @@
             delta = jnp.sum(probs * grad_probs, -1, keepdims=True)
             grad_scores = (probs * (grad_probs - delta)).astype(BF16)
             dq.append(dot(grad_scores, keys))
-            more_dk = dot(own_query.T, grad_scores)
-            more_dv = dot(own_grad.T, probs.astype(BF16))
-            dk = more_dk if dk is None else dk + more_dk
-            dv = more_dv if dv is None else dv + more_dv
+            rows = slice(h * HS, (h + 1) * HS)
+            dk.append(dot(query_turned[rows], grad_scores))
+            dv.append(dot(grad_turned[rows], probs.astype(BF16)))
+        dk, dv = jnp.concatenate(dk, axis=0), jnp.concatenate(dv, axis=0)
         for i in range(count):
             lanes = slice(i * TILE, (i + 1) * TILE)
             dk_acc[first + i] += dk[:, lanes]
@@ -401,7 +402,7 @@
         )
         out_ref[0, rows, :] = turned.astype(BF16)
 
-    for n in range(1, k_ref.shape[0] // TILE // 2 + 1):
+    for n in range(SHORTEST, k_ref.shape[0] // TILE // 2 + 1):
         pl.when(half == n)(functools.partial(run, 2 * n))
 
     @pl.when(part == parts - 1)
@@ -868,13 +869,25 @@
         chunk_send(c, k).wait_recv()
         if k == 0:
             fetch(c).wait()
-            r0[c] = r0[c] + inbuf[c % SUM_SLOTS]
+
+            def add(e, carry):
+                for y in range(2):
+                    place = (e // 4, e // 2 % 2, e % 2, y)
+                    r0[(c,) + place] = r0[(c,) + place] + inbuf[(c % SUM_SLOTS,) + place]
+                return carry
+
+            lax.fori_loop(0, 8, add, 0)
             return
-        own = half_of(received[k - 1], c, k - 1, bits[axes_of(c)[k - 1]])[...]
+        own = half_of(received[k - 1], c, k - 1, bits[axes_of(c)[k - 1]])
         if k < 4:
-            received[k][c] = received[k][c] + own
+
+            def add(e, carry):
+                received[k][c, e] = received[k][c, e] + own[e]
+                return carry
+
+            lax.fori_loop(0, 2, add, 0)
             return
-        dense = r4[c] + own
+        dense = r4[c] + own[...]
         quarter = owned_ref.shape[1] // 4
         for i, rows in enumerate(from_dense(dense)):
             owned_ref[c, i * quarter : (i + 1) * quarter, :] = rows
@@ -1074,7 +1087,9 @@
 
 
 def gather_kernel(
-    place_ref, own_ref, mask_ref, project_out, outward_out, expand_out, contract_out, count_ref,
+    place_ref, own_ref, codon_ref, target_ref, mask_ref, segments_ref,
+    project_out, outward_out, expand_out, contract_out,
+    count_ref, column_ref, seg_row_ref, cos_ref, sin_ref, low_ref, half_ref,
     packed, held, store, project, outward, expand, contract, counts,
     own_sem, send_sem, recv_sem, count_send, count_recv, out_sem, *, sizes,
 ):
@@ -1141,6 +1156,29 @@
 
         lax.fori_loop(0, devices, body, 0, unroll=2)
 
+    def describe_rows():
+        length = codon_ref.shape[1]
+        segment = segments_ref[pl.ds(shard, 1), :]
+        stacked = jnp.concatenate([codon_ref[...], target_ref[...], mask_ref[...], segment], axis=0)
+        filler = jnp.zeros((LANES - stacked.shape[0], LANES), jnp.int32)
+        for i in range(length // LANES):
+            lanes = slice(i * LANES, (i + 1) * LANES)
+            column_ref[lanes, :] = jnp.concatenate([stacked[:, lanes], filler], axis=0).T
+            seg_row_ref[i] = segment[:, lanes]
+        for i in range(length // ROWS):
+            first = segment[:, i * ROWS : i * ROWS + 1]
+            final = segment[:, (i + 1) * ROWS - 1 : (i + 1) * ROWS]
+            before = jnp.sum(jnp.where(segment < first, 1.0, 0.0)).astype(jnp.int32)
+            until = jnp.sum(jnp.where(segment <= final, 1.0, 0.0)).astype(jnp.int32)
+            low_ref[i], half_ref[i] = span_of(before, until, length // TILE)
+
+    def rotary_rows(i, carry):
+        rows = pl.ds(pl.multiple_of(i * LANES, LANES), LANES)
+        place = lax.broadcasted_iota(jnp.int32, (LANES, LANES), 0) + i * LANES
+        lane = lax.broadcasted_iota(jnp.int32, (LANES, LANES), 1)
+        cos_ref[rows, :], sin_ref[rows, :] = rotary_of(place, lane)
+        return carry
+
     stage = 0
     for position, code in enumerate(GATHER_ORDER):
         c, k = code % 1000 // 10, code % 10
@@ -1152,6 +1190,10 @@
             move(c, k).wait_recv()
             if k == 4:
                 unpack(c)
+        if position == 10:
+            describe_rows()
+        if position == 30:
+            lax.fori_loop(0, cos_ref.shape[0] // LANES, rotary_rows, 0)
         if position == 0:
             count_copy(0).start()
         elif position % 12 == 0 and stage < 5:
@@ -1189,20 +1231,27 @@
         pltpu.make_async_copy(inside, outside, out_sem.at[n]).wait()
 
 
-def gather_everywhere(place, own, mask, devices, sizes):
+def gather_everywhere(place, own, codons, targets, mask, segments, devices, sizes):
     slots, edge, _ = own.shape
     width, _, _, hidden_width = sizes
     strip = PACK * edge
     shapes = matrix_shapes(width, hidden_width)
+    length = codons.shape[1]
+    inside, scalars = pl.BlockSpec(memory_space=pltpu.VMEM), pl.BlockSpec(memory_space=pltpu.SMEM)
     return pl.pallas_call(
         functools.partial(gather_kernel, sizes=sizes),
-        out_shape=shapes + (jax.ShapeDtypeStruct((8, LANES), F32),),
-        in_specs=[
-            pl.BlockSpec(memory_space=pltpu.SMEM),
-            pl.BlockSpec(memory_space=pltpu.VMEM),
-            pl.BlockSpec(memory_space=pltpu.VMEM),
-        ],
-        out_specs=(pl.BlockSpec(memory_space=pl.ANY),) * 4 + (pl.BlockSpec(memory_space=pltpu.VMEM),),
+        out_shape=shapes
+        + (
+            jax.ShapeDtypeStruct((8, LANES), F32),
+            jax.ShapeDtypeStruct((length, LANES), jnp.int32),
+            jax.ShapeDtypeStruct((length // TILE, 1, TILE), jnp.int32),
+            jax.ShapeDtypeStruct((length, LANES), F32),
+            jax.ShapeDtypeStruct((length, LANES), F32),
+            jax.ShapeDtypeStruct((length // ROWS,), jnp.int32),
+            jax.ShapeDtypeStruct((length // ROWS,), jnp.int32),
+        ),
+        in_specs=[scalars] + [inside] * 5,
+        out_specs=(pl.BlockSpec(memory_space=pl.ANY),) * 4 + (inside,) * 5 + (scalars,) * 2,
         scratch_shapes=[
             pltpu.VMEM((PACK_GROUPS, edge, strip), BF16),
             pltpu.VMEM((GATHER_CHUNKS, devices, edge // HALVES, strip), BF16),
@@ -1218,7 +1267,7 @@
         ],
         compiler_params=params(collective_id=2, has_side_effects=True),
         name="gather_weights",
-    )(place, own, mask)
+    )(place, own, codons, targets, mask, segments)
 
 
 def split_two(values):
@@ -1329,13 +1378,18 @@
     )(corrections, stats, grad, left, right, left_root, right_root, weight, norm_grad, moment, second, norms)
 
 
-def rotary_tables(length):
-    lane = jnp.arange(LANES, dtype=jnp.int32)[None, :]
+def rotary_of(place, lane):
     half = HS // 2
     freqs = jnp.exp(-math.log(ROTARY_BASE) * (2.0 * (lane % half).astype(F32) / HS))
-    angles = jnp.arange(length, dtype=F32)[:, None] * freqs
+    angles = place.astype(F32) * freqs
     sine = jnp.sin(angles)
     return jnp.cos(angles), jnp.where(lane % HS < half, -sine, sine)
+
+
+def span_of(before, until, tiles):
+    low, high = before // TILE, (until + TILE - 1) // TILE
+    half = jnp.maximum((high - low + 1) // 2, SHORTEST)
+    return jnp.minimum(low, tiles - 2 * half), half
 
 
 def pack_blocks(blocks):
@@ -1344,7 +1398,7 @@
     return groups.reshape(count // PACK, edge, PACK * edge)
 
 
-def gather_weights(own, mask, owner_map, known, sizes):
+def gather_weights(own, codons, targets, mask, segments, owner_map, known, sizes):
     everyone = ("dp", "tensor")
     slots, edge, _ = own.shape
     shards = sizes[1]
@@ -1357,11 +1411,24 @@
         for g in range(1, PACK_GROUPS):
             entry = jnp.where(group == g, gather_entry(g, bits), entry)
         place = ((group * 32 + entry) * PACK + slot % PACK).reshape(-1)
-        return gather_everywhere(place, own, mask, 32, sizes)
+        return gather_everywhere(place, own, codons, targets, mask, segments, 32, sizes)
     packed = pack_blocks(lax.all_gather(own.astype(BF16), everyone, axis=0, tiled=True))
     count = jnp.maximum(lax.psum(jnp.sum(mask.astype(F32)), everyone), 1.0)
     place = ((owner * shards + shard) * slots + slot).reshape(-1)
-    return assemble(place, packed, sizes) + (jnp.broadcast_to(count, (8, LANES)),)
+    length = codons.shape[1]
+    tiles = length // TILE
+    segment = lax.dynamic_index_in_dim(segments, lax.axis_index("tensor"), 0, keepdims=False)
+    columns = jnp.stack([codons[0], targets[0], mask[0], segment], 1)
+    tiled = segment.reshape(length // ROWS, ROWS)
+    before = jnp.sum((segment[None, :] < tiled[:, :1]).astype(jnp.int32), -1)
+    until = jnp.sum((segment[None, :] <= tiled[:, -1:]).astype(jnp.int32), -1)
+    spans = span_of(before, until, tiles)
+    cosine, sine = rotary_of(
+        jnp.arange(length, dtype=jnp.int32)[:, None], jnp.arange(LANES, dtype=jnp.int32)[None, :]
+    )
+    return assemble(place, packed, sizes) + (
+        jnp.broadcast_to(count, (8, LANES)), columns, segment.reshape(tiles, 1, TILE), cosine, sine,
+    ) + spans
 
 
 def body(
@@ -1392,34 +1459,22 @@
     slots = block_weight.shape[1]
     edge = block_weight.shape[-1]
     blocks = owner_map.shape[0]
-    length = codons.shape[1]
     shard_width = width // shards
 
     known = on_known_slice(owners, shards, slots)
     sizes = (width, shards, shard_width, FF)
-    project, outward, expand, contract, count = gather_weights(
-        block_weight[0], loss_mask, owner_map, known, sizes
+    project, outward, expand, contract, count, columns, seg_row, cosine, sine, *spans = gather_weights(
+        block_weight[0], codons, targets, loss_mask, segments, owner_map, known, sizes
     )
-    segment = lax.dynamic_index_in_dim(segments, lax.axis_index("tensor"), 0, keepdims=False)
-    tiles = length // TILE
-    columns = jnp.stack([codons[0], targets[0], loss_mask[0], segment], 1)
-    seg_row = segment.reshape(tiles, 1, TILE)
-    tiled = segment.reshape(length // ROWS, ROWS)
-    before = jnp.sum((segment[None, :] < tiled[:, :1]).astype(jnp.int32), -1)
-    until = jnp.sum((segment[None, :] <= tiled[:, -1:]).astype(jnp.int32), -1)
-    low, high = before // TILE, (until + TILE - 1) // TILE
-    half = (high - low + 1) // 2
-    low = jnp.minimum(low, tiles - 2 * half)
-    cosine, sine = rotary_tables(length)
 
     x0, h1, query, keys, values = front(columns, embedding_weight, norm_params, project, cosine, sine)
-    attended, lse = attend(low, half, query, keys, values, columns, seg_row)
+    attended, lse = attend(*spans, query, keys, values, columns, seg_row)
     (h2, active, d_two, ghid, d_one, gatt, gx, head_grad, norm_grad) = middle_rows(
         x0, attended, columns, count, norm_params, embedding_weight,
         outward, expand, contract,
     )
     gproj = attend_back(
-        low, half, query, keys, values, gatt, lse, columns, seg_row, cosine, sine
+        *spans, query, keys, values, gatt, lse, columns, seg_row, cosine, sine
     )
     table_grad, norm_grad = tail_rows(
         columns, x0, gx, gproj, norm_params, project, head_grad, norm_grad

time: 426 us -> 412 us (0.967)
  Pallas kernels: 411 us -> 404 us
  other arithmetic: 7.08 us -> 2.73 us
where the time goes in v3:
time: 412 us; the launch traced here: 411 us
  Pallas kernels  404 us (98%)
    pallas_call x1, Pallas kernels, sum_everywhere(): pl.pallas_call(sum_kernel, out_shape=(jax.ShapeDtypeStruct((chunks, edge,...  131 us
    pallas_call x1, Pallas kernels, gather_everywhere(): pl.pallas_call(functools.partial(gather_kernel, sizes=sizes), out_shape=s...  81.4 us
    pallas_call x1, Pallas kernels, middle_rows(): pl.pallas_call(middle_kernel, out_shape=(low, low_broad, low, low_broad,...  47.9 us
    pallas_call x1, Pallas kernels, attend_back(): pl.pallas_call(attend_back_kernel, out_shape=jax.ShapeDtypeStruct((3, len...  42.2 us
    pallas_call x1, Pallas kernels, weight_grads(): pl.pallas_call(functools.partial(weight_grad_kernel, sizes=sizes, edge=ed...  32 us
    pallas_call x1, Pallas kernels, attend(): pl.pallas_call(attend_kernel, out_shape=(jax.ShapeDtypeStruct((length, wi...  29.8 us
    pallas_call x1, Pallas kernels, tail_rows(): pl.pallas_call(tail_kernel, out_shape=(jax.ShapeDtypeStruct(head.shape, F...  12.1 us
    pallas_call x1, Pallas kernels, front(): pl.pallas_call(front_kernel, out_shape=(jax.ShapeDtypeStruct((length, wid...  11.5 us

profile of v3, /device:TPU:0, one launch (start us, length us, event | category | flops | bytes accessed | tf_op | source)
XLA Modules:
  0.0 411.4 jit_solution(9290510300752440095)
XLA Ops:
  0.6 0.7 broadcast_multiply_fusion.3
  1.4 0.7 broadcast_compare_fusion.4
  2.1 0.1 fusion.4
  2.2 0.1 add.352
  2.3 0.1 add.361
  2.3 0.1 add.369
  2.4 0.1 reshape.266
  2.5 0.1 add.340
  2.6 0.1 add.383
  2.7 0.1 broadcast_in_dim.57
  2.8 0.1 broadcast_in_dim.59
  2.9 0.1 broadcast_in_dim.61
  3.0 0.1 broadcast_in_dim.63
  3.1 0.6 multiply_add_fusion.place_ref
  3.7 81.4 %gather_weights.1 = (bf16[768,2304]{1,0:T(8,128)(2,1)}, bf16[768,768]{1,0:T(8,128)(2,1)}, bf16[768,3072]{1,0:T(8,128)(2,1)}, bf16[3072,768]{1,0:T(8,128)(2,1)}, ...) custom-call(s32[768]{0:T(1024)} %multiply_add_fusion.place_ref, ...), custom_call_target="tpu_custom_call" | custom-call | tf_op jit(solution)/shard_map/gather_weights/pallas_call | solution.py:1241
  85.1 11.5 %embed_project.1 = (f32[1024,768]{1,0:T(8,128)}, bf16[1024,768]{1,0:T(8,128)(2,1)}, bf16[1024,768]{1,0:T(8,128)(2,1)}, bf16[1024,768]{1,0:T(8,128)(2,1)}, bf16[1024,768]{1,0:T(8,128)(2,1)}) custom-call(s32[1024,128]{1,0:T(8,128)} %get-tuple-element.59.column_ref, f32[128,768]{1,0:T(8,128)} %weight_ref.1, f32[6,768]{1,0:T(8,128)} %norm_ref.7, ...), custom_call_target="tpu_custom_call" | custom-call | tf_op jit(solution)/shard_map/embed_project/pallas_call | solution.py:267
  96.6 29.8 %attend_forward.1 = (bf16[1024,768]{1,0:T(8,128)(2,1)}, f32[1024,768]{1,0:T(8,128)}) custom-call(s32[2]{0:T(128)} %get-tuple-element.64.low_ref, s32[2]{0:T(128)} %get-tuple-element.65.half_ref, bf16[1024,768]{1,0:T(8,128)(2,1)} %get-tuple-element.66.q_ref, bf16[1024,768]{1,0:T(8,128)(2,1)} %get-tuple-element.67.k_ref, ...), custom_call_target="tpu_custom_call" | custom-call | tf_op jit(solution)/shard_map/attend_forward/pallas_call | solution.py:334
  126.4 47.9 %middle_rows.1 = (bf16[1024,768]{1,0:T(8,128)(2,1)}, bf16[1024,3072]{1,0:T(8,128)(2,1)}, bf16[1024,768]{1,0:T(8,128)(2,1)}, bf16[1024,3072]{1,0:T(8,128)(2,1)}, ...) custom-call(f32[1024,768]{1,0:T(8,128)} %get-tuple-element.71.x_ref,, ...), custom_call_target="tpu_custom_call" | custom-call | tf_op jit(solution)/shard_map/middle_rows/pallas_call | solution.py:537
  174.3 42.2 %attend_backward.1.gproj.gproj_ref = bf16[3,1024,768]{2,1,0:T(8,128)(2,1)} custom-call(s32[2]{0:T(128)} %get-tuple-element.64.low_ref, s32[2]{0:T(128)} %get-tuple-element.65.half_ref, bf16[1024,768]{1,0:T(8,128)(2,1)} %get-tuple-element.66.q_ref, bf16[1024,768]{1,0:T(8,128)(2,1)} %get-tuple-element.67.k_ref, bf16[1024,768]{1,0:T(8,128)(2,1)} %get-tuple-element.68.v_ref, ...), custom_call_target="tpu_custom_call" | custom-call | tf_op jit(solution)/shard_map/attend_backward/pallas_call | solution.py:422
  216.6 12.1 %tail_rows.1 = (f32[128,768]{1,0:T(8,128)}, f32[8,768]{1,0:T(8,128)}) custom-call(s32[1024,128]{1,0:T(8,128)} %get-tuple-element.59.column_ref, f32[1024,768]{1,0:T(8,128)} %get-tuple-element.71.x_ref, f32[1024,768]{1,0:T(8,128)} %get-tuple-element.83.gx_ref, bf16[3,1024,768]{2,1,0:T(8,128)(2,1)} %attend_backward.1.gproj.gproj_ref, f32[6,768]{1,0:T(8,128)} %norm_ref.7, ...), custom_call_target="tpu_custom_call" | custom-call | tf_op jit(solution)/shard_map/tail_rows/pallas_call | solution.py:596
  228.7 0.7 add.338.place_ref
  229.4 32.0 %weight_gradients.1 = f32[768,72,128]{2,1,0:T(8,128)} custom-call(s32[768]{0:T(1024)} %add.338.place_ref, bf16[1024,768]{1,0:T(8,128)(2,1)} %get-tuple-element.63.h_one, bf16[1024,768]{1,0:T(8,128)(2,1)} %get-tuple-element.70.att_ref.att, bf16[1024,768]{1,0:T(8,128)(2,1)} %get-tuple-element.76.h_two, bf16[1024,3072]{1,0:T(8,128)(2,1)} %get-tuple-element.77.active, ...), custom_call_target="tpu_custom_call" | custom-call | tf_op jit(solution)/shard_map/weight_gradients/pallas_call | solution.py:707
  261.4 130.8 %sum_gradients.1 = (f32[24,96,96]{2,1,0:T(8,128)}, f32[128,768]{1,0:T(8,128)}, f32[8,768]{1,0:T(8,128)}, f32[8,128]{1,0:T(8,128)}) custom-call(f32[24,2,2,2,2,2,72,128]{7,6,5,4,3,2,1,0:T(8,128)} %bitcast.16, f32[128,768]{1,0:T(8,128)} %get-tuple-element.86.table_ref, f32[8,768]{1,0:T(8,128)} %get-tuple-element.87.norm_ref, f32[8,128]{1,0:T(8,128)} %get-tuple-element.72.count_ref), custom_call_target="tpu_custom_call" | custom-call | tf_op jit(solution)/shard_map/sum_gradients/pallas_call | solution.py:1031
  392.9 0.6 maximum_bitcast_fusion.step_ref
  393.5 6.8 %update_table.1 = (f32[128,768]{1,0:T(8,128)}, f32[128,128]{1,0:T(8,128)}, f32[768,768]{1,0:T(8,128)}, f32[128,768]{1,0:T(8,128)}, f32[6,768]{1,0:T(8,128)}, /*i...) custom-call(f32[1,2]{1,0:T(1,128)} %maximum_bitcast_fusion.step_ref, f32[8,128]{1,0:T(8,128)} %get-tuple-element.88.stats_ref, ...), custom_call_target="tpu_custom_call" | custom-call | tf_op jit(solution)/shard_map/update_table/pallas_call | solution.py:1372
  400.3 9.8 %update_blocks.1 = (f32[24,96,96]{2,1,0:T(8,128)}, f32[24,96,96]{2,1,0:T(8,128)}, f32[24,96,96]{2,1,0:T(8,128)}, f32[24,96,96]{2,1,0:T(8,128)}) custom-call(f32[8,128]{1,0:T(8,128)} %get-tuple-element.88.stats_ref, f32[24,96,96]{2,1,0:T(8,128)} %get-tuple-element.89.grad_ref, f32[24,96,96]{2,1,0:T(8,128)} %bitcast.19, f32[24,96,96]{2,1,0:T(8,128)} %bitcast.20, ...), custom_call_target="tpu_custom_call" | custom-call | tf_op jit(solution)/shard_map/update_blocks/pallas_call | solution.py:1314
  410.2 1.3 fusion.7
  (13 shorter events, 0.1 us)

commit v4 on v3

--- a/solution.py
+++ b/solution.py
@@ -231,20 +231,19 @@
     return values * cosine + other * sine
 
 
-def front_kernel(
-    column_ref, table_ref, norm_ref, project_ref, cos_ref, sin_ref, x_ref, h_ref, q_ref, k_ref, v_ref
-):
-    rows = column_ref.shape[0]
-    vocab, width = table_ref.shape
+def embed_rows(codon_col, table, gain, bias):
+    rows, (vocab, width) = codon_col.shape[0], table.shape
     index = lax.broadcasted_iota(jnp.int32, (rows, vocab), 1)
-    hot = jnp.where(column_ref[:, 0:1] == index, 1.0, 0.0).astype(BF16)
-    high, middle, low = split_three(table_ref[...])
-    embedded = (dot(hot, high) + dot(hot, middle)) + dot(hot, low)
-    embedded = embedded * math.sqrt(width)
-    x_ref[...] = embedded
+    hot = jnp.where(codon_col == index, 1.0, 0.0).astype(BF16)
+    high, middle, low = split_three(table)
+    embedded = ((dot(hot, high) + dot(hot, middle)) + dot(hot, low)) * math.sqrt(width)
     unit, _ = norm_parts(embedded)
-    normed = (unit * norm_ref[0:1, :] + norm_ref[1:2, :]).astype(BF16)
-    h_ref[...] = normed
+    return embedded, (unit * gain + bias).astype(BF16)
+
+
+def front_kernel(h_ref, project_ref, cos_ref, sin_ref, q_ref, k_ref, v_ref):
+    width = h_ref.shape[1]
+    normed = h_ref[...]
     cosine = cos_ref[...]
     sine = sin_ref[...]
     for part, out_ref in ((0, q_ref), (1, k_ref), (2, v_ref)):
@@ -258,28 +257,20 @@
             out_ref[:, c * LANES : (c + 1) * LANES] = piece.astype(BF16)
 
 
-def front(columns, table, norm_params, project, cosine, sine):
-    length, kinds = columns.shape
-    vocab, width = table.shape
+def front(normed, project, cosine, sine):
+    length, width = normed.shape
     rows = 256
     spec = pl.BlockSpec((rows, width), lambda i: (i, 0))
-    low = jax.ShapeDtypeStruct((length, width), BF16)
+    narrow = pl.BlockSpec((rows, LANES), lambda i: (i, 0))
     return pl.pallas_call(
         front_kernel,
-        out_shape=(jax.ShapeDtypeStruct((length, width), F32), low, low, low, low),
+        out_shape=(jax.ShapeDtypeStruct((length, width), BF16),) * 3,
         grid=(length // rows,),
-        in_specs=[
-            pl.BlockSpec((rows, kinds), lambda i: (i, 0)),
-            whole(table.shape),
-            whole(norm_params.shape),
-            whole(project.shape),
-            pl.BlockSpec((rows, LANES), lambda i: (i, 0)),
-            pl.BlockSpec((rows, LANES), lambda i: (i, 0)),
-        ],
-        out_specs=(spec, spec, spec, spec, spec),
+        in_specs=[spec, whole(project.shape), narrow, narrow],
+        out_specs=(spec,) * 3,
         compiler_params=params(),
-        name="embed_project",
-    )(columns, table, norm_params, project, cosine, sine)
+        name="project_rotate",
+    )(normed, project, cosine, sine)
 
 
 ROWS = 512
@@ -453,9 +444,9 @@
 
 def middle_kernel(
     x_ref, att_ref, column_ref, count_ref, norm_ref, table_ref,
-    outward_ref, expand_ref, contract_ref,
+    outward_ref, expand_in, contract_in,
     h_ref, active_ref, d_two_ref, ghid_ref, d_one_ref, gatt_ref, gx_ref, head_ref, norm_grad_ref,
-    slope,
+    slope, expand_ref, contract_ref, weight_sem,
 ):
     step = pl.program_id(0)
     rows, width = x_ref.shape
@@ -463,8 +454,15 @@
     ff = expand_ref.shape[1]
     part = width
 
+    fetches = (
+        pltpu.make_async_copy(expand_in, expand_ref, weight_sem.at[0]),
+        pltpu.make_async_copy(contract_in, contract_ref, weight_sem.at[1]),
+    )
+
     @pl.when(step == 0)
     def _():
+        for fetch in fetches:
+            fetch.start()
         head_ref[...] = jnp.zeros_like(head_ref)
         norm_grad_ref[...] = jnp.zeros_like(norm_grad_ref)
 
@@ -473,6 +471,11 @@
     gain_two = norm_ref[2:3, :]
     normed_two = (unit_two * gain_two + norm_ref[3:4, :]).astype(BF16)
     h_ref[...] = normed_two
+
+    @pl.when(step == 0)
+    def _():
+        for fetch in fetches:
+            fetch.wait()
 
     def forward(c, total):
         cols = pl.ds(pl.multiple_of(c * part, part), part)
@@ -545,13 +548,18 @@
         grid=(length // rows,),
         in_specs=[
             narrow, narrow, column, whole(count.shape), whole(norm_params.shape), whole(table.shape),
-            whole(outward.shape), whole(expand.shape), whole(contract.shape),
+            whole(outward.shape), pl.BlockSpec(memory_space=pl.ANY), pl.BlockSpec(memory_space=pl.ANY),
         ],
         out_specs=(
             narrow, broad, narrow, broad, narrow, narrow, narrow,
             whole((vocab, width)), whole((8, width)),
         ),
-        scratch_shapes=[pltpu.VMEM((rows, ff), F32)],
+        scratch_shapes=[
+            pltpu.VMEM((rows, ff), F32),
+            pltpu.VMEM(expand.shape, BF16),
+            pltpu.VMEM(contract.shape, BF16),
+            pltpu.SemaphoreType.DMA((2,)),
+        ],
         compiler_params=params(),
         name="middle_rows",
     )(x, att, columns, count, norm_params, table, outward, expand, contract)
@@ -1068,6 +1076,7 @@
     (NEAR_X, NEAR_Z, FAR_Z, NEAR_Y),
     (NEAR_Y, NEAR_X, FAR_Z, NEAR_Z),
 )
+EMBED_ROWS = 256
 HALVES = 2
 GATHER_CHUNKS = PACK_GROUPS * HALVES
 GATHER_ORDER = (
@@ -1087,11 +1096,11 @@
 
 
 def gather_kernel(
-    place_ref, own_ref, codon_ref, target_ref, mask_ref, segments_ref,
-    project_out, outward_out, expand_out, contract_out,
+    place_ref, own_ref, codon_ref, target_ref, mask_ref, segments_ref, table_ref, norm_ref,
+    project_out, outward_out, expand_out, contract_out, x_out, h_out,
     count_ref, column_ref, seg_row_ref, cos_ref, sin_ref, low_ref, half_ref,
-    packed, held, store, project, outward, expand, contract, counts,
-    own_sem, send_sem, recv_sem, count_send, count_recv, out_sem, *, sizes,
+    packed, held, store, project, outward, expand, contract, x_rows, h_rows, counts,
+    own_sem, send_sem, recv_sem, count_send, count_recv, out_sem, row_sem, *, sizes,
 ):
     owner, shard, bits = own_bits()
     edge = own_ref.shape[1]
@@ -1154,7 +1163,7 @@
             unpack_rows(store, (group * devices + e) * PACK, held[c, e], offset, edge)
             return carry
 
-        lax.fori_loop(0, devices, body, 0, unroll=2)
+        lax.fori_loop(0, devices, body, 0, unroll=4)
 
     def describe_rows():
         length = codon_ref.shape[1]
@@ -1179,6 +1188,17 @@
         cos_ref[rows, :], sin_ref[rows, :] = rotary_of(place, lane)
         return carry
 
+    def embed(i, carry):
+        rows = pl.ds(pl.multiple_of(i * EMBED_ROWS, EMBED_ROWS), EMBED_ROWS)
+        x_rows[rows, :], h_rows[rows, :] = embed_rows(
+            column_ref[rows, 0:1], table_ref[...], norm_ref[0:1, :], norm_ref[1:2, :]
+        )
+        return carry
+
+    row_copies = (
+        pltpu.make_async_copy(x_rows, x_out, row_sem.at[0]),
+        pltpu.make_async_copy(h_rows, h_out, row_sem.at[1]),
+    )
     stage = 0
     for position, code in enumerate(GATHER_ORDER):
         c, k = code % 1000 // 10, code % 10
@@ -1194,6 +1214,10 @@
             describe_rows()
         if position == 30:
             lax.fori_loop(0, cos_ref.shape[0] // LANES, rotary_rows, 0)
+        if position == 55:
+            lax.fori_loop(0, x_rows.shape[0] // EMBED_ROWS, embed, 0)
+            for copy in row_copies:
+                copy.start()
         if position == 0:
             count_copy(0).start()
         elif position % 12 == 0 and stage < 5:
@@ -1229,19 +1253,23 @@
         count_copy(k).wait_send()
     for n, (inside, outside) in enumerate(staged):
         pltpu.make_async_copy(inside, outside, out_sem.at[n]).wait()
-
-
-def gather_everywhere(place, own, codons, targets, mask, segments, devices, sizes):
+    for copy in row_copies:
+        copy.wait()
+
+
+def gather_everywhere(place, own, rows, table, norm_params, devices, sizes):
     slots, edge, _ = own.shape
     width, _, _, hidden_width = sizes
     strip = PACK * edge
     shapes = matrix_shapes(width, hidden_width)
-    length = codons.shape[1]
+    length = rows[0].shape[1]
     inside, scalars = pl.BlockSpec(memory_space=pltpu.VMEM), pl.BlockSpec(memory_space=pltpu.SMEM)
     return pl.pallas_call(
         functools.partial(gather_kernel, sizes=sizes),
         out_shape=shapes
         + (
+            jax.ShapeDtypeStruct((length, width), F32),
+            jax.ShapeDtypeStruct((length, width), BF16),
             jax.ShapeDtypeStruct((8, LANES), F32),
             jax.ShapeDtypeStruct((length, LANES), jnp.int32),
             jax.ShapeDtypeStruct((length // TILE, 1, TILE), jnp.int32),
@@ -1250,13 +1278,15 @@
             jax.ShapeDtypeStruct((length // ROWS,), jnp.int32),
             jax.ShapeDtypeStruct((length // ROWS,), jnp.int32),
         ),
-        in_specs=[scalars] + [inside] * 5,
-        out_specs=(pl.BlockSpec(memory_space=pl.ANY),) * 4 + (inside,) * 5 + (scalars,) * 2,
+        in_specs=[scalars] + [inside] * 7,
+        out_specs=(pl.BlockSpec(memory_space=pl.ANY),) * 6 + (inside,) * 5 + (scalars,) * 2,
         scratch_shapes=[
             pltpu.VMEM((PACK_GROUPS, edge, strip), BF16),
             pltpu.VMEM((GATHER_CHUNKS, devices, edge // HALVES, strip), BF16),
             pltpu.VMEM((devices * slots, edge, LANES), BF16),
             *[pltpu.VMEM(shape.shape, shape.dtype) for shape in shapes],
+            pltpu.VMEM((length, width), F32),
+            pltpu.VMEM((length, width), BF16),
             pltpu.VMEM((10, 8, LANES), F32),
             pltpu.SemaphoreType.DMA((GATHER_CHUNKS,)),
             pltpu.SemaphoreType.DMA((GATHER_CHUNKS, 5)),
@@ -1264,10 +1294,11 @@
             pltpu.SemaphoreType.DMA((5,)),
             pltpu.SemaphoreType.DMA((5,)),
             pltpu.SemaphoreType.DMA((4,)),
+            pltpu.SemaphoreType.DMA((2,)),
         ],
         compiler_params=params(collective_id=2, has_side_effects=True),
         name="gather_weights",
-    )(place, own, codons, targets, mask, segments)
+    )(place, own, *rows, table, norm_params)
 
 
 def split_two(values):
@@ -1293,11 +1324,31 @@
     return new_left, new_right, new_weight
 
 
-def block_update_kernel(
-    stats_ref, grad_ref, left_ref, right_ref, left_root_ref, right_root_ref, weight_ref,
+TABLE_STEP = 3
+
+
+def update_kernel(
+    corrections_ref, stats_ref, table_grad_ref, table_left_ref, table_left_root_ref, table_ref,
+    norm_grad_ref, moment_ref, second_ref, norm_ref, table_right_in, table_right_root_in,
+    grad_ref, left_ref, right_ref, left_root_ref, right_root_ref, weight_ref,
+    table_grad_out, table_left_out, table_right_out, table_out,
+    norm_grad_out, moment_out, second_out, norm_out,
     grad_out, left_out, right_out, weight_out,
+    grad_parts, precond, table_right, table_right_root, sem,
 ):
+    step, steps = pl.program_id(0), pl.num_programs(0)
     factor = stats_ref[0:1, 0:1]
+    fetches = (
+        pltpu.make_async_copy(table_right_in, table_right, sem.at[0]),
+        pltpu.make_async_copy(table_right_root_in, table_right_root, sem.at[1]),
+    )
+    keep = pltpu.make_async_copy(table_right, table_right_out, sem.at[2])
+
+    @pl.when(step == 0)
+    def _():
+        for fetch in fetches:
+            fetch.start()
+
     for b in range(grad_ref.shape[0]):
         grad = grad_ref[b] * factor
         grad_out[b] = grad
@@ -1305,77 +1356,83 @@
             grad, left_ref[b], right_ref[b], left_root_ref[b], right_root_ref[b], weight_ref[b]
         )
 
-
-def update_blocks(stats, grads, left, right, left_root, right_root, weight):
-    count, edge, _ = grads.shape
+    @pl.when(step == jnp.minimum(TABLE_STEP, steps - 1))
+    def _():
+        for fetch in fetches:
+            fetch.wait()
+        grad = table_grad_ref[...] * factor
+        table_grad_out[...] = grad
+        parts = split_two(grad)
+        table_left_out[...] = STAT_DECAY * table_left_ref[...] + (1.0 - STAT_DECAY) * dot_split(
+            parts, parts, ((1,), (1,))
+        )
+        half = split_two(dot_split(split_two(table_left_root_ref[...]), parts, ((1,), (0,))))
+        for n in range(2):
+            grad_parts[n] = parts[n]
+        width = grad.shape[1]
+        strip = width // 3
+
+        def strip_body(i, carry):
+            cols = pl.ds(pl.multiple_of(i * strip, strip), strip)
+            own = (grad_parts[0, :, cols], grad_parts[1, :, cols])
+            table_right[cols, :] = STAT_DECAY * table_right[cols, :] + (1.0 - STAT_DECAY) * dot_split(
+                own, parts, ((0,), (0,))
+            )
+            precond[:, cols] = dot_split(half, split_two(table_right_root[:, cols]), ((1,), (0,)))
+            return carry
+
+        lax.fori_loop(0, 3, strip_body, 0)
+        keep.start()
+        turned = precond[...]
+        mean = total_of(turned * turned) * (1.0 / (grad.shape[0] * width))
+        table_out[...] = table_ref[...] * (
+            1.0 - MATRIX_RATE * WEIGHT_DECAY
+        ) - MATRIX_RATE * turned * lax.rsqrt(mean + ROOT_EPSILON)
+        clipped = norm_grad_ref[0 : norm_ref.shape[0], :] * factor
+        norm_grad_out[...] = clipped
+        moment = FIRST_BETA * moment_ref[...] + (1.0 - FIRST_BETA) * clipped
+        second = SECOND_BETA * second_ref[...] + (1.0 - SECOND_BETA) * clipped * clipped
+        moment_out[...] = moment
+        second_out[...] = second
+        one = moment / corrections_ref[0:1, 0:1]
+        two = second / corrections_ref[0:1, 1:2]
+        weight = norm_ref[...]
+        norm_out[...] = weight - VECTOR_RATE * (
+            one / (jnp.sqrt(two) + ADAM_EPSILON) + WEIGHT_DECAY * weight
+        )
+
+    @pl.when(step == steps - 1)
+    def _():
+        keep.wait()
+
+
+def update_all(small, right, right_root, blocks):
+    corrections, stats, table_grad, table_left, table_left_root, table, norm_grad, moment, second, norms = small
+    count, edge, _ = blocks[0].shape
     per_step = PACK if count % PACK == 0 else 1
     spec = pl.BlockSpec((per_step, edge, edge), lambda i: (i, 0, 0))
-    out = jax.ShapeDtypeStruct(grads.shape, F32)
-    return pl.pallas_call(
-        block_update_kernel,
-        out_shape=(out,) * 4,
-        grid=(count // per_step,),
-        in_specs=[whole(stats.shape)] + [spec] * 6,
-        out_specs=(spec,) * 4,
-        compiler_params=params(),
-        name="update_blocks",
-    )(stats, grads, left, right, left_root, right_root, weight)
-
-
-def table_update_kernel(
-    step_ref, stats_ref, grad_ref, left_ref, right_ref, left_root_ref, right_root_ref, weight_ref,
-    norm_grad_ref, moment_ref, second_ref, norm_ref,
-    grad_out, left_out, right_out, weight_out, norm_grad_out, moment_out, second_out, norm_out,
-    grad_parts, precond,
-):
-    factor = stats_ref[0:1, 0:1]
-    grad = grad_ref[...] * factor
-    grad_out[...] = grad
-    parts = split_two(grad)
-    left_out[...] = STAT_DECAY * left_ref[...] + (1.0 - STAT_DECAY) * dot_split(parts, parts, ((1,), (1,)))
-    half = split_two(dot_split(split_two(left_root_ref[...]), parts, ((1,), (0,))))
-    for n in range(2):
-        grad_parts[n] = parts[n]
-    width = grad.shape[1]
-    strip = width // 3
-
-    def strip_body(i, carry):
-        cols = pl.ds(pl.multiple_of(i * strip, strip), strip)
-        own = (grad_parts[0, :, cols], grad_parts[1, :, cols])
-        right_out[cols, :] = STAT_DECAY * right_ref[cols, :] + (1.0 - STAT_DECAY) * dot_split(
-            own, parts, ((0,), (0,))
-        )
-        precond[:, cols] = dot_split(half, split_two(right_root_ref[:, cols]), ((1,), (0,)))
-        return carry
-
-    lax.fori_loop(0, 3, strip_body, 0)
-    turned = precond[...]
-    mean = total_of(turned * turned) * (1.0 / (grad.shape[0] * width))
-    weight_out[...] = weight_ref[...] * (1.0 - MATRIX_RATE * WEIGHT_DECAY) - MATRIX_RATE * turned * lax.rsqrt(
-        mean + ROOT_EPSILON
-    )
-    rows = norm_ref.shape[0]
-    clipped = norm_grad_ref[0:rows, :] * factor
-    norm_grad_out[...] = clipped
-    moment = FIRST_BETA * moment_ref[...] + (1.0 - FIRST_BETA) * clipped
-    second = SECOND_BETA * second_ref[...] + (1.0 - SECOND_BETA) * clipped * clipped
-    moment_out[...] = moment
-    second_out[...] = second
-    one = moment / step_ref[0:1, 0:1]
-    two = second / step_ref[0:1, 1:2]
-    weight = norm_ref[...]
-    norm_out[...] = weight - VECTOR_RATE * (one / (jnp.sqrt(two) + ADAM_EPSILON) + WEIGHT_DECAY * weight)
-
-
-def update_table(corrections, stats, grad, left, right, left_root, right_root, weight, norm_grad, moment, second, norms):
+    anywhere = pl.BlockSpec(memory_space=pl.ANY)
     like = lambda array: jax.ShapeDtypeStruct(array.shape, F32)
     return pl.pallas_call(
-        table_update_kernel,
-        out_shape=(like(grad), like(left), like(right), like(weight)) + (like(norms),) * 4,
-        scratch_shapes=[pltpu.VMEM((2,) + grad.shape, BF16), pltpu.VMEM(grad.shape, F32)],
+        update_kernel,
+        out_shape=(like(table_grad), like(table_left), like(right), like(table))
+        + (like(norms),) * 4
+        + (like(blocks[0]),) * 4,
+        grid=(count // per_step,),
+        in_specs=[whole(array.shape) for array in small] + [anywhere] * 2 + [spec] * 6,
+        out_specs=(whole(table_grad.shape), whole(table_left.shape), anywhere, whole(table.shape))
+        + (whole(norms.shape),) * 4
+        + (spec,) * 4,
+        scratch_shapes=[
+            pltpu.VMEM((2,) + table_grad.shape, BF16),
+            pltpu.VMEM(table_grad.shape, F32),
+            pltpu.VMEM(right.shape, F32),
+            pltpu.VMEM(right.shape, F32),
+            pltpu.SemaphoreType.DMA((3,)),
+        ],
         compiler_params=params(),
-        name="update_table",
-    )(corrections, stats, grad, left, right, left_root, right_root, weight, norm_grad, moment, second, norms)
+        name="update_all",
+    )(*small, right, right_root, *blocks)
 
 
 def rotary_of(place, lane):
@@ -1398,8 +1455,9 @@
     return groups.reshape(count // PACK, edge, PACK * edge)
 
 
-def gather_weights(own, codons, targets, mask, segments, owner_map, known, sizes):
+def gather_weights(own, rows, table, norm_params, owner_map, known, sizes):
     everyone = ("dp", "tensor")
+    codons, targets, mask, segments = rows
     slots, edge, _ = own.shape
     shards = sizes[1]
     owner, slot = owner_map[None, :] // slots, owner_map[None, :] % slots
@@ -1411,7 +1469,7 @@
         for g in range(1, PACK_GROUPS):
             entry = jnp.where(group == g, gather_entry(g, bits), entry)
         place = ((group * 32 + entry) * PACK + slot % PACK).reshape(-1)
-        return gather_everywhere(place, own, codons, targets, mask, segments, 32, sizes)
+        return gather_everywhere(place, own, rows, table, norm_params, 32, sizes)
     packed = pack_blocks(lax.all_gather(own.astype(BF16), everyone, axis=0, tiled=True))
     count = jnp.maximum(lax.psum(jnp.sum(mask.astype(F32)), everyone), 1.0)
     place = ((owner * shards + shard) * slots + slot).reshape(-1)
@@ -1426,7 +1484,7 @@
     cosine, sine = rotary_of(
         jnp.arange(length, dtype=jnp.int32)[:, None], jnp.arange(LANES, dtype=jnp.int32)[None, :]
     )
-    return assemble(place, packed, sizes) + (
+    return assemble(place, packed, sizes) + embed_rows(columns[:, :1], table, norm_params[0:1], norm_params[1:2]) + (
         jnp.broadcast_to(count, (8, LANES)), columns, segment.reshape(tiles, 1, TILE), cosine, sine,
     ) + spans
 
@@ -1463,11 +1521,10 @@
 
     known = on_known_slice(owners, shards, slots)
     sizes = (width, shards, shard_width, FF)
-    project, outward, expand, contract, count, columns, seg_row, cosine, sine, *spans = gather_weights(
-        block_weight[0], codons, targets, loss_mask, segments, owner_map, known, sizes
+    project, outward, expand, contract, x0, h1, count, columns, seg_row, cosine, sine, *spans = gather_weights(
+        block_weight[0], (codons, targets, loss_mask, segments), embedding_weight, norm_params, owner_map, known, sizes
     )
-
-    x0, h1, query, keys, values = front(columns, embedding_weight, norm_params, project, cosine, sine)
+    query, keys, values = front(h1, project, cosine, sine)
     attended, lse = attend(*spans, query, keys, values, columns, seg_row)
     (h2, active, d_two, ghid, d_one, gatt, gx, head_grad, norm_grad) = middle_rows(
         x0, attended, columns, count, norm_params, embedding_weight,
@@ -1505,15 +1562,18 @@
     loss_value, grad_norm = stats[2, 0], stats[1, 0]
     step_value = step_count.astype(F32)
     corrections = jnp.stack([1.0 - FIRST_BETA**step_value, 1.0 - SECOND_BETA**step_value]).reshape(1, 2)
-    block_grad, new_left, new_right, new_weight = update_blocks(
-        stats, owned, block_left[0], block_right[0], block_left_root[0], block_right_root[0], block_weight[0]
-    )
     (
         table_clipped, table_left_new, table_right_new, table_weight_new,
         norm_clipped, moment_new, second_new, params_new,
-    ) = update_table(
-        corrections, stats, table_grad, table_left, table_right, table_left_root, table_right_root,
-        embedding_weight, norm_grad, norm_moment, norm_second, norm_params,
+        block_grad, new_left, new_right, new_weight,
+    ) = update_all(
+        (
+            corrections, stats, table_grad, table_left, table_left_root, embedding_weight,
+            norm_grad, norm_moment, norm_second, norm_params,
+        ),
+        table_right,
+        table_right_root,
+        (owned, block_left[0], block_right[0], block_left_root[0], block_right_root[0], block_weight[0]),
     )
     return (
         loss_value,

time: 412 us -> 403 us (0.978)
  Pallas kernels: 404 us -> 397 us
    pallas_call x1, Pallas kernels: 81.4 us -> 77.2 us  [gather_everywhere(): pl.pallas_call(functools.partial(gather_kernel, sizes=sizes), out_shape=s...]
    pallas_call x2 -> x1, Pallas kernels: 16.6 us -> 15 us  [update_all(): pl.pallas_call(update_kernel, out_shape=(like(table_grad), like(table_lef...]
where the time goes in v4:
time: 403 us; the launch traced here: 404 us
  Pallas kernels  397 us (99%)
    pallas_call x1, Pallas kernels, sum_everywhere(): pl.pallas_call(sum_kernel, out_shape=(jax.ShapeDtypeStruct((chunks, edge,...  133 us
    pallas_call x1, Pallas kernels, gather_everywhere(): pl.pallas_call(functools.partial(gather_kernel, sizes=sizes), out_shape=s...  77.2 us
    pallas_call x1, Pallas kernels, middle_rows(): pl.pallas_call(middle_kernel, out_shape=(low, low_broad, low, low_broad,...  47.6 us
    pallas_call x1, Pallas kernels, attend_back(): pl.pallas_call(attend_back_kernel, out_shape=jax.ShapeDtypeStruct((3, len...  42.2 us
    pallas_call x1, Pallas kernels, weight_grads(): pl.pallas_call(functools.partial(weight_grad_kernel, sizes=sizes, edge=ed...  32 us
    pallas_call x1, Pallas kernels, attend(): pl.pallas_call(attend_kernel, out_shape=(jax.ShapeDtypeStruct((length, wi...  29.8 us
    pallas_call x1, Pallas kernels, update_all(): pl.pallas_call(update_kernel, out_shape=(like(table_grad), like(table_lef...  15 us
    pallas_call x1, Pallas kernels, tail_rows(): pl.pallas_call(tail_kernel, out_shape=(jax.ShapeDtypeStruct(head.shape, F...  12.1 us

profile of v4, /device:TPU:0, one launch (start us, length us, event | category | flops | bytes accessed | tf_op | source)
XLA Modules:
  0.0 403.6 jit_solution(4979779101187404233)
XLA Ops:
  0.6 0.7 broadcast_multiply_fusion.3
  1.4 0.7 broadcast_compare_fusion.4
  2.1 0.1 fusion.4
  2.2 0.1 add.352
  2.3 0.1 add.361
  2.3 0.1 add.369
  2.4 0.1 reshape.266
  2.5 0.1 add.340
  2.6 0.1 add.383
  2.7 0.1 broadcast_in_dim.57
  2.8 0.1 broadcast_in_dim.59
  2.9 0.1 broadcast_in_dim.61
  3.0 0.1 broadcast_in_dim.63
  3.1 0.6 multiply_add_fusion.place_ref
  3.7 77.2 %gather_weights.1 = (bf16[768,2304]{1,0:T(8,128)(2,1)}, bf16[768,768]{1,0:T(8,128)(2,1)}, bf16[768,3072]{1,0:T(8,128)(2,1)}, bf16[3072,768]{1,0:T(8,128)(2,1)}, ...) custom-call(s32[768]{0:T(1024)} %multiply_add_fusion.place_ref, ...), custom_call_target="tpu_custom_call" | custom-call | tf_op jit(solution)/shard_map/gather_weights/pallas_call | solution.py:1267
  80.9 8.1 %project_rotate.1 = (bf16[1024,768]{1,0:T(8,128)(2,1)}, bf16[1024,768]{1,0:T(8,128)(2,1)}, bf16[1024,768]{1,0:T(8,128)(2,1)}) custom-call(bf16[1024,768]{1,0:T(8,128)(2,1)} %get-tuple-element.59.h_ref.h_one, bf16[768,2304]{1,0:T(8,128)(2,1)} %get-tuple-element.62.project_ref, f32[1024,128]{1,0:T(8,128)} %get-tuple-element.63.cos_ref, ...), custom_call_target="tpu_custom_call" | custom-call | tf_op jit(solution)/shard_map/project_rotate/pallas_call | solution.py:265
  89.0 29.8 %attend_forward.1 = (bf16[1024,768]{1,0:T(8,128)(2,1)}, f32[1024,768]{1,0:T(8,128)}) custom-call(s32[2]{0:T(128)} %get-tuple-element.60.low_ref, s32[2]{0:T(128)} %get-tuple-element.61.half_ref, bf16[1024,768]{1,0:T(8,128)(2,1)} %get-tuple-element.65.q_ref, bf16[1024,768]{1,0:T(8,128)(2,1)} %get-tuple-element.66.k_ref, ...), custom_call_target="tpu_custom_call" | custom-call | tf_op jit(solution)/shard_map/attend_forward/pallas_call | solution.py:325
  118.8 47.6 %middle_rows.1 = (bf16[1024,768]{1,0:T(8,128)(2,1)}, bf16[1024,3072]{1,0:T(8,128)(2,1)}, bf16[1024,768]{1,0:T(8,128)(2,1)}, bf16[1024,3072]{1,0:T(8,128)(2,1)}, ...) custom-call(f32[1024,768]{1,0:T(8,128)} %get-tuple-element.71.x_ref,, ...), custom_call_target="tpu_custom_call" | custom-call | tf_op jit(solution)/shard_map/middle_rows/pallas_call | solution.py:540
  166.4 42.2 %attend_backward.1.gproj.gproj_ref = bf16[3,1024,768]{2,1,0:T(8,128)(2,1)} custom-call(s32[2]{0:T(128)} %get-tuple-element.60.low_ref, s32[2]{0:T(128)} %get-tuple-element.61.half_ref, bf16[1024,768]{1,0:T(8,128)(2,1)} %get-tuple-element.65.q_ref, bf16[1024,768]{1,0:T(8,128)(2,1)} %get-tuple-element.66.k_ref, bf16[1024,768]{1,0:T(8,128)(2,1)} %get-tuple-element.67.v_ref, ...), custom_call_target="tpu_custom_call" | custom-call | tf_op jit(solution)/shard_map/attend_backward/pallas_call | solution.py:413
  208.5 12.1 %tail_rows.1 = (f32[128,768]{1,0:T(8,128)}, f32[8,768]{1,0:T(8,128)}) custom-call(s32[1024,128]{1,0:T(8,128)} %get-tuple-element.68.column_ref, f32[1024,768]{1,0:T(8,128)} %get-tuple-element.71.x_ref, f32[1024,768]{1,0:T(8,128)} %get-tuple-element.83.gx_ref, bf16[3,1024,768]{2,1,0:T(8,128)(2,1)} %attend_backward.1.gproj.gproj_ref, f32[6,768]{1,0:T(8,128)} %norm_ref.7, ...), custom_call_target="tpu_custom_call" | custom-call | tf_op jit(solution)/shard_map/tail_rows/pallas_call | solution.py:604
  220.6 0.7 add.338.place_ref
  221.3 32.0 %weight_gradients.1 = f32[768,72,128]{2,1,0:T(8,128)} custom-call(s32[768]{0:T(1024)} %add.338.place_ref, bf16[1024,768]{1,0:T(8,128)(2,1)} %get-tuple-element.59.h_ref.h_one, bf16[1024,768]{1,0:T(8,128)(2,1)} %get-tuple-element.70.att_ref.att, bf16[1024,768]{1,0:T(8,128)(2,1)} %get-tuple-element.76.h_two, bf16[1024,3072]{1,0:T(8,128)(2,1)} %get-tuple-element.77.active, ...), custom_call_target="tpu_custom_call" | custom-call | tf_op jit(solution)/shard_map/weight_gradients/pallas_call | solution.py:715
  253.3 132.6 %sum_gradients.1 = (f32[24,96,96]{2,1,0:T(8,128)}, f32[128,768]{1,0:T(8,128)}, f32[8,768]{1,0:T(8,128)}, f32[8,128]{1,0:T(8,128)}) custom-call(f32[24,2,2,2,2,2,72,128]{7,6,5,4,3,2,1,0:T(8,128)} %bitcast.16, f32[128,768]{1,0:T(8,128)} %get-tuple-element.86.table_ref, f32[8,768]{1,0:T(8,128)} %get-tuple-element.87.norm_ref, f32[8,128]{1,0:T(8,128)} %get-tuple-element.72.count_ref), custom_call_target="tpu_custom_call" | custom-call | tf_op jit(solution)/shard_map/sum_gradients/pallas_call | solution.py:1039
  386.7 0.6 maximum_bitcast_fusion.corrections_ref
  387.3 15.0 %update_all.1 = (f32[128,768]{1,0:T(8,128)}, f32[128,128]{1,0:T(8,128)}, f32[768,768]{1,0:T(8,128)}, f32[128,768]{1,0:T(8,128)}, f32[6,768]{1,0:T(8,128)}, /*ind...) custom-call(f32[1,2]{1,0:T(1,128)} %maximum_bitcast_fusion.correctio, ...), custom_call_target="tpu_custom_call" | custom-call | tf_op jit(solution)/shard_map/update_all/pallas_call | solution.py:1416
  402.3 1.3 fusion.7
  (13 shorter events, 0.1 us)

commit v5 on v4

--- a/solution.py
+++ b/solution.py
@@ -1210,11 +1210,11 @@
             move(c, k).wait_recv()
             if k == 4:
                 unpack(c)
-        if position == 10:
+        if position == 16:
             describe_rows()
-        if position == 30:
+        if position == 45:
             lax.fori_loop(0, cos_ref.shape[0] // LANES, rotary_rows, 0)
-        if position == 55:
+        if position == 80:
             lax.fori_loop(0, x_rows.shape[0] // EMBED_ROWS, embed, 0)
             for copy in row_copies:
                 copy.start()

time: 403 us -> 403 us (level)
    pallas_call x1, Pallas kernels: 133 us -> 138 us  [sum_everywhere(): pl.pallas_call(sum_kernel, out_shape=(jax.ShapeDtypeStruct((chunks, edge,...]
    pallas_call x1, Pallas kernels: 42.2 us -> 37.8 us  [attend_back(): pl.pallas_call(attend_back_kernel, out_shape=jax.ShapeDtypeStruct((3, len...]
where the time goes in v5:
time: 403 us
  Pallas kernels  396 us (98%)
    pallas_call x1, Pallas kernels, sum_everywhere(): pl.pallas_call(sum_kernel, out_shape=(jax.ShapeDtypeStruct((chunks, edge,...  138 us
    pallas_call x1, Pallas kernels, gather_everywhere(): pl.pallas_call(functools.partial(gather_kernel, sizes=sizes), out_shape=s...  78.8 us
    pallas_call x1, Pallas kernels, middle_rows(): pl.pallas_call(middle_kernel, out_shape=(low, low_broad, low, low_broad,...  47.6 us
    pallas_call x1, Pallas kernels, attend_back(): pl.pallas_call(attend_back_kernel, out_shape=jax.ShapeDtypeStruct((3, len...  37.8 us
    pallas_call x1, Pallas kernels, weight_grads(): pl.pallas_call(functools.partial(weight_grad_kernel, sizes=sizes, edge=ed...  32 us
    pallas_call x1, Pallas kernels, attend(): pl.pallas_call(attend_kernel, out_shape=(jax.ShapeDtypeStruct((length, wi...  26.1 us
    pallas_call x1, Pallas kernels, update_all(): pl.pallas_call(update_kernel, out_shape=(like(table_grad), like(table_lef...  14.9 us
    pallas_call x1, Pallas kernels, tail_rows(): pl.pallas_call(tail_kernel, out_shape=(jax.ShapeDtypeStruct(head.shape, F...  12.1 us

profile of v5, /device:TPU:0, one launch (start us, length us, event | category | flops | bytes accessed | tf_op | source)
XLA Modules:
  0.0 402.8 jit_solution(9833469918272494190)
XLA Ops:
  0.6 0.7 broadcast_multiply_fusion.3
  1.4 0.7 broadcast_compare_fusion.4
  2.1 0.1 fusion.4
  2.2 0.1 add.352
  2.3 0.1 add.361
  2.3 0.1 add.369
  2.4 0.1 reshape.266
  2.5 0.1 add.340
  2.6 0.1 add.383
  2.7 0.1 broadcast_in_dim.57
  2.8 0.1 broadcast_in_dim.59
  2.9 0.1 broadcast_in_dim.61
  3.0 0.1 broadcast_in_dim.63
  3.1 0.6 multiply_add_fusion.place_ref
  3.7 78.8 %gather_weights.1 = (bf16[768,2304]{1,0:T(8,128)(2,1)}, bf16[768,768]{1,0:T(8,128)(2,1)}, bf16[768,3072]{1,0:T(8,128)(2,1)}, bf16[3072,768]{1,0:T(8,128)(2,1)}, ...) custom-call(s32[768]{0:T(1024)} %multiply_add_fusion.place_ref, ...), custom_call_target="tpu_custom_call" | custom-call | tf_op jit(solution)/shard_map/gather_weights/pallas_call | solution.py:1267
  82.5 8.1 %project_rotate.1 = (bf16[1024,768]{1,0:T(8,128)(2,1)}, bf16[1024,768]{1,0:T(8,128)(2,1)}, bf16[1024,768]{1,0:T(8,128)(2,1)}) custom-call(bf16[1024,768]{1,0:T(8,128)(2,1)} %get-tuple-element.59.h_ref.h_one, bf16[768,2304]{1,0:T(8,128)(2,1)} %get-tuple-element.62.project_ref, f32[1024,128]{1,0:T(8,128)} %get-tuple-element.63.cos_ref, ...), custom_call_target="tpu_custom_call" | custom-call | tf_op jit(solution)/shard_map/project_rotate/pallas_call | solution.py:265
  90.6 26.1 %attend_forward.1 = (bf16[1024,768]{1,0:T(8,128)(2,1)}, f32[1024,768]{1,0:T(8,128)}) custom-call(s32[2]{0:T(128)} %get-tuple-element.60.low_ref, s32[2]{0:T(128)} %get-tuple-element.61.half_ref, bf16[1024,768]{1,0:T(8,128)(2,1)} %get-tuple-element.65.q_ref, bf16[1024,768]{1,0:T(8,128)(2,1)} %get-tuple-element.66.k_ref, ...), custom_call_target="tpu_custom_call" | custom-call | tf_op jit(solution)/shard_map/attend_forward/pallas_call | solution.py:325
  116.7 47.6 %middle_rows.1 = (bf16[1024,768]{1,0:T(8,128)(2,1)}, bf16[1024,3072]{1,0:T(8,128)(2,1)}, bf16[1024,768]{1,0:T(8,128)(2,1)}, bf16[1024,3072]{1,0:T(8,128)(2,1)}, ...) custom-call(f32[1024,768]{1,0:T(8,128)} %get-tuple-element.71.x_ref,, ...), custom_call_target="tpu_custom_call" | custom-call | tf_op jit(solution)/shard_map/middle_rows/pallas_call | solution.py:540
  164.3 37.8 %attend_backward.1.gproj.gproj_ref = bf16[3,1024,768]{2,1,0:T(8,128)(2,1)} custom-call(s32[2]{0:T(128)} %get-tuple-element.60.low_ref, s32[2]{0:T(128)} %get-tuple-element.61.half_ref, bf16[1024,768]{1,0:T(8,128)(2,1)} %get-tuple-element.65.q_ref, bf16[1024,768]{1,0:T(8,128)(2,1)} %get-tuple-element.66.k_ref, bf16[1024,768]{1,0:T(8,128)(2,1)} %get-tuple-element.67.v_ref, ...), custom_call_target="tpu_custom_call" | custom-call | tf_op jit(solution)/shard_map/attend_backward/pallas_call | solution.py:413
  202.1 12.1 %tail_rows.1 = (f32[128,768]{1,0:T(8,128)}, f32[8,768]{1,0:T(8,128)}) custom-call(s32[1024,128]{1,0:T(8,128)} %get-tuple-element.68.column_ref, f32[1024,768]{1,0:T(8,128)} %get-tuple-element.71.x_ref, f32[1024,768]{1,0:T(8,128)} %get-tuple-element.83.gx_ref, bf16[3,1024,768]{2,1,0:T(8,128)(2,1)} %attend_backward.1.gproj.gproj_ref, f32[6,768]{1,0:T(8,128)} %norm_ref.7, ...), custom_call_target="tpu_custom_call" | custom-call | tf_op jit(solution)/shard_map/tail_rows/pallas_call | solution.py:604
  214.3 0.7 add.338.place_ref
  214.9 32.0 %weight_gradients.1 = f32[768,72,128]{2,1,0:T(8,128)} custom-call(s32[768]{0:T(1024)} %add.338.place_ref, bf16[1024,768]{1,0:T(8,128)(2,1)} %get-tuple-element.59.h_ref.h_one, bf16[1024,768]{1,0:T(8,128)(2,1)} %get-tuple-element.70.att_ref.att, bf16[1024,768]{1,0:T(8,128)(2,1)} %get-tuple-element.76.h_two, bf16[1024,3072]{1,0:T(8,128)(2,1)} %get-tuple-element.77.active, ...), custom_call_target="tpu_custom_call" | custom-call | tf_op jit(solution)/shard_map/weight_gradients/pallas_call | solution.py:715
  246.9 138.3 %sum_gradients.1 = (f32[24,96,96]{2,1,0:T(8,128)}, f32[128,768]{1,0:T(8,128)}, f32[8,768]{1,0:T(8,128)}, f32[8,128]{1,0:T(8,128)}) custom-call(f32[24,2,2,2,2,2,72,128]{7,6,5,4,3,2,1,0:T(8,128)} %bitcast.16, f32[128,768]{1,0:T(8,128)} %get-tuple-element.86.table_ref, f32[8,768]{1,0:T(8,128)} %get-tuple-element.87.norm_ref, f32[8,128]{1,0:T(8,128)} %get-tuple-element.72.count_ref), custom_call_target="tpu_custom_call" | custom-call | tf_op jit(solution)/shard_map/sum_gradients/pallas_call | solution.py:1039
  385.9 0.6 maximum_bitcast_fusion.corrections_ref
  386.5 14.9 %update_all.1 = (f32[128,768]{1,0:T(8,128)}, f32[128,128]{1,0:T(8,128)}, f32[768,768]{1,0:T(8,128)}, f32[128,768]{1,0:T(8,128)}, f32[6,768]{1,0:T(8,128)}, /*ind...) custom-call(f32[1,2]{1,0:T(1,128)} %maximum_bitcast_fusion.correctio, ...), custom_call_target="tpu_custom_call" | custom-call | tf_op jit(solution)/shard_map/update_all/pallas_call | solution.py:1416
  401.5 1.3 fusion.7
  (13 shorter events, 0.1 us)
